TPU v7x, 32 devices: a whole 2x2x4 slice. The times are simulated.
32 devices in a mesh: slab: 2 (over x), gal: 4 (over y, core), qb: 4 (over z).
Axes of the slice: x: 2, y: 2, z: 4, core: 2. Of those that a mesh axis runs over, the one named last changes fastest.
Arguments:
- gallery: bfloat16 [16384, 768], P(('slab', 'gal')), parts along dimension 0, may hold values from -512 to 512
- querybank: bfloat16 [8, 2048, 768], P(('slab', 'qb'), 'gal'), parts along dimension 0, may hold values from -512 to 512
- test_queries: bfloat16 [8, 512, 768], P(('slab', 'qb'), 'gal'), parts along dimension 0, may hold values from -512 to 512
Outputs:
- logprob: float32 [4096, 8192], P(('slab', 'qb'), 'gal'), parts along dimension 0
- normalizer: float32 [16384], P(('slab', 'gal')), parts along dimension 0
There are 2 independent parts, one for each index of `slab`. A program takes and returns all parts, laid end to end along the dimension named above; each array names one. Nothing has to cross between parts.
All inputs are finite; a program needn't handle non-finite values.
Results may differ from a plain program's by a relative error of at most 0.00049.
Values may be sent and summed in bfloat16 or wider, within the bound.
No kernel may reach another device: no remote copies, remote signals or barrier semaphores. Data moves between devices by JAX's collectives and lax.ppermute only.
A program may use at most 64 MiB of HBM per device.

v0:
```python
import math

import jax
import jax.numpy as jnp
from jax import lax
from jax.sharding import PartitionSpec as P

sharpness = 20.0


def unit_rows(values):
    wide = values.astype(jnp.float32)
    scaled = wide * lax.rsqrt(jnp.sum(wide * wide, axis=-1, keepdims=True) + 1e-06)
    return scaled.astype(jnp.bfloat16)


def column_terms(bank_block, gallery_unit):
    scores = lax.dot_general(
        bank_block, gallery_unit, (((1,), (1,)), ((), ())), preferred_element_type=jnp.float32
    )
    return jnp.sum(jnp.exp(sharpness * (scores - 1.0)), axis=0)


def bank_columns(bank_block, gallery_unit):
    rows = bank_block.shape[0]
    height = math.gcd(rows, 512)

    def add_block(index, running):
        piece = lax.dynamic_slice_in_dim(bank_block, index * height, height, 0)
        return running + column_terms(piece, gallery_unit)

    initial = jnp.zeros((gallery_unit.shape[0],), jnp.float32)
    return lax.fori_loop(0, rows // height, add_block, initial)


def per_device(gallery, querybank, test_queries):
    gallery_unit = unit_rows(gallery)
    bank_local = unit_rows(querybank[0])
    test_local = unit_rows(test_queries[0])
    bank_all = lax.all_gather(bank_local, "gal", axis=0, tiled=True)
    column_part = bank_columns(bank_all, gallery_unit)
    test_all = lax.all_gather(test_local, "gal", axis=0, tiled=True)
    column_total = lax.psum(column_part, "qb")
    normalizer = sharpness + jnp.log(column_total)
    bank_count = querybank.shape[1] * lax.axis_size("gal") * lax.axis_size("qb")
    offset = 2.0 * sharpness - math.log(bank_count)
    scores = lax.dot_general(
        test_all, gallery_unit, (((1,), (1,)), ((), ())), preferred_element_type=jnp.float32
    )
    logits = sharpness * scores - normalizer[None, :] - offset
    row_part = jnp.sum(jnp.exp(logits), axis=1)
    row_total = lax.psum(row_part, "gal")
    logprob = logits - jnp.log(row_total)[:, None]
    return (logprob, normalizer)


def solution(mesh):
    placed = (
        P(("slab", "gal"), None),
        P(("slab", "qb"), "gal", None),
        P(("slab", "qb"), "gal", None),
    )
    return jax.shard_map(
        per_device,
        mesh=mesh,
        in_specs=placed,
        out_specs=(P(("slab", "qb"), "gal"), P(("slab", "gal"))),
        check_vma=False,
    )
```

profile of v0, /device:TPU:0, one launch (start us, length us, event | category | flops | bytes accessed | tf_op | source)
XLA Modules:
  0.0 94.0 jit_solution(4073056862240279345)
XLA Ops:
  7.2 0.0 copy-start.1
  7.2 0.0 copy-start
  7.2 0.0 all-gather.2.cloned.1.call-start
  7.2 1.5 %fusion.5 = f32[512]{0:T(512)S(1)} fusion(bf16[1,512,768]{2,1,0:T(8,128)(2,1)} %param.6), kind=kLoop, calls=%fused_computation.13 | loop fusion | flops 1179136 | bytes 788480 | tf_op jit(solution)/shard_map/reduce_sum | solution.py:13
  8.8 2.2 %fusion.6 = bf16[512,768]{1,0:T(8,128)(2,1)} fusion(bf16[1,512,768]{2,1,0:T(8,128)(2,1)} %param.6, f32[512]{0:T(512)S(1)} %add_rsqrt_fusion.1), kind=kLoop, calls=%fused_computation.14 | loop fusion | flops 1179648 | bytes 1574912 | tf_op jit(solution)/shard_map/convert_element_type | solution.py:14
  11.0 0.0 all-gather.2.cloned.1.call-update
  11.0 1.0 %fusion.7 = f32[128]{0:T(128)S(1)} fusion(bf16[1,128,768]{2,1,0:T(8,128)(2,1)} %param.7), kind=kLoop, calls=%fused_computation.17 | loop fusion | flops 294784 | bytes 197120 | tf_op jit(solution)/shard_map/reduce_sum | solution.py:13
  12.1 0.0 copy-done
  12.1 0.7 fusion.2
  12.8 0.0 copy-done.1
  12.8 0.1 fusion.8
  12.9 10.6 %all_gather.6 = bf16[512,768]{1,0:T(8,128)(2,1)} all-gather(bf16[128,768]{1,0:T(8,128)(2,1)S(1)} %fusion.8), channel_id=1, replica_groups=mesh['slab'=2,'gal'=4,'qb'=4] {'gal'}, dimensions={0}, use_global_device_ids=true | all-gather | bytes 983040 | tf_op jit(solution)/shard_map/all_gather | solution.py:42
  23.5 2.3 %fusion.3 = bf16[2048,768]{1,0:T(8,128)(2,1)} fusion(bf16[2048,768]{1,0:T(8,128)(2,1)S(1)} %copy-done, f32[2048]{0:T(1024)S(1)} %add_rsqrt_fusion), kind=kLoop, calls=%fused_computation.7 | loop fusion | flops 4718592 | bytes 6299648 | tf_op jit(solution)/shard_map/convert_element_type | solution.py:14
  25.8 16.6 %all-gather.2.cloned.1.call-done = bf16[2048,768]{1,0:T(8,128)(2,1)} async-done(((bf16[512,768]{1,0:T(8,128)(2,1)}), bf16[2048,768]{1,0:T(8,128)(2,1)}) %all-gather.2.cloned.1.call-update) | async-done | bytes 3145744 | tf_op jit(solution)/shard_map/all_gather | solution.py:40
  42.4 0.0 copy-start.2
  42.4 16.3 %while.16 = (s32[]{:T(128)}, f32[2048]{0:T(1024)S(1)}, bf16[2048,768]{1,0:T(8,128)(2,1)}, bf16[2048,768]{1,0:T(8,128)(2,1)}, s32[]{:T(128)}, /*index=5*/s32[]{:T(128)}, s32[]{:T(128)}, s32[]{:T(128)}) while((s32[]{:T(128)}, f32[2048]{0:T(1024)S(1)}, bf16[2048,768]{1,0:T(8,128)(2,1)}, bf16[2048,768]{1,0:T(8,128)(2,1)}, s32[]{:T(128)}, ...), condition=%wide.region_5.0_spmd.clone, body=%wide.region_3.0_spmd.clone.sunk | while | flops 1613760512 | bytes 3965081 | solution.py:33
  42.4 4.1 %exponential_reduce_fusion.3 = f32[2048]{0:T(1024)S(1)} fusion(bf16[2048,768]{1,0:T(8,128)(2,1)} %get-tuple-element.182, bf16[2048,768]{1,0:T(8,128)(2,1)} %get-tuple-element.181, s32[]{:T(128)S(6)} %select_n.12), kind=kOutput, calls=%fused_computation.clone.1 | convolution fusion | flops 1613756416 | bytes 3940356 | tf_op jit(solution)/shard_map/while/body/eval_jaxpr/dot_general | solution.py:18
  46.5 4.0 %exponential_reduce_fusion.3 = f32[2048]{0:T(1024)S(1)} fusion(bf16[2048,768]{1,0:T(8,128)(2,1)} %get-tuple-element.182, bf16[2048,768]{1,0:T(8,128)(2,1)} %get-tuple-element.181, s32[]{:T(128)S(6)} %select_n.12), kind=kOutput, calls=%fused_computation.clone.1 | convolution fusion | flops 1613756416 | bytes 3940356 | tf_op jit(solution)/shard_map/while/body/eval_jaxpr/dot_general | solution.py:18
  50.6 4.0 %exponential_reduce_fusion.3 = f32[2048]{0:T(1024)S(1)} fusion(bf16[2048,768]{1,0:T(8,128)(2,1)} %get-tuple-element.182, bf16[2048,768]{1,0:T(8,128)(2,1)} %get-tuple-element.181, s32[]{:T(128)S(6)} %select_n.12), kind=kOutput, calls=%fused_computation.clone.1 | convolution fusion | flops 1613756416 | bytes 3940356 | tf_op jit(solution)/shard_map/while/body/eval_jaxpr/dot_general | solution.py:18
  54.6 4.0 %exponential_reduce_fusion.3 = f32[2048]{0:T(1024)S(1)} fusion(bf16[2048,768]{1,0:T(8,128)(2,1)} %get-tuple-element.182, bf16[2048,768]{1,0:T(8,128)(2,1)} %get-tuple-element.181, s32[]{:T(128)S(6)} %select_n.12), kind=kOutput, calls=%fused_computation.clone.1 | convolution fusion | flops 1613756416 | bytes 3940356 | tf_op jit(solution)/shard_map/while/body/eval_jaxpr/dot_general | solution.py:18
  58.7 11.8 %psum.14 = f32[2048]{0:T(1024)S(1)} all-reduce(f32[2048]{0:T(1024)S(1)} %get-tuple-element.112), channel_id=1, replica_groups=mesh['slab'=2,'gal'=4,'qb'=4] {'qb'}, use_global_device_ids=true, to_apply=%region_6.0 | all-reduce | flops 2048 | bytes 16384 | tf_op jit(solution)/shard_map/psum | solution.py:43
  70.5 0.0 copy-done.2
  70.5 0.0 copy-start.3
  70.6 5.9 %exponential_reduce_fusion.1 = (f32[512]{0:T(512)S(1)}, f32[512,2048]{1,0:T(8,128)}) fusion(f32[2048]{0:T(1024)S(1)} %log_add_fusion, bf16[512,768]{1,0:T(8,128)(2,1)S(1)} %copy-done.2, bf16[2048,768]{1,0:T(8,128)(2,1)} %get-tuple-element.188), kind=kOutput, calls=%fused_computation.8 | convolution fusion | flops 1614806528 | bytes 8136704 | tf_op jit(solution)/shard_map/dot_general | solution.py:47
  76.5 5.9 %psum.15 = f32[512]{0:T(512)S(1)} all-reduce(f32[512]{0:T(512)S(1)} %get-tuple-element.136), channel_id=1, replica_groups=mesh['slab'=2,'gal'=4,'qb'=4] {'gal'}, use_global_device_ids=true, to_apply=%region_8.0 | all-reduce | flops 512 | bytes 4096 | tf_op jit(solution)/shard_map/psum | solution.py:52
  82.4 0.0 copy-done.3
  82.4 4.8 %fusion.4 = f32[512,2048]{1,0:T(8,128)} fusion(f32[512,2048]{1,0:T(8,128)} %get-tuple-element.137, f32[512]{0:T(512)S(1)} %log.7, f32[2048]{0:T(1024)S(1)} %log_add_fusion), kind=kLoop, calls=%fused_computation.10 | loop fusion | flops 4194304 | bytes 8398848 | tf_op jit(solution)/shard_map/sub | solution.py:53
  (10 shorter events, 0.1 us)
Async XLA Ops:
  7.2 5.6 %copy-start.1 = (bf16[1,128,768]{2,1,0:T(8,128)(2,1)S(1)}, bf16[1,128,768]{2,1,0:T(8,128)(2,1)}, u32[]{:S(2)}) copy-start(bf16[1,128,768]{2,1,0:T(8,128)(2,1)} %param.7) | copy-start | bytes 589828
  7.2 4.9 %copy-start = (bf16[2048,768]{1,0:T(8,128)(2,1)S(1)}, bf16[2048,768]{1,0:T(8,128)(2,1)}, u32[]{:S(2)}) copy-start(bf16[2048,768]{1,0:T(8,128)(2,1)} %param.5) | copy-start | bytes 9437188
  7.2 35.2 %all-gather.2.cloned.1.call-start = ((), (), s32[]{:S(2)}) async-start(), calls=%async_computation | async-start | bytes 3932160 | tf_op jit(solution)/shard_map/all_gather | solution.py:40
  42.4 28.2 %copy-start.2 = (bf16[512,768]{1,0:T(8,128)(2,1)S(1)}, bf16[512,768]{1,0:T(8,128)(2,1)}, u32[]{:S(2)}) copy-start(bf16[512,768]{1,0:T(8,128)(2,1)} %all_gather.6) | copy-start | bytes 2359300
  70.5 11.9 %copy-start.3 = (f32[2048]{0:T(1024)}, f32[2048]{0:T(1024)S(1)}, u32[]{:S(2)}) copy-start(f32[2048]{0:T(1024)S(1)} %log_add_fusion) | copy-start | bytes 24580
Sparse Core Ops, SparseCore 0:
  11.1 31.2 all-gather.1
where the time goes:
time: 94.4 us; the launch traced here: 94 us
  blocking collectives  28.3 us (30%)
  matrix products  22.1 us (23%)
  waiting for transfers between devices  16.6 us (18%)
  between operations  14.1 us (15%)
  other arithmetic  12.7 us (13%)
    all_gather x1, waiting for transfers between devices, per_device(): bank_all = lax.all_gather(bank_local, 'gal', axis=0, tiled=True)  16.6 us
    dot_general x4, matrix products, column_terms(): lax.dot_general(bank_block, gallery_unit, (((1,), (1,)), ((), ())), prefe...  16.1 us
    psum x1, blocking collectives, per_device(): column_total = lax.psum(column_part, 'qb')  11.8 us
    all_gather x1, blocking collectives, per_device(): test_all = lax.all_gather(test_local, 'gal', axis=0, tiled=True)  10.6 us
    dot_general x1, matrix products, per_device(): lax.dot_general(test_all, gallery_unit, (((1,), (1,)), ((), ())), preferr...  5.95 us
    psum x1, blocking collectives, per_device(): row_total = lax.psum(row_part, 'gal')  5.9 us
    sub x1, other arithmetic, per_device(): logprob = logits - jnp.log(row_total)[:, None]  4.79 us
    convert_element_type x3, other arithmetic, unit_rows(): return scaled.astype(jnp.bfloat16)  4.59 us
  transfers between devices with their start and end apart: 1, of which 1 were waited for; matrix products, arithmetic and copies ran while one was open for 4% of the time, Pallas kernels for 0%

commit v1 on v0

v1 whole, which is shorter than its diff:
```python
import functools
import math

import jax
import jax.numpy as jnp
from jax import lax
from jax.experimental import pallas as pl
from jax.experimental.pallas import tpu as pltpu
from jax.sharding import PartitionSpec as P


sharpness = 20.0
LOG2E = math.log2(math.e)
LN2 = math.log(2.0)
LANES = 128


VMEM = pl.BlockSpec(memory_space=pltpu.VMEM)


def params(mib):
    return pltpu.CompilerParams(vmem_limit_bytes=mib << 20)


def unit_rows(values):
    wide = values.astype(jnp.float32)
    scaled = wide * lax.rsqrt(jnp.sum(wide * wide, axis=-1, keepdims=True) + 1e-06)
    return scaled.astype(jnp.bfloat16)


def inner(rows, columns):
    return lax.dot_general(
        rows, columns, (((1,), (1,)), ((), ())), preferred_element_type=jnp.float32
    )


def unit_kernel(values_ref, unit_ref):
    unit_ref[...] = unit_rows(values_ref[...])


def unit_call(values):
    return pl.pallas_call(
        unit_kernel,
        out_shape=jax.ShapeDtypeStruct(values.shape, jnp.bfloat16),
        in_specs=[VMEM],
        out_specs=VMEM,
        compiler_params=params(16),
        name="unit",
        cost_estimate=pl.CostEstimate(
            flops=4 * values.size, bytes_accessed=4 * values.size, transcendentals=values.shape[0]
        ),
    )(values)


def bank_kernel(count, tile, *refs):
    blocks, gallery_ref, earlier, total_ref = (
        refs[:count],
        refs[count],
        refs[count + 1 : -1],
        refs[-1],
    )
    units = [unit_rows(block[...]) for block in blocks]
    unit = jnp.concatenate(units, axis=0) if count > 1 else units[0]
    for start in range(0, gallery_ref.shape[0], tile):
        scores = inner(unit, gallery_ref[start : start + tile, :])
        total = jnp.sum(jnp.exp2(scores * (sharpness * LOG2E)), axis=0, keepdims=True)
        for other in earlier:
            total = total + other[:, start : start + tile]
        total_ref[:, start : start + tile] = total


def bank_call(blocks, gallery_unit, earlier=()):
    columns, depth = gallery_unit.shape
    rows = sum(block.shape[0] for block in blocks)
    tile = math.gcd(columns, 256)
    return pl.pallas_call(
        functools.partial(bank_kernel, len(blocks), tile),
        out_shape=jax.ShapeDtypeStruct((1, columns), jnp.float32),
        in_specs=[VMEM] * (len(blocks) + 1 + len(earlier)),
        out_specs=VMEM,
        compiler_params=params(16),
        name="bank",
        cost_estimate=pl.CostEstimate(
            flops=2 * rows * columns * depth,
            bytes_accessed=2 * depth * (rows + columns),
            transcendentals=rows * columns,
        ),
    )(*blocks, gallery_unit, *earlier)


def test_kernel(count, tile, *refs):
    blocks, gallery_ref, score_ref = refs[:count], refs[count], refs[-1]
    units = [unit_rows(block[...]) for block in blocks]
    unit = jnp.concatenate(units, axis=0) if count > 1 else units[0]
    for start in range(0, gallery_ref.shape[0], tile):
        scores = inner(unit, gallery_ref[start : start + tile, :])
        score_ref[:, start : start + tile] = scores * (sharpness * LOG2E)


def test_call(blocks, gallery_unit):
    columns, depth = gallery_unit.shape
    rows = sum(block.shape[0] for block in blocks)
    tile = math.gcd(columns, 256)
    return pl.pallas_call(
        functools.partial(test_kernel, len(blocks), tile),
        out_shape=jax.ShapeDtypeStruct((rows, columns), jnp.float32),
        in_specs=[VMEM] * (len(blocks) + 1),
        out_specs=VMEM,
        compiler_params=params(16),
        name="test",
        cost_estimate=pl.CostEstimate(
            flops=2 * rows * columns * depth,
            bytes_accessed=2 * depth * (rows + columns) + 4 * rows * columns,
            transcendentals=0,
        ),
    )(*blocks, gallery_unit)


def row_kernel(groups, count, *refs):
    totals, scores, (log_ref, norm_ref, rows_ref) = (
        refs[:groups],
        refs[groups : groups + count],
        refs[-3:],
    )
    total = totals[0][...]
    for other in totals[1:]:
        total = total + other[...]
    log_ref[...] = jnp.log2(total)
    norm_ref[...] = jnp.log(total)
    width = rows_ref.shape[1]
    columns = log_ref.shape[1]
    place = 0
    for score_ref in scores:
        for first in range(0, score_ref.shape[0], width):
            running = jnp.zeros((width, LANES), jnp.float32)
            for start in range(0, columns, LANES):
                piece = score_ref[first : first + width, start : start + LANES]
                running = running + jnp.exp2(piece - log_ref[:, start : start + LANES])
            rows_ref[place : place + 1, :] = jnp.sum(running.T, axis=0, keepdims=True)
            place += 1


def row_call(totals, scores, width):
    columns = scores[0].shape[1]
    rows = sum(score.shape[0] for score in scores)
    return pl.pallas_call(
        functools.partial(row_kernel, len(totals), len(scores)),
        out_shape=(
            jax.ShapeDtypeStruct((1, columns), jnp.float32),
            jax.ShapeDtypeStruct((1, columns), jnp.float32),
            jax.ShapeDtypeStruct((rows // width, width), jnp.float32),
        ),
        in_specs=[VMEM] * (len(totals) + len(scores)),
        out_specs=(VMEM, VMEM, VMEM),
        compiler_params=params(16),
        name="rows",
        cost_estimate=pl.CostEstimate(
            flops=3 * rows * columns,
            bytes_accessed=4 * rows * columns,
            transcendentals=rows * columns,
        ),
    )(*totals, *scores)


def out_kernel(orders, count, split, place_ref, *refs):
    parts, scores, (log_ref, out_ref) = (
        refs[: len(orders)],
        refs[len(orders) : len(orders) + count],
        refs[-2:],
    )
    step = pl.program_id(0)
    height = out_ref.shape[0]
    width = parts[0].shape[1]
    line = height // width
    for block in range(len(orders)):

        @pl.when(step == block)
        def _(block=block):
            for sub in range(line):
                total = None
                for part, order in zip(parts, orders):
                    at = order[block] * line + sub
                    row = part[at : at + 1, :]
                    total = row if total is None else total + row
                wide = jnp.broadcast_to(jnp.log2(total), (LANES, width)).T
                source = scores[block // split]
                first = block % split * height + sub * width
                for start in range(0, log_ref.shape[1], LANES):
                    cut = slice(start, start + LANES)
                    value = source[first : first + width, cut] - log_ref[:, cut] - wide
                    out_ref[sub * width : (sub + 1) * width, cut] = value * LN2


def out_call(place, parts, orders, scores, log_total):
    columns = log_total.shape[1]
    rows = sum(score.shape[0] for score in scores)
    height = rows // len(orders)
    split = scores[0].shape[0] // height
    return pl.pallas_call(
        functools.partial(out_kernel, orders, len(scores), split),
        out_shape=jax.ShapeDtypeStruct((rows, columns), jnp.float32),
        grid_spec=pltpu.PrefetchScalarGridSpec(
            num_scalar_prefetch=1,
            grid=(len(orders),),
            in_specs=[VMEM] * (len(parts) + len(scores) + 1),
            out_specs=pl.BlockSpec((height, columns), lambda step, place: (place[step], 0)),
        ),
        compiler_params=params(16),
        name="out",
        cost_estimate=pl.CostEstimate(
            flops=3 * rows * columns, bytes_accessed=8 * rows * columns, transcendentals=0
        ),
    )(place, *parts, *scores, log_total)


def after(value, token):
    return lax.optimization_barrier((value, token))[0]


def chunk_sizes(rows):
    if rows % 64:
        return [rows]
    return [rows // 2, rows // 4, rows // 4]


def per_device(gallery, querybank, test_queries):
    bank = querybank[0]
    test = test_queries[0]
    gal = lax.axis_size("gal")
    groups = lax.axis_size("qb")
    core = 2 if gal % 2 == 0 else 1
    pairs = gal // core

    def shift(value, pair, flip):
        moves = [
            (i, (i // core + pair) % pairs * core + (i % core ^ flip)) for i in range(gal)
        ]
        return lax.ppermute(value, "gal", moves)

    sizes = chunk_sizes(bank.shape[0])
    starts = [sum(sizes[:i]) for i in range(len(sizes))]
    chunks = [lax.slice_in_dim(bank, s, s + n, axis=0) for s, n in zip(starts, sizes)]

    crossed = []
    for chunk in chunks:
        crossed.append([shift(chunk, pair, 0) for pair in range(1, pairs)])
    test_crossed = [shift(test, pair, 0) for pair in range(1, pairs)]

    def with_partner(block):
        return [block, shift(block, 0, 1)] if core == 2 else [block]

    near = with_partner(bank)
    near_tests = with_partner(test)
    gallery_unit = unit_call(gallery)
    total = bank_call(near, gallery_unit)
    scores = [test_call(near_tests, after(gallery_unit, total))]
    total = after(total, scores[0])
    for group in crossed:
        for block in group:
            block = after(block, total)
            total = bank_call(with_partner(block), gallery_unit, [total])

    totals = [total] + [
        lax.ppermute(total, "qb", [(i, (i + s) % groups) for i in range(groups)])
        for s in range(1, groups)
    ]
    for block in test_crossed:
        block = after(block, total)
        blocks = with_partner(block)
        scores.append(test_call(blocks, gallery_unit))
    width = math.gcd(test.shape[0], LANES)
    log_total, normalizer, part = row_call(totals, scores, width)

    origins = [(pair, flip) for pair in range(pairs) for flip in range(core)]
    parts = [part if pair + flip == 0 else shift(part, pair, flip) for pair, flip in origins]
    orders = [
        [origins.index(((p - pair) % pairs, f ^ flip)) for p, f in origins]
        for pair, flip in origins
    ]

    me = lax.axis_index("gal")
    place = jnp.stack(
        [(me // core - p) % pairs * core + (me % core ^ f) for p, f in origins]
    ).astype(jnp.int32)
    logprob = out_call(place, parts, orders, scores, log_total)
    return (logprob, normalizer.reshape(-1))


def solution(mesh):
    placed = (
        P(("slab", "gal"), None),
        P(("slab", "qb"), "gal", None),
        P(("slab", "qb"), "gal", None),
    )

    return jax.shard_map(
        per_device,
        mesh=mesh,
        in_specs=placed,
        out_specs=(P(("slab", "qb"), "gal"), P(("slab", "gal"))),
        check_vma=False,
    )
```

time: 94.4 us -> 54.3 us (0.58)
  blocking collectives: 28.3 us -> 0 us
  matrix products: 22.1 us -> 0 us
  starting transfers between devices: 0.04 us -> 15.3 us
  Pallas kernels: 0 us -> 15.1 us
  between operations: 14.1 us -> 0.76 us
  other arithmetic: 12.7 us -> 0.08 us
  waiting for transfers between devices: 16.6 us -> 19.7 us
  local copies, waits for them, and re-layouts: 0.03 us -> 3.09 us
    dot_general x5 -> x0, matrix products: 22.1 us -> none  [the longest x4 16.1 us: column_terms(): lax.dot_general(bank_block, gallery_unit, (((1,), (1,)), ((), ())), prefe...]
    ppermute x0 -> x16, waiting for transfers between devices: none -> 19.7 us  [the longest x13 16.3 us: shift(): return lax.ppermute(value, 'gal', moves)]
    psum x2 -> x0, blocking collectives: 17.7 us -> none  [the longest x1 11.8 us: per_device(): column_total = lax.psum(column_part, 'qb')]
    all_gather x1 -> x0, waiting for transfers between devices: 16.6 us -> none  [per_device(): bank_all = lax.all_gather(bank_local, 'gal', axis=0, tiled=True)]
    ppermute x0 -> x16, starting transfers between devices: none -> 15.3 us  [the longest x13 10.5 us: shift(): return lax.ppermute(value, 'gal', moves)]
    pallas_call x0 -> x9, Pallas kernels: none -> 15.1 us  [the longest x4 7.67 us: bank_call(): pl.pallas_call(functools.partial(bank_kernel, len(blocks), tile), out_sha...]
    all_gather x1 -> x0, blocking collectives: 10.6 us -> none  [per_device(): test_all = lax.all_gather(test_local, 'gal', axis=0, tiled=True)]
    sub x1 -> x0, other arithmetic: 4.79 us -> none  [per_device(): logprob = logits - jnp.log(row_total)[:, None]]
  transfers between devices with their start and end apart: 1 -> 16, of which waited for: 1 -> 8; matrix products, arithmetic and copies ran while one was open for 4% -> 2% of each run, Pallas kernels for 0% -> 20%
where the time goes in v1:
time: 54.3 us; the launch traced here: 54.1 us
  waiting for transfers between devices  19.7 us (36%)
  starting transfers between devices  15.3 us (28%)
  Pallas kernels  15.1 us (28%)
  local copies, waits for them, and re-layouts  3.09 us (6%)
  between operations  0.76 us (1%)
    ppermute x13, waiting for transfers between devices, shift(): return lax.ppermute(value, 'gal', moves)  16.3 us
    ppermute x13, starting transfers between devices, shift(): return lax.ppermute(value, 'gal', moves)  10.5 us
    pallas_call x4, Pallas kernels, bank_call(): pl.pallas_call(functools.partial(bank_kernel, len(blocks), tile), out_sha...  7.67 us
    ppermute x3, starting transfers between devices, per_device(): lax.ppermute(total, 'qb', [(i, (i + s) % groups) for i in range(groups)])  4.84 us
    ppermute x3, waiting for transfers between devices, per_device(): lax.ppermute(total, 'qb', [(i, (i + s) % groups) for i in range(groups)])  3.37 us
    pallas_call x1, Pallas kernels, out_call(): pl.pallas_call(functools.partial(out_kernel, orders, len(scores), split),...  3.23 us
    pallas_call x2, Pallas kernels, test_call(): pl.pallas_call(functools.partial(test_kernel, len(blocks), tile), out_sha...  2.1 us
    unnamed x10, local copies, waits for them, and re-layouts  2.04 us
  transfers between devices with their start and end apart: 16, of which 8 were waited for; matrix products, arithmetic and copies ran while one was open for 2% of the time, Pallas kernels for 20%

profile of v1, /device:TPU:0, one launch (start us, length us, event | category | flops | bytes accessed | tf_op | source)
XLA Modules:
  0.0 54.1 jit_solution(17329813365021280334)
XLA Ops:
  0.6 0.6 %collective-permute-start.3 = (bf16[512,768]{1,0:T(8,128)(2,1)}, bf16[512,768]{1,0:T(8,128)(2,1)S(1)}, u32[]{:S(2)}, u32[]{:S(2)}) collective-permute-start(bf16[512,768]{1,0:T(8,128)(2,1)} %bitcast.13), channel_id=1, source_target_pairs={{0,4},{4,0},{8,12},{12,8},{1,5},{5,1},{9,13},{13,9},{2,6},{6,2},{1... | collective-permute-start | bytes 2359304 | tf_op jit(solution)/shard_map/ppermute | solution.py:238
  1.2 1.0 %slice_bitcast_fusion = bf16[256,768]{1,0:T(8,128)(2,1)S(1)} fusion(bf16[1,512,768]{2,1,0:T(8,128)(2,1)} %param.4), kind=kLoop, calls=%fused_computation | loop fusion | bytes 786432 | tf_op jit(solution)/shard_map/slice | solution.py:242
  2.2 2.6 %collective-permute-start.2 = (bf16[256,768]{1,0:T(8,128)(2,1)S(1)}, bf16[256,768]{1,0:T(8,128)(2,1)S(1)}, u32[]{:S(2)}, u32[]{:S(2)}) collective-permute-start(bf16[256,768]{1,0:T(8,128)(2,1)S(1)} %slice_bitcast_fusion), channel_id=1, source_target_pairs={{0,8},{4,12},{8,0},{12,4},{1,9},{5,13},{9,1},{13,5},{2,10},{6,14},... | collective-permute-start | bytes 1179656 | tf_op jit(solution)/shard_map/ppermute | solution.py:238
  4.8 0.2 collective-permute-start.4
  5.0 1.9 %copy-done.2 = bf16[2048,768]{1,0:T(8,128)(2,1)S(1)} copy-done((bf16[2048,768]{1,0:T(8,128)(2,1)S(1)}, bf16[2048,768]{1,0:T(8,128)(2,1)}, u32[]{:S(2)}) %copy-start.2) | copy-done | bytes 3145752
  6.9 1.0 %unit.1.refs_2_ = bf16[2048,768]{1,0:T(8,128)(2,1)S(1)} custom-call(bf16[2048,768]{1,0:T(8,128)(2,1)S(1)} %copy-done.2), custom_call_target="tpu_custom_call" | custom-call | flops 6291456 | bytes 6291456 | tf_op jit(solution)/shard_map/unit/pallas_call | solution.py:42
  7.9 0.0 copy-start.4
  7.9 0.0 collective-permute-done.3.refs_1_
  7.9 0.1 copy-done.3
  8.0 3.6 %bank.4.refs_3_ = f32[1,2048]{1,0:T(1,128)S(1)} custom-call(bf16[512,768]{1,0:T(8,128)(2,1)S(1)} %bitcast.14, bf16[512,768]{1,0:T(8,128)(2,1)S(1)} %collective-permute-done.3.refs_1_, bf16[2048,768]{1,0:T(8,128)(2,1)S(1)} %unit.1.refs_2_), custom_call_target="tpu_custom_call" | custom-call | flops 3221225472 | bytes 4718592 | tf_op jit(solution)/shard_map/bank/pallas_call | solution.py:76
  11.6 0.0 collective-permute-done.4.refs_1_
  11.7 0.0 copy-done.4
  11.7 1.0 %test.2.refs_4_ = f32[256,2048]{1,0:T(8,128)S(1)} custom-call(bf16[128,768]{1,0:T(8,128)(2,1)S(1)} %bitcast.16, bf16[128,768]{1,0:T(8,128)(2,1)S(1)} %collective-permute-done.4.refs_1_, bf16[2048,768]{1,0:T(8,128)(2,1)S(1)} %unit.1.refs_2_), custom_call_target="tpu_custom_call" | custom-call | flops 805306368 | bytes 5636096 | tf_op jit(solution)/shard_map/test/pallas_call | solution.py:104
  12.7 0.0 copy-start
  12.7 1.8 %collective-permute-done.2.refs_0_ = bf16[256,768]{1,0:T(8,128)(2,1)S(1)} collective-permute-done((bf16[256,768]{1,0:T(8,128)(2,1)S(1)}, bf16[256,768]{1,0:T(8,128)(2,1)S(1)}, u32[]{:S(2)}, u32[]{:S(2)}) %collective-permute-start.2) | collective-permute-done | bytes 393248 | tf_op jit(solution)/shard_map/ppermute | solution.py:238
  14.6 0.0 collective-permute-start.5
  14.6 1.8 %collective-permute-start.1 = (bf16[128,768]{1,0:T(8,128)(2,1)S(1)}, bf16[128,768]{1,0:T(8,128)(2,1)S(1)}, u32[]{:S(2)}, u32[]{:S(2)}) collective-permute-start(bf16[128,768]{1,0:T(8,128)(2,1)S(1)} %get-tuple-element.20), channel_id=1, source_target_pairs={{0,8},{4,12},{8,0},{12,4},{1,9},{5,13},{9,1},{13,5},{2,10},{6,14},... | collective-permute-start | bytes 589832 | tf_op jit(solution)/shard_map/ppermute | solution.py:238
  16.4 0.0 collective-permute-done.5.refs_1_
  16.4 1.9 %bank.5.refs_3_ = f32[1,2048]{1,0:T(1,128)S(1)} custom-call(bf16[256,768]{1,0:T(8,128)(2,1)S(1)} %collective-permute-done.2.refs_0_, bf16[256,768]{1,0:T(8,128)(2,1)S(1)} %collective-permute-done.5.refs_1_, bf16[2048,768]{1,0:T(8,128)(2,1)S(1)} %unit.1.refs_2_, f32[1,2048]{1,0:T(1,128)S(1)} %bank.4.refs_3_), custom_call_target="tpu_custom_call" | custom-call | flops 1610612736 | bytes 3932160 | tf_op jit(solution)/shard_map/bank/pallas_call | solution.py:76
  18.3 3.6 %collective-permute-done.1.refs_0_ = bf16[128,768]{1,0:T(8,128)(2,1)S(1)} collective-permute-done((bf16[128,768]{1,0:T(8,128)(2,1)S(1)}, bf16[128,768]{1,0:T(8,128)(2,1)S(1)}, u32[]{:S(2)}, u32[]{:S(2)}) %collective-permute-start.1) | collective-permute-done | bytes 196640 | tf_op jit(solution)/shard_map/ppermute | solution.py:238
  22.0 0.0 collective-permute-start.6
  22.0 1.7 %collective-permute-start = (bf16[128,768]{1,0:T(8,128)(2,1)S(1)}, bf16[128,768]{1,0:T(8,128)(2,1)S(1)}, u32[]{:S(2)}, u32[]{:S(2)}) collective-permute-start(bf16[128,768]{1,0:T(8,128)(2,1)S(1)} %get-tuple-element.21), channel_id=1, source_target_pairs={{0,8},{4,12},{8,0},{12,4},{1,9},{5,13},{9,1},{13,5},{2,10},{6,14},... | collective-permute-start | bytes 589832 | tf_op jit(solution)/shard_map/ppermute | solution.py:238
  23.7 0.0 collective-permute-done.6.refs_1_
  23.7 1.1 %bank.6.refs_3_ = f32[1,2048]{1,0:T(1,128)S(1)} custom-call(bf16[128,768]{1,0:T(8,128)(2,1)S(1)} %collective-permute-done.1.refs_0_, bf16[128,768]{1,0:T(8,128)(2,1)S(1)} %collective-permute-done.6.refs_1_, bf16[2048,768]{1,0:T(8,128)(2,1)S(1)} %unit.1.refs_2_, f32[1,2048]{1,0:T(1,128)S(1)} %bank.5.refs_3_), custom_call_target="tpu_custom_call" | custom-call | flops 805306368 | bytes 3538944 | tf_op jit(solution)/shard_map/bank/pallas_call | solution.py:76
  24.8 4.5 %collective-permute-done.refs_0_ = bf16[128,768]{1,0:T(8,128)(2,1)S(1)} collective-permute-done((bf16[128,768]{1,0:T(8,128)(2,1)S(1)}, bf16[128,768]{1,0:T(8,128)(2,1)S(1)}, u32[]{:S(2)}, u32[]{:S(2)}) %collective-permute-start) | collective-permute-done | bytes 196640 | tf_op jit(solution)/shard_map/ppermute | solution.py:238
  29.3 0.0 collective-permute-start.7
  29.3 1.7 %collective-permute-start.11 = (bf16[128,768]{1,0:T(8,128)(2,1)S(1)}, bf16[128,768]{1,0:T(8,128)(2,1)S(1)}, u32[]{:S(2)}, u32[]{:S(2)}) collective-permute-start(bf16[128,768]{1,0:T(8,128)(2,1)S(1)} %bitcast.17), channel_id=1, source_target_pairs={{0,8},{4,12},{8,0},{12,4},{1,9},{5,13},{9,1},{13,5},{2,10},{6,14},... | collective-permute-start | bytes 589832 | tf_op jit(solution)/shard_map/ppermute | solution.py:238
  31.0 0.0 collective-permute-done.7.refs_1_
  31.0 1.1 %bank.7.refs_0_ = f32[1,2048]{1,0:T(1,128)S(1)} custom-call(bf16[128,768]{1,0:T(8,128)(2,1)S(1)} %collective-permute-done.refs_0_, bf16[128,768]{1,0:T(8,128)(2,1)S(1)} %collective-permute-done.7.refs_1_, bf16[2048,768]{1,0:T(8,128)(2,1)S(1)} %unit.1.refs_2_, f32[1,2048]{1,0:T(1,128)S(1)} %bank.6.refs_3_), custom_call_target="tpu_custom_call" | custom-call | flops 805306368 | bytes 3538944 | tf_op jit(solution)/shard_map/bank/pallas_call | solution.py:76
  32.1 4.5 %collective-permute-done.11.refs_0_ = bf16[128,768]{1,0:T(8,128)(2,1)S(1)} collective-permute-done((bf16[128,768]{1,0:T(8,128)(2,1)S(1)}, bf16[128,768]{1,0:T(8,128)(2,1)S(1)}, u32[]{:S(2)}, u32[]{:S(2)}) %collective-permute-start.11) | collective-permute-done | bytes 196640 | tf_op jit(solution)/shard_map/ppermute | solution.py:238
  36.6 0.0 collective-permute-start.12
  36.6 3.8 %collective-permute-start.10 = (f32[1,2048]{1,0:T(1,128)S(1)}, f32[1,2048]{1,0:T(1,128)S(1)}, u32[]{:S(2)}, u32[]{:S(2)}) collective-permute-start(f32[1,2048]{1,0:T(1,128)S(1)} %bank.7.refs_0_), channel_id=1, source_target_pairs={{0,3},{1,0},{2,1},{3,2},{4,7},{5,4},{6,5},{7,6},{8,11},{9,8},{10,9... | collective-permute-start | bytes 24584 | tf_op jit(solution)/shard_map/ppermute | solution.py:264
  40.4 0.0 collective-permute-start.9
  40.4 1.0 %collective-permute-start.8 = (f32[1,2048]{1,0:T(1,128)S(1)}, f32[1,2048]{1,0:T(1,128)S(1)}, u32[]{:S(2)}, u32[]{:S(2)}) collective-permute-start(f32[1,2048]{1,0:T(1,128)S(1)} %bank.7.refs_0_), channel_id=1, source_target_pairs={{0,1},{1,2},{2,3},{3,0},{4,5},{5,6},{6,7},{7,4},{8,9},{9,10},{10,1... | collective-permute-start | bytes 24584 | tf_op jit(solution)/shard_map/ppermute | solution.py:264
  41.5 0.0 collective-permute-done.12.refs_1_
  41.5 1.0 %test.3.refs_5_ = f32[256,2048]{1,0:T(8,128)S(1)} custom-call(bf16[128,768]{1,0:T(8,128)(2,1)S(1)} %collective-permute-done.11.refs_0_, bf16[128,768]{1,0:T(8,128)(2,1)S(1)} %collective-permute-done.12.refs_1_, bf16[2048,768]{1,0:T(8,128)(2,1)S(1)} %unit.1.refs_2_), custom_call_target="tpu_custom_call" | custom-call | flops 805306368 | bytes 5636096 | tf_op jit(solution)/shard_map/test/pallas_call | solution.py:104
  42.5 0.0 collective-permute-done.10.refs_3_
  42.5 2.5 %collective-permute-done.9.refs_2_ = f32[1,2048]{1,0:T(1,128)S(1)} collective-permute-done((f32[1,2048]{1,0:T(1,128)S(1)}, f32[1,2048]{1,0:T(1,128)S(1)}, u32[]{:S(2)}, u32[]{:S(2)}) %collective-permute-start.9) | collective-permute-done | bytes 8224 | tf_op jit(solution)/shard_map/ppermute | solution.py:264
  45.0 0.9 %collective-permute-done.8.refs_1_ = f32[1,2048]{1,0:T(1,128)S(1)} collective-permute-done((f32[1,2048]{1,0:T(1,128)S(1)}, f32[1,2048]{1,0:T(1,128)S(1)}, u32[]{:S(2)}, u32[]{:S(2)}) %collective-permute-start.8) | collective-permute-done | bytes 8224 | tf_op jit(solution)/shard_map/ppermute | solution.py:264
  45.9 1.2 %rows.1 = (f32[1,2048]{1,0:T(1,128)S(1)}, f32[1,2048]{1,0:T(1,128)}, f32[4,128]{1,0:T(4,128)S(1)}) custom-call(f32[1,2048]{1,0:T(1,128)S(1)} %bank.7.refs_0_, f32[1,2048]{1,0:T(1,128)S(1)} %collective-permute-done.8.refs_1_, f32[1,2048]{1,0:T(1,128)S(1)} %collective-permute-done.9.refs_2_, f32[1,2048]{1,0:T(1,128)S(1)} %collective-permute-done.10.refs_3_, ...), custom_call_target="tpu_custom_call" | custom-call | flops 3145728 | bytes 4194304 | tf_op jit(solution)/shard_map/rows/pallas_call | solution.py:146
  47.1 0.2 collective-permute-start.15
  47.3 1.3 %collective-permute-start.14 = (f32[4,128]{1,0:T(4,128)S(1)}, f32[4,128]{1,0:T(4,128)S(1)}, u32[]{:S(2)}, u32[]{:S(2)}) collective-permute-start(f32[4,128]{1,0:T(4,128)S(1)} %get-tuple-element.17.refs_0_), channel_id=1, source_target_pairs={{0,8},{4,12},{8,0},{12,4},{1,9},{5,13},{9,1},{13,5},{2,10},{6,14},... | collective-permute-start | bytes 6152 | tf_op jit(solution)/shard_map/ppermute | solution.py:238
  48.6 0.3 collective-permute-start.13
  48.9 0.1 pad_add_fusion.place_ref
  49.0 1.1 %collective-permute-done.15.refs_3_ = f32[4,128]{1,0:T(4,128)S(1)} collective-permute-done((f32[4,128]{1,0:T(4,128)S(1)}, f32[4,128]{1,0:T(4,128)S(1)}, u32[]{:S(2)}, u32[]{:S(2)}) %collective-permute-start.15) | collective-permute-done | bytes 2080 | tf_op jit(solution)/shard_map/ppermute | solution.py:238
  50.1 0.8 %collective-permute-done.14.refs_2_ = f32[4,128]{1,0:T(4,128)S(1)} collective-permute-done((f32[4,128]{1,0:T(4,128)S(1)}, f32[4,128]{1,0:T(4,128)S(1)}, u32[]{:S(2)}, u32[]{:S(2)}) %collective-permute-start.14) | collective-permute-done | bytes 2080 | tf_op jit(solution)/shard_map/ppermute | solution.py:238
  50.8 0.0 collective-permute-done.13.refs_1_
  50.8 3.2 %out.1 = f32[512,2048]{1,0:T(8,128)} custom-call(s32[4]{0:T(128)S(1)} %pad_add_fusion.place_ref, f32[4,128]{1,0:T(4,128)S(1)} %get-tuple-element.17.refs_0_, f32[4,128]{1,0:T(4,128)S(1)} %collective-permute-done.13.refs_1_, f32[4,128]{1,0:T(4,128)S(1)} %collective-permute-done.14.refs_2_, f32[4,128]{1,0:T(4,128)S(1)} %collective-permute-done.15.refs_3_, ...), custom_call_target="tpu_custom_call" | custom-call | flops 3145728 | bytes 8388608 | tf_op jit(solution)/shard_map/out/pallas_call | solution.py:199
  (6 shorter events, 0.0 us)
Async XLA Ops:
  0.6 7.3 %collective-permute-start.3 = (bf16[512,768]{1,0:T(8,128)(2,1)}, bf16[512,768]{1,0:T(8,128)(2,1)S(1)}, u32[]{:S(2)}, u32[]{:S(2)}) collective-permute-start(bf16[512,768]{1,0:T(8,128)(2,1)} %bitcast.13), channel_id=1, source_target_pairs={{0,4},{4,0},{8,12},{12,8},{1,5},{5,1},{9,13},{13,9},{2,6},{6,2},{1... | collective-permute-start | bytes 2359304 | tf_op jit(solution)/shard_map/ppermute | solution.py:238
  2.2 12.4 %collective-permute-start.2 = (bf16[256,768]{1,0:T(8,128)(2,1)S(1)}, bf16[256,768]{1,0:T(8,128)(2,1)S(1)}, u32[]{:S(2)}, u32[]{:S(2)}) collective-permute-start(bf16[256,768]{1,0:T(8,128)(2,1)S(1)} %slice_bitcast_fusion), channel_id=1, source_target_pairs={{0,8},{4,12},{8,0},{12,4},{1,9},{5,13},{9,1},{13,5},{2,10},{6,14},... | collective-permute-start | bytes 1179656 | tf_op jit(solution)/shard_map/ppermute | solution.py:238
  4.8 6.9 %collective-permute-start.4 = (bf16[128,768]{1,0:T(8,128)(2,1)}, bf16[128,768]{1,0:T(8,128)(2,1)S(1)}, u32[]{:S(2)}, u32[]{:S(2)}) collective-permute-start(bf16[128,768]{1,0:T(8,128)(2,1)} %bitcast.15), channel_id=1, source_target_pairs={{0,4},{4,0},{8,12},{12,8},{1,5},{5,1},{9,13},{13,9},{2,6},{6,2},{1... | collective-permute-start | bytes 589832 | tf_op jit(solution)/shard_map/ppermute | solution.py:238
  5.0 1.9 %copy-start.2 = (bf16[2048,768]{1,0:T(8,128)(2,1)S(1)}, bf16[2048,768]{1,0:T(8,128)(2,1)}, u32[]{:S(2)}) copy-start(bf16[2048,768]{1,0:T(8,128)(2,1)} %values_ref.1) | copy-start | bytes 9437188
  6.9 1.1 %copy-start.3 = (bf16[1,512,768]{2,1,0:T(8,128)(2,1)S(1)}, bf16[1,512,768]{2,1,0:T(8,128)(2,1)}, u32[]{:S(2)}) copy-start(bf16[1,512,768]{2,1,0:T(8,128)(2,1)} %param.4) | copy-start | bytes 2359300
  7.9 3.8 %copy-start.4 = (bf16[1,128,768]{2,1,0:T(8,128)(2,1)S(1)}, bf16[1,128,768]{2,1,0:T(8,128)(2,1)}, u32[]{:S(2)}) copy-start(bf16[1,128,768]{2,1,0:T(8,128)(2,1)} %param.5) | copy-start | bytes 589828
  12.7 5.6 %copy-start = (f32[256,2048]{1,0:T(8,128)}, f32[256,2048]{1,0:T(8,128)S(1)}, u32[]{:S(2)}) copy-start(f32[256,2048]{1,0:T(8,128)S(1)} %test.2.refs_4_) | copy-start | bytes 6291460
  14.6 1.8 %collective-permute-start.5 = (bf16[256,768]{1,0:T(8,128)(2,1)S(1)}, bf16[256,768]{1,0:T(8,128)(2,1)S(1)}, u32[]{:S(2)}, u32[]{:S(2)}) collective-permute-start(bf16[256,768]{1,0:T(8,128)(2,1)S(1)} %collective-permute-done.2.refs_0_), channel_id=1, source_target_pairs={{0,4},{4,0},{8,12},{12,8},{1,5},{5,1},{9,13},{13,9},{2,6},{6,2},{1... | collective-permute-start | bytes 1179656 | tf_op jit(solution)/shard_map/ppermute | solution.py:238
  14.6 7.4 %collective-permute-start.1 = (bf16[128,768]{1,0:T(8,128)(2,1)S(1)}, bf16[128,768]{1,0:T(8,128)(2,1)S(1)}, u32[]{:S(2)}, u32[]{:S(2)}) collective-permute-start(bf16[128,768]{1,0:T(8,128)(2,1)S(1)} %get-tuple-element.20), channel_id=1, source_target_pairs={{0,8},{4,12},{8,0},{12,4},{1,9},{5,13},{9,1},{13,5},{2,10},{6,14},... | collective-permute-start | bytes 589832 | tf_op jit(solution)/shard_map/ppermute | solution.py:238
  22.0 1.7 %collective-permute-start.6 = (bf16[128,768]{1,0:T(8,128)(2,1)S(1)}, bf16[128,768]{1,0:T(8,128)(2,1)S(1)}, u32[]{:S(2)}, u32[]{:S(2)}) collective-permute-start(bf16[128,768]{1,0:T(8,128)(2,1)S(1)} %collective-permute-done.1.refs_0_), channel_id=1, source_target_pairs={{0,4},{4,0},{8,12},{12,8},{1,5},{5,1},{9,13},{13,9},{2,6},{6,2},{1... | collective-permute-start | bytes 589832 | tf_op jit(solution)/shard_map/ppermute | solution.py:238
  22.0 7.3 %collective-permute-start = (bf16[128,768]{1,0:T(8,128)(2,1)S(1)}, bf16[128,768]{1,0:T(8,128)(2,1)S(1)}, u32[]{:S(2)}, u32[]{:S(2)}) collective-permute-start(bf16[128,768]{1,0:T(8,128)(2,1)S(1)} %get-tuple-element.21), channel_id=1, source_target_pairs={{0,8},{4,12},{8,0},{12,4},{1,9},{5,13},{9,1},{13,5},{2,10},{6,14},... | collective-permute-start | bytes 589832 | tf_op jit(solution)/shard_map/ppermute | solution.py:238
  29.3 1.7 %collective-permute-start.7 = (bf16[128,768]{1,0:T(8,128)(2,1)S(1)}, bf16[128,768]{1,0:T(8,128)(2,1)S(1)}, u32[]{:S(2)}, u32[]{:S(2)}) collective-permute-start(bf16[128,768]{1,0:T(8,128)(2,1)S(1)} %collective-permute-done.refs_0_), channel_id=1, source_target_pairs={{0,4},{4,0},{8,12},{12,8},{1,5},{5,1},{9,13},{13,9},{2,6},{6,2},{1... | collective-permute-start | bytes 589832 | tf_op jit(solution)/shard_map/ppermute | solution.py:238
  29.3 7.3 %collective-permute-start.11 = (bf16[128,768]{1,0:T(8,128)(2,1)S(1)}, bf16[128,768]{1,0:T(8,128)(2,1)S(1)}, u32[]{:S(2)}, u32[]{:S(2)}) collective-permute-start(bf16[128,768]{1,0:T(8,128)(2,1)S(1)} %bitcast.17), channel_id=1, source_target_pairs={{0,8},{4,12},{8,0},{12,4},{1,9},{5,13},{9,1},{13,5},{2,10},{6,14},... | collective-permute-start | bytes 589832 | tf_op jit(solution)/shard_map/ppermute | solution.py:238
  36.6 4.8 %collective-permute-start.12 = (bf16[128,768]{1,0:T(8,128)(2,1)S(1)}, bf16[128,768]{1,0:T(8,128)(2,1)S(1)}, u32[]{:S(2)}, u32[]{:S(2)}) collective-permute-start(bf16[128,768]{1,0:T(8,128)(2,1)S(1)} %collective-permute-done.11.refs_0_), channel_id=1, source_target_pairs={{0,4},{4,0},{8,12},{12,8},{1,5},{5,1},{9,13},{13,9},{2,6},{6,2},{1... | collective-permute-start | bytes 589832 | tf_op jit(solution)/shard_map/ppermute | solution.py:238
  36.6 9.3 %copy-start.1 = (f32[256,2048]{1,0:T(8,128)S(1)}, f32[256,2048]{1,0:T(8,128)}, u32[]{:S(2)}) copy-start(f32[256,2048]{1,0:T(8,128)} %copy-done) | copy-start | bytes 6291460
  36.6 5.9 %collective-permute-start.10 = (f32[1,2048]{1,0:T(1,128)S(1)}, f32[1,2048]{1,0:T(1,128)S(1)}, u32[]{:S(2)}, u32[]{:S(2)}) collective-permute-start(f32[1,2048]{1,0:T(1,128)S(1)} %bank.7.refs_0_), channel_id=1, source_target_pairs={{0,3},{1,0},{2,1},{3,2},{4,7},{5,4},{6,5},{7,6},{8,11},{9,8},{10,9... | collective-permute-start | bytes 24584 | tf_op jit(solution)/shard_map/ppermute | solution.py:264
  40.4 4.5 %collective-permute-start.9 = (f32[1,2048]{1,0:T(1,128)S(1)}, f32[1,2048]{1,0:T(1,128)S(1)}, u32[]{:S(2)}, u32[]{:S(2)}) collective-permute-start(f32[1,2048]{1,0:T(1,128)S(1)} %bank.7.refs_0_), channel_id=1, source_target_pairs={{0,2},{1,3},{2,0},{3,1},{4,6},{5,7},{6,4},{7,5},{8,10},{9,11},{10,... | collective-permute-start | bytes 24584 | tf_op jit(solution)/shard_map/ppermute | solution.py:264
  40.4 5.4 %collective-permute-start.8 = (f32[1,2048]{1,0:T(1,128)S(1)}, f32[1,2048]{1,0:T(1,128)S(1)}, u32[]{:S(2)}, u32[]{:S(2)}) collective-permute-start(f32[1,2048]{1,0:T(1,128)S(1)} %bank.7.refs_0_), channel_id=1, source_target_pairs={{0,1},{1,2},{2,3},{3,0},{4,5},{5,6},{6,7},{7,4},{8,9},{9,10},{10,1... | collective-permute-start | bytes 24584 | tf_op jit(solution)/shard_map/ppermute | solution.py:264
  47.1 3.0 %collective-permute-start.15 = (f32[4,128]{1,0:T(4,128)S(1)}, f32[4,128]{1,0:T(4,128)S(1)}, u32[]{:S(2)}, u32[]{:S(2)}) collective-permute-start(f32[4,128]{1,0:T(4,128)S(1)} %get-tuple-element.17.refs_0_), channel_id=1, source_target_pairs={{0,12},{4,8},{8,4},{12,0},{1,13},{5,9},{9,5},{13,1},{2,14},{6,10},... | collective-permute-start | bytes 6152 | tf_op jit(solution)/shard_map/ppermute | solution.py:238
  47.3 3.6 %collective-permute-start.14 = (f32[4,128]{1,0:T(4,128)S(1)}, f32[4,128]{1,0:T(4,128)S(1)}, u32[]{:S(2)}, u32[]{:S(2)}) collective-permute-start(f32[4,128]{1,0:T(4,128)S(1)} %get-tuple-element.17.refs_0_), channel_id=1, source_target_pairs={{0,8},{4,12},{8,0},{12,4},{1,9},{5,13},{9,1},{13,5},{2,10},{6,14},... | collective-permute-start | bytes 6152 | tf_op jit(solution)/shard_map/ppermute | solution.py:238
  48.6 2.3 %collective-permute-start.13 = (f32[4,128]{1,0:T(4,128)S(1)}, f32[4,128]{1,0:T(4,128)S(1)}, u32[]{:S(2)}, u32[]{:S(2)}) collective-permute-start(f32[4,128]{1,0:T(4,128)S(1)} %get-tuple-element.17.refs_0_), channel_id=1, source_target_pairs={{0,4},{4,0},{8,12},{12,8},{1,5},{5,1},{9,13},{13,9},{2,6},{6,2},{1... | collective-permute-start | bytes 6152 | tf_op jit(solution)/shard_map/ppermute | solution.py:238

commit v2 on v1

v2 whole, which is shorter than its diff:
```python
import functools
import math

import jax
import jax.numpy as jnp
from jax import lax
from jax.experimental import pallas as pl
from jax.experimental.pallas import tpu as pltpu
from jax.sharding import PartitionSpec as P


sharpness = 20.0
LOG2E = math.log2(math.e)
LANES = 128


VMEM = pl.BlockSpec(memory_space=pltpu.VMEM)


def params(mib):
    return pltpu.CompilerParams(vmem_limit_bytes=mib << 20)


def unit_rows(values):
    wide = values.astype(jnp.float32)
    scaled = wide * lax.rsqrt(jnp.sum(wide * wide, axis=-1, keepdims=True) + 1e-06)
    return scaled.astype(jnp.bfloat16)


def inner(rows, columns):
    return lax.dot_general(
        rows, columns, (((1,), (1,)), ((), ())), preferred_element_type=jnp.float32
    )


def unit_kernel(values_ref, unit_ref):
    unit_ref[...] = unit_rows(values_ref[...])


def unit_call(values):
    return pl.pallas_call(
        unit_kernel,
        out_shape=jax.ShapeDtypeStruct(values.shape, jnp.bfloat16),
        in_specs=[VMEM],
        out_specs=VMEM,
        compiler_params=params(16),
        name="unit",
        cost_estimate=pl.CostEstimate(
            flops=4 * values.size, bytes_accessed=4 * values.size, transcendentals=values.shape[0]
        ),
    )(values)


def bank_kernel(count, tile, *refs):
    blocks, gallery_ref, earlier, total_ref = (
        refs[:count],
        refs[count],
        refs[count + 1 : -1],
        refs[-1],
    )
    units = [unit_rows(block[...]) for block in blocks]
    unit = jnp.concatenate(units, axis=0) if count > 1 else units[0]
    for start in range(0, gallery_ref.shape[0], tile):
        scores = inner(unit, gallery_ref[start : start + tile, :])
        total = jnp.sum(jnp.exp2(scores * (sharpness * LOG2E)), axis=0, keepdims=True)
        for other in earlier:
            total = total + other[:, start : start + tile]
        total_ref[:, start : start + tile] = total


def bank_call(blocks, gallery_unit, earlier=()):
    columns, depth = gallery_unit.shape
    rows = sum(block.shape[0] for block in blocks)
    tile = math.gcd(columns, 256)
    return pl.pallas_call(
        functools.partial(bank_kernel, len(blocks), tile),
        out_shape=jax.ShapeDtypeStruct((1, columns), jnp.float32),
        in_specs=[VMEM] * (len(blocks) + 1 + len(earlier)),
        out_specs=VMEM,
        compiler_params=params(16),
        name="bank",
        cost_estimate=pl.CostEstimate(
            flops=2 * rows * columns * depth,
            bytes_accessed=2 * depth * (rows + columns),
            transcendentals=rows * columns,
        ),
    )(*blocks, gallery_unit, *earlier)


def test_kernel(count, tile, *refs):
    blocks, gallery_ref, (score_ref, power_ref) = refs[:count], refs[count], refs[-2:]
    units = [unit_rows(block[...]) for block in blocks]
    unit = jnp.concatenate(units, axis=0) if count > 1 else units[0]
    for start in range(0, gallery_ref.shape[0], tile):
        scores = inner(unit, gallery_ref[start : start + tile, :])
        score_ref[:, start : start + tile] = scores * sharpness
        power_ref[:, start : start + tile] = jnp.exp2(scores * (sharpness * LOG2E))


def test_call(blocks, gallery_unit):
    columns, depth = gallery_unit.shape
    rows = sum(block.shape[0] for block in blocks)
    tile = math.gcd(columns, 256)
    shape = jax.ShapeDtypeStruct((rows, columns), jnp.float32)
    return pl.pallas_call(
        functools.partial(test_kernel, len(blocks), tile),
        out_shape=(shape, shape),
        in_specs=[VMEM] * (len(blocks) + 1),
        out_specs=(VMEM, VMEM),
        compiler_params=params(16),
        name="test",
        cost_estimate=pl.CostEstimate(
            flops=2 * rows * columns * depth,
            bytes_accessed=2 * depth * (rows + columns) + 8 * rows * columns,
            transcendentals=rows * columns,
        ),
    )(*blocks, gallery_unit)


def keep_kernel(total_ref, kept_ref):
    kept_ref[...] = total_ref[...]


def keep_call(total):
    return pl.pallas_call(
        keep_kernel,
        out_shape=jax.ShapeDtypeStruct(total.shape, total.dtype),
        in_specs=[VMEM],
        out_specs=VMEM,
        compiler_params=params(16),
        name="keep",
        cost_estimate=pl.CostEstimate(
            flops=total.size, bytes_accessed=8 * total.size, transcendentals=0
        ),
    )(total)


def row_kernel(groups, *refs):
    totals, powers, (total_ref, rows_ref, inverse_ref) = (
        refs[:groups],
        refs[groups:-3],
        refs[-3:],
    )
    total = totals[0][...]
    for other in totals[1:]:
        total = total + other[...]
    total_ref[...] = total
    inverse_ref[...] = 1.0 / total
    width = rows_ref.shape[1]
    place = 0
    for power_ref in powers:
        for first in range(0, power_ref.shape[0], width):
            running = jnp.zeros((width, LANES), jnp.float32)
            for start in range(0, total_ref.shape[1], LANES):
                cut = slice(start, start + LANES)
                running = running + power_ref[first : first + width, cut] * inverse_ref[:, cut]
            rows_ref[place : place + 1, :] = jnp.sum(running.T, axis=0, keepdims=True)
            place += 1


def row_call(totals, powers, width):
    columns = powers[0].shape[1]
    rows = sum(power.shape[0] for power in powers)
    return pl.pallas_call(
        functools.partial(row_kernel, len(totals)),
        out_shape=(
            jax.ShapeDtypeStruct((1, columns), jnp.float32),
            jax.ShapeDtypeStruct((rows // width, width), jnp.float32),
        ),
        in_specs=[VMEM] * (len(totals) + len(powers)),
        out_specs=(VMEM, VMEM),
        scratch_shapes=[pltpu.VMEM((1, columns), jnp.float32)],
        compiler_params=params(16),
        name="rows",
        cost_estimate=pl.CostEstimate(
            flops=2 * rows * columns, bytes_accessed=4 * rows * columns, transcendentals=0
        ),
    )(*totals, *powers)


def log_kernel(total_ref, log_ref, again_ref):
    value = jnp.log(total_ref[...])
    log_ref[...] = value
    again_ref[...] = value


def log_call(total):
    shape = jax.ShapeDtypeStruct(total.shape, jnp.float32)
    return pl.pallas_call(
        log_kernel,
        out_shape=(shape, shape),
        in_specs=[VMEM],
        out_specs=(VMEM, VMEM),
        compiler_params=params(16),
        name="logs",
        cost_estimate=pl.CostEstimate(
            flops=total.size, bytes_accessed=12 * total.size, transcendentals=total.size
        ),
    )(total)


def out_kernel(origins, orders, pairs, core, height, *refs):
    count = len(origins)
    parts, scores, (log_ref, out_ref, stage, sems) = (
        refs[:count],
        refs[count:-4],
        refs[-4:],
    )
    width = parts[0].shape[1]
    line = height // width
    step = math.gcd(width, 64)
    where = lax.axis_index("gal")
    pair_at, core_at = lax.div(where, core), lax.rem(where, core)
    rows_of = [(score, first) for score in scores for first in range(0, score.shape[0], height)]
    copies = []
    for block, (pair, flip) in enumerate(origins):
        side = core_at if flip == 0 else 1 - core_at
        place = (lax.rem(pair_at + (pairs - pair), pairs) * core + side) * height
        source, first = rows_of[block]
        for sub in range(0, height, width):
            total = None
            for part, order in zip(parts, orders):
                at = order[block] * line + sub // width
                row = part[at : at + 1, :]
                total = row if total is None else total + row
            wide = jnp.broadcast_to(jnp.log(total), (LANES, width)).T
            for piece in range(0, width, step):
                at = len(copies) * step
                begin = first + sub + piece
                for start in range(0, log_ref.shape[1], LANES):
                    cut = slice(start, start + LANES)
                    value = source[begin : begin + step, cut] - log_ref[:, cut]
                    stage[at : at + step, cut] = value - wide[piece : piece + step, :]
                target = pl.multiple_of(place + (sub + piece), step)
                copies.append(
                    pltpu.make_async_copy(
                        stage.at[pl.ds(at, step)],
                        out_ref.at[pl.ds(target, step)],
                        sems.at[len(copies)],
                    )
                )
                if len(copies) > 1:
                    copies[-2].start()
    copies[-1].start()
    for copy in copies:
        copy.wait()


def out_call(origins, orders, pairs, core, parts, scores, log_total):
    columns = log_total.shape[1]
    rows = sum(score.shape[0] for score in scores)
    height = rows // len(origins)
    step = math.gcd(parts[0].shape[1], 64)
    return pl.pallas_call(
        functools.partial(out_kernel, origins, orders, pairs, core, height),
        out_shape=jax.ShapeDtypeStruct((rows, columns), jnp.float32),
        in_specs=[VMEM] * (len(parts) + len(scores) + 1),
        out_specs=pl.BlockSpec(memory_space=pl.ANY),
        scratch_shapes=[
            pltpu.VMEM((rows, columns), jnp.float32),
            pltpu.SemaphoreType.DMA((rows // step,)),
        ],
        compiler_params=params(16),
        name="out",
        cost_estimate=pl.CostEstimate(
            flops=3 * rows * columns, bytes_accessed=8 * rows * columns, transcendentals=0
        ),
    )(*parts, *scores, log_total)


def after(value, token):
    return lax.optimization_barrier((value, token))[0]


def chunk_sizes(rows):
    if rows % 128:
        return [rows]
    first, last = rows // 4, rows // 8
    middle = rows - first - last
    half = (middle // 2 + 15) // 16 * 16
    return [first, half, middle - half, last]


def per_device(gallery, querybank, test_queries):
    bank = querybank[0]
    test = test_queries[0]
    gal = lax.axis_size("gal")
    groups = lax.axis_size("qb")
    core = 2 if gal % 2 == 0 else 1
    pairs = gal // core

    def shift(value, pair, flip):
        moves = [
            (i, (i // core + pair) % pairs * core + (i % core ^ flip)) for i in range(gal)
        ]
        return lax.ppermute(value, "gal", moves)

    sizes = chunk_sizes(bank.shape[0])
    starts = [sum(sizes[:i]) for i in range(len(sizes))]
    chunks = [lax.slice_in_dim(bank, s, s + n, axis=0) for s, n in zip(starts, sizes)]

    crossed = []
    for chunk in chunks:
        crossed += [shift(chunk, pair, 0) for pair in range(1, pairs)]
    test_crossed = [shift(test, pair, 0) for pair in range(1, pairs)]

    near, near_tests = [bank], [test]
    if core == 2:
        near.append(shift(bank, 0, 1))
        near_tests.append(shift(test, 0, 1))
    gallery_unit = unit_call(gallery)
    total = bank_call(near, gallery_unit)
    tables = [test_call(near_tests, after(gallery_unit, total))]
    total = after(total, tables[0][0])

    behind = [total, total]
    for block in crossed:
        blocks = [after(block, behind[-2])]
        if core == 2:
            blocks.append(shift(blocks[0], 0, 1))
        behind.append(bank_call(blocks, gallery_unit, [behind[-1]]))
    total = behind[-1]

    totals = [total]
    for s in range(1, groups):
        totals.append(
            lax.ppermute(total, "qb", [(i, (i + s) % groups) for i in range(groups)])
        )
    totals[0] = keep_call(total)
    for block in test_crossed:
        block = after(block, totals[0])
        blocks = [block]
        if core == 2:
            blocks.append(shift(block, 0, 1))
        for part in blocks:
            tables.append(test_call([part], gallery_unit))
    scores = [score for score, _ in tables]
    width = math.gcd(test.shape[0], LANES)
    total, part = row_call(totals, [power for _, power in tables], width)

    origins = [(pair, flip) for pair in range(pairs) for flip in range(core)]
    parts = [part]
    orders = [list(range(len(origins)))]
    for pair, flip in origins[1:]:
        parts.append(shift(part, pair, flip))
        orders.append(
            [origins.index(((p - pair) % pairs, f ^ flip)) for p, f in origins]
        )
    log_total, normalizer = log_call(total)
    logprob = out_call(origins, orders, pairs, core, parts, scores, log_total)
    return (logprob, normalizer.reshape(-1))


def solution(mesh):
    placed = (
        P(("slab", "gal"), None),
        P(("slab", "qb"), "gal", None),
        P(("slab", "qb"), "gal", None),
    )

    return jax.shard_map(
        per_device,
        mesh=mesh,
        in_specs=placed,
        out_specs=(P(("slab", "qb"), "gal"), P(("slab", "gal"))),
        check_vma=False,
    )
```

time: 54.3 us -> 48.2 us (0.89)
  waiting for transfers between devices: 19.7 us -> 11.1 us
  Pallas kernels: 15.1 us -> 16.2 us
  local copies, waits for them, and re-layouts: 3.09 us -> 4.07 us
    ppermute x13 -> x15, waiting for transfers between devices: 16.3 us -> 11.1 us  [shift(): return lax.ppermute(value, 'gal', moves)]
    ppermute x3, waiting for transfers between devices: 3.37 us -> 0.01 us  [per_device(): lax.ppermute(total, 'qb', [(i, (i + s) % groups) for i in range(groups)])]
    pallas_call x2 -> x3, Pallas kernels: 2.1 us -> 3.47 us  [test_call(): pl.pallas_call(functools.partial(test_kernel, len(blocks), tile), out_sha...]
    pallas_call x2 -> x4, Pallas kernels: 4.38 us -> 3.34 us  [the longest x1 2.34 us: out_call(): pl.pallas_call(functools.partial(out_kernel, origins, orders, pairs, core...]
    slice x2 -> x3, local copies, waits for them, and re-layouts: 1.05 us -> 2.04 us  [per_device(): lax.slice_in_dim(bank, s, s + n, axis=0)]
    ppermute x3, starting transfers between devices: 4.84 us -> 5.73 us  [per_device(): lax.ppermute(total, 'qb', [(i, (i + s) % groups) for i in range(groups)])]
    pallas_call x4 -> x5, Pallas kernels: 7.67 us -> 8.43 us  [bank_call(): pl.pallas_call(functools.partial(bank_kernel, len(blocks), tile), out_sha...]
    ppermute x13 -> x15, starting transfers between devices: 10.5 us -> 10 us  [shift(): return lax.ppermute(value, 'gal', moves)]
  transfers between devices with their start and end apart: 16 -> 18, of which waited for: 8 -> 5; matrix products, arithmetic and copies ran while one was open for 2% -> 4% of each run, Pallas kernels for 20% -> 28%
where the time goes in v2:
time: 48.2 us; the launch traced here: 47.9 us
  Pallas kernels  16.2 us (34%)
  starting transfers between devices  15.8 us (33%)
  waiting for transfers between devices  11.1 us (23%)
  local copies, waits for them, and re-layouts  4.07 us (8%)
  between operations  0.84 us (2%)
    ppermute x15, waiting for transfers between devices, shift(): return lax.ppermute(value, 'gal', moves)  11.1 us
    ppermute x15, starting transfers between devices, shift(): return lax.ppermute(value, 'gal', moves)  10 us
    pallas_call x5, Pallas kernels, bank_call(): pl.pallas_call(functools.partial(bank_kernel, len(blocks), tile), out_sha...  8.43 us
    ppermute x3, starting transfers between devices, per_device(): lax.ppermute(total, 'qb', [(i, (i + s) % groups) for i in range(groups)])  5.73 us
    pallas_call x3, Pallas kernels, test_call(): pl.pallas_call(functools.partial(test_kernel, len(blocks), tile), out_sha...  3.47 us
    pallas_call x1, Pallas kernels, out_call(): pl.pallas_call(functools.partial(out_kernel, origins, orders, pairs, core...  2.34 us
    slice x3, local copies, waits for them, and re-layouts, per_device(): lax.slice_in_dim(bank, s, s + n, axis=0)  2.04 us
    unnamed x6, local copies, waits for them, and re-layouts  2.02 us
  transfers between devices with their start and end apart: 18, of which 5 were waited for; matrix products, arithmetic and copies ran while one was open for 4% of the time, Pallas kernels for 28%

profile of v2, /device:TPU:0, one launch (start us, length us, event | category | flops | bytes accessed | tf_op | source)
XLA Modules:
  0.0 47.9 jit_solution(5373662734211114369)
XLA Ops:
  0.6 0.6 %collective-permute-start.2 = (bf16[512,768]{1,0:T(8,128)(2,1)}, bf16[512,768]{1,0:T(8,128)(2,1)S(1)}, u32[]{:S(2)}, u32[]{:S(2)}) collective-permute-start(bf16[512,768]{1,0:T(8,128)(2,1)} %bitcast.11), channel_id=1, source_target_pairs={{0,4},{4,0},{8,12},{12,8},{1,5},{5,1},{9,13},{13,9},{2,6},{6,2},{1... | collective-permute-start | bytes 2359304 | tf_op jit(solution)/shard_map/ppermute | solution.py:296
  1.2 0.1 collective-permute-start.3
  1.3 0.9 %slice_bitcast_fusion.2 = bf16[128,768]{1,0:T(8,128)(2,1)S(1)} fusion(bf16[1,512,768]{2,1,0:T(8,128)(2,1)} %param.4), kind=kLoop, calls=%fused_computation.2 | loop fusion | bytes 393216 | tf_op jit(solution)/shard_map/slice | solution.py:300
  2.2 3.0 %collective-permute-start.5 = (bf16[128,768]{1,0:T(8,128)(2,1)S(1)}, bf16[128,768]{1,0:T(8,128)(2,1)S(1)}, u32[]{:S(2)}, u32[]{:S(2)}) collective-permute-start(bf16[128,768]{1,0:T(8,128)(2,1)S(1)} %slice_bitcast_fusion.2), channel_id=1, source_target_pairs={{0,8},{4,12},{8,0},{12,4},{1,9},{5,13},{9,1},{13,5},{2,10},{6,14},... | collective-permute-start | bytes 589832 | tf_op jit(solution)/shard_map/ppermute | solution.py:296
  5.2 1.1 %slice_bitcast_fusion = (bf16[160,768]{1,0:T(8,128)(2,1)S(1)}, bf16[160,768]{1,0:T(8,128)(2,1)S(1)}) fusion(bf16[1,512,768]{2,1,0:T(8,128)(2,1)} %param.4), kind=kLoop, calls=%fused_computation | loop fusion | bytes 983040 | tf_op jit(solution)/shard_map/slice | solution.py:300
  6.3 0.1 collective-permute-start.1
  6.4 1.9 %copy-done = bf16[2048,768]{1,0:T(8,128)(2,1)S(1)} copy-done((bf16[2048,768]{1,0:T(8,128)(2,1)S(1)}, bf16[2048,768]{1,0:T(8,128)(2,1)}, u32[]{:S(2)}) %copy-start) | copy-done | bytes 3145752
  8.3 1.0 %unit.1.refs_2_.refs_1_ = bf16[2048,768]{1,0:T(8,128)(2,1)S(1)} custom-call(bf16[2048,768]{1,0:T(8,128)(2,1)S(1)} %copy-done), custom_call_target="tpu_custom_call" | custom-call | flops 6291456 | bytes 6291456 | tf_op jit(solution)/shard_map/unit/pallas_call | solution.py:41
  9.3 0.0 copy-start.2
  9.3 0.0 collective-permute-done.2.refs_1_
  9.3 0.1 copy-done.1
  9.4 3.6 %bank.5.refs_3_ = f32[1,2048]{1,0:T(1,128)S(1)} custom-call(bf16[512,768]{1,0:T(8,128)(2,1)S(1)} %bitcast.12, bf16[512,768]{1,0:T(8,128)(2,1)S(1)} %collective-permute-done.2.refs_1_, bf16[2048,768]{1,0:T(8,128)(2,1)S(1)} %unit.1.refs_2_.refs_1_), custom_call_target="tpu_custom_call" | custom-call | flops 3221225472 | bytes 4718592 | tf_op jit(solution)/shard_map/bank/pallas_call | solution.py:75
  13.0 0.0 collective-permute-done.3.refs_1_
  13.0 1.1 %test.3 = (f32[256,2048]{1,0:T(8,128)S(1)}, f32[256,2048]{1,0:T(8,128)S(1)}) custom-call(bf16[128,768]{1,0:T(8,128)(2,1)S(1)} %bitcast.14, bf16[128,768]{1,0:T(8,128)(2,1)S(1)} %collective-permute-done.3.refs_1_, bf16[2048,768]{1,0:T(8,128)(2,1)S(1)} %unit.1.refs_2_.refs_1_), custom_call_target="tpu_custom_call" | custom-call | flops 805306368 | bytes 7733248 | tf_op jit(solution)/shard_map/test/pallas_call | solution.py:105
  14.1 0.0 collective-permute-done.5.refs_0_
  14.1 0.1 collective-permute-start.6
  14.2 2.1 %collective-permute-start.8 = (bf16[160,768]{1,0:T(8,128)(2,1)S(1)}, bf16[160,768]{1,0:T(8,128)(2,1)S(1)}, u32[]{:S(2)}, u32[]{:S(2)}) collective-permute-start(bf16[160,768]{1,0:T(8,128)(2,1)S(1)} %get-tuple-element.36), channel_id=1, source_target_pairs={{0,8},{4,12},{8,0},{12,4},{1,9},{5,13},{9,1},{13,5},{2,10},{6,14},... | collective-permute-start | bytes 737288 | tf_op jit(solution)/shard_map/ppermute | solution.py:296
  16.3 0.2 collective-permute-start.4
  16.4 0.0 collective-permute-done.6.refs_1_
  16.4 1.1 %bank.6.refs_3_ = f32[1,2048]{1,0:T(1,128)S(1)} custom-call(bf16[128,768]{1,0:T(8,128)(2,1)S(1)} %collective-permute-done.5.refs_0_, bf16[128,768]{1,0:T(8,128)(2,1)S(1)} %collective-permute-done.6.refs_1_, bf16[2048,768]{1,0:T(8,128)(2,1)S(1)} %unit.1.refs_2_.refs_1_, f32[1,2048]{1,0:T(1,128)S(1)} %bank.5.refs_3_), custom_call_target="tpu_custom_call" | custom-call | flops 805306368 | bytes 3538944 | tf_op jit(solution)/shard_map/bank/pallas_call | solution.py:75
  17.5 5.3 %collective-permute-done.8.refs_0_ = bf16[160,768]{1,0:T(8,128)(2,1)S(1)} collective-permute-done((bf16[160,768]{1,0:T(8,128)(2,1)S(1)}, bf16[160,768]{1,0:T(8,128)(2,1)S(1)}, u32[]{:S(2)}, u32[]{:S(2)}) %collective-permute-start.8) | collective-permute-done | bytes 245792 | tf_op jit(solution)/shard_map/ppermute | solution.py:296
  22.9 1.8 %collective-permute-start = (bf16[64,768]{1,0:T(8,128)(2,1)S(1)}, bf16[64,768]{1,0:T(8,128)(2,1)S(1)}, u32[]{:S(2)}, u32[]{:S(2)}) collective-permute-start(bf16[64,768]{1,0:T(8,128)(2,1)S(1)} %slice_bitcast_fusion.3), channel_id=1, source_target_pairs={{0,8},{4,12},{8,0},{12,4},{1,9},{5,13},{9,1},{13,5},{2,10},{6,14},... | collective-permute-start | bytes 294920 | tf_op jit(solution)/shard_map/ppermute | solution.py:296
  24.7 0.3 collective-permute-start.13
  24.9 0.0 collective-permute-done.4.refs_1_
  24.9 1.3 %bank.7.refs_3_ = f32[1,2048]{1,0:T(1,128)S(1)} custom-call(bf16[160,768]{1,0:T(8,128)(2,1)S(1)} %collective-permute-done.1.refs_0_, bf16[160,768]{1,0:T(8,128)(2,1)S(1)} %collective-permute-done.4.refs_1_, bf16[2048,768]{1,0:T(8,128)(2,1)S(1)} %unit.1.refs_2_.refs_1_, f32[1,2048]{1,0:T(1,128)S(1)} %bank.6.refs_3_), custom_call_target="tpu_custom_call" | custom-call | flops 1006632960 | bytes 3637248 | tf_op jit(solution)/shard_map/bank/pallas_call | solution.py:75
  26.2 2.4 %collective-permute-done.refs_0_ = bf16[64,768]{1,0:T(8,128)(2,1)S(1)} collective-permute-done((bf16[64,768]{1,0:T(8,128)(2,1)S(1)}, bf16[64,768]{1,0:T(8,128)(2,1)S(1)}, u32[]{:S(2)}, u32[]{:S(2)}) %collective-permute-start) | collective-permute-done | bytes 98336 | tf_op jit(solution)/shard_map/ppermute | solution.py:296
  28.6 0.0 collective-permute-start.7
  28.6 1.3 %bank.8.refs_3_ = f32[1,2048]{1,0:T(1,128)S(1)} custom-call(bf16[160,768]{1,0:T(8,128)(2,1)S(1)} %collective-permute-done.8.refs_0_, bf16[160,768]{1,0:T(8,128)(2,1)S(1)} %collective-permute-done.9.refs_1_, bf16[2048,768]{1,0:T(8,128)(2,1)S(1)} %unit.1.refs_2_.refs_1_, f32[1,2048]{1,0:T(1,128)S(1)} %bank.7.refs_3_), custom_call_target="tpu_custom_call" | custom-call | flops 1006632960 | bytes 3637248 | tf_op jit(solution)/shard_map/bank/pallas_call | solution.py:75
  29.9 1.2 %bank.9.total_ref = f32[1,2048]{1,0:T(1,128)S(1)} custom-call(bf16[64,768]{1,0:T(8,128)(2,1)S(1)} %collective-permute-done.refs_0_, bf16[64,768]{1,0:T(8,128)(2,1)S(1)} %collective-permute-done.7.refs_1_, bf16[2048,768]{1,0:T(8,128)(2,1)S(1)} %unit.1.refs_2_.refs_1_, f32[1,2048]{1,0:T(1,128)S(1)} %bank.8.refs_3_), custom_call_target="tpu_custom_call" | custom-call | flops 402653184 | bytes 3342336 | tf_op jit(solution)/shard_map/bank/pallas_call | solution.py:75
  31.1 1.2 %collective-permute-done.13.refs_0_ = bf16[128,768]{1,0:T(8,128)(2,1)S(1)} collective-permute-done((bf16[128,768]{1,0:T(8,128)(2,1)S(1)}, bf16[128,768]{1,0:T(8,128)(2,1)S(1)}, u32[]{:S(2)}, u32[]{:S(2)}) %collective-permute-start.13) | collective-permute-done | bytes 196640 | tf_op jit(solution)/shard_map/ppermute | solution.py:296
  32.3 0.0 collective-permute-start.14
  32.3 1.8 %collective-permute-start.10 = (f32[1,2048]{1,0:T(1,128)S(1)}, f32[1,2048]{1,0:T(1,128)S(1)}, u32[]{:S(2)}, u32[]{:S(2)}) collective-permute-start(f32[1,2048]{1,0:T(1,128)S(1)} %bank.9.total_ref), channel_id=1, source_target_pairs={{0,1},{1,2},{2,3},{3,0},{4,5},{5,6},{6,7},{7,4},{8,9},{9,10},{10,1... | collective-permute-start | bytes 24584 | tf_op jit(solution)/shard_map/ppermute | solution.py:327
  34.1 2.6 %collective-permute-start.11 = (f32[1,2048]{1,0:T(1,128)S(1)}, f32[1,2048]{1,0:T(1,128)S(1)}, u32[]{:S(2)}, u32[]{:S(2)}) collective-permute-start(f32[1,2048]{1,0:T(1,128)S(1)} %bank.9.total_ref), channel_id=1, source_target_pairs={{0,2},{1,3},{2,0},{3,1},{4,6},{5,7},{6,4},{7,5},{8,10},{9,11},{10,... | collective-permute-start | bytes 24584 | tf_op jit(solution)/shard_map/ppermute | solution.py:327
  36.7 1.3 %collective-permute-start.12 = (f32[1,2048]{1,0:T(1,128)S(1)}, f32[1,2048]{1,0:T(1,128)S(1)}, u32[]{:S(2)}, u32[]{:S(2)}) collective-permute-start(f32[1,2048]{1,0:T(1,128)S(1)} %bank.9.total_ref), channel_id=1, source_target_pairs={{0,3},{1,0},{2,1},{3,2},{4,7},{5,4},{6,5},{7,6},{8,11},{9,8},{10,9... | collective-permute-start | bytes 24584 | tf_op jit(solution)/shard_map/ppermute | solution.py:327
  38.1 1.2 %test.4 = (f32[128,2048]{1,0:T(8,128)S(1)}, f32[128,2048]{1,0:T(8,128)S(1)}) custom-call(bf16[128,768]{1,0:T(8,128)(2,1)S(1)} %collective-permute-done.13.refs_0_, bf16[2048,768]{1,0:T(8,128)(2,1)S(1)} %unit.1.refs_2_.refs_1_), custom_call_target="tpu_custom_call" | custom-call | flops 402653184 | bytes 5439488 | tf_op jit(solution)/shard_map/test/pallas_call | solution.py:105
  39.3 0.0 collective-permute-done.14.refs_0_
  39.3 1.2 %test.5 = (f32[128,2048]{1,0:T(8,128)S(1)}, f32[128,2048]{1,0:T(8,128)S(1)}) custom-call(bf16[128,768]{1,0:T(8,128)(2,1)S(1)} %collective-permute-done.14.refs_0_, bf16[2048,768]{1,0:T(8,128)(2,1)S(1)} %unit.1.refs_2_.refs_1_), custom_call_target="tpu_custom_call" | custom-call | flops 402653184 | bytes 5439488 | tf_op jit(solution)/shard_map/test/pallas_call | solution.py:105
  40.5 0.0 collective-permute-done.11.refs_2_
  40.5 0.0 collective-permute-done.12.refs_3_
  40.5 0.4 rows.1
  40.9 0.1 collective-permute-start.15
  41.0 1.6 %collective-permute-start.16 = (f32[4,128]{1,0:T(4,128)S(1)}, f32[4,128]{1,0:T(4,128)S(1)}, u32[]{:S(2)}, u32[]{:S(2)}) collective-permute-start(f32[4,128]{1,0:T(4,128)S(1)} %get-tuple-element.30.refs_0_), channel_id=1, source_target_pairs={{0,8},{4,12},{8,0},{12,4},{1,9},{5,13},{9,1},{13,5},{2,10},{6,14},... | collective-permute-start | bytes 6152 | tf_op jit(solution)/shard_map/ppermute | solution.py:296
  42.6 0.2 collective-permute-start.17
  42.8 0.6 %logs.1 = (f32[1,2048]{1,0:T(1,128)S(1)}, f32[1,2048]{1,0:T(1,128)}) custom-call(f32[1,2048]{1,0:T(1,128)S(1)} %get-tuple-element.33.total_ref), custom_call_target="tpu_custom_call" | custom-call | flops 2048 | bytes 24576 | tf_op jit(solution)/shard_map/logs/pallas_call | solution.py:189
  43.4 0.0 collective-permute-done.15.refs_1_
  43.4 1.2 %collective-permute-done.16.refs_2_ = f32[4,128]{1,0:T(4,128)S(1)} collective-permute-done((f32[4,128]{1,0:T(4,128)S(1)}, f32[4,128]{1,0:T(4,128)S(1)}, u32[]{:S(2)}, u32[]{:S(2)}) %collective-permute-start.16) | collective-permute-done | bytes 2080 | tf_op jit(solution)/shard_map/ppermute | solution.py:296
  44.6 1.0 %collective-permute-done.17.refs_3_ = f32[4,128]{1,0:T(4,128)S(1)} collective-permute-done((f32[4,128]{1,0:T(4,128)S(1)}, f32[4,128]{1,0:T(4,128)S(1)}, u32[]{:S(2)}, u32[]{:S(2)}) %collective-permute-start.17) | collective-permute-done | bytes 2080 | tf_op jit(solution)/shard_map/ppermute | solution.py:296
  45.6 2.3 %out.1 = f32[512,2048]{1,0:T(8,128)} custom-call(f32[4,128]{1,0:T(4,128)S(1)} %get-tuple-element.30.refs_0_, f32[4,128]{1,0:T(4,128)S(1)} %collective-permute-done.15.refs_1_, f32[4,128]{1,0:T(4,128)S(1)} %collective-permute-done.16.refs_2_, f32[4,128]{1,0:T(4,128)S(1)} %collective-permute-done.17.refs_3_, f32[256,2048]{1,0:T(8,128)S(1)} %get-tuple-element.20.refs_4_, ...), custom_call_target="tpu_custom_call" | custom-call | flops 3145728 | bytes 8388608 | tf_op jit(solution)/shard_map/out/pallas_call | solution.py:254
  (10 shorter events, 0.0 us)
Async XLA Ops:
  0.6 8.6 %collective-permute-start.2 = (bf16[512,768]{1,0:T(8,128)(2,1)}, bf16[512,768]{1,0:T(8,128)(2,1)S(1)}, u32[]{:S(2)}, u32[]{:S(2)}) collective-permute-start(bf16[512,768]{1,0:T(8,128)(2,1)} %bitcast.11), channel_id=1, source_target_pairs={{0,4},{4,0},{8,12},{12,8},{1,5},{5,1},{9,13},{13,9},{2,6},{6,2},{1... | collective-permute-start | bytes 2359304 | tf_op jit(solution)/shard_map/ppermute | solution.py:296
  1.2 11.8 %collective-permute-start.3 = (bf16[128,768]{1,0:T(8,128)(2,1)}, bf16[128,768]{1,0:T(8,128)(2,1)S(1)}, u32[]{:S(2)}, u32[]{:S(2)}) collective-permute-start(bf16[128,768]{1,0:T(8,128)(2,1)} %bitcast.13), channel_id=1, source_target_pairs={{0,4},{4,0},{8,12},{12,8},{1,5},{5,1},{9,13},{13,9},{2,6},{6,2},{1... | collective-permute-start | bytes 589832 | tf_op jit(solution)/shard_map/ppermute | solution.py:296
  2.2 11.9 %collective-permute-start.5 = (bf16[128,768]{1,0:T(8,128)(2,1)S(1)}, bf16[128,768]{1,0:T(8,128)(2,1)S(1)}, u32[]{:S(2)}, u32[]{:S(2)}) collective-permute-start(bf16[128,768]{1,0:T(8,128)(2,1)S(1)} %slice_bitcast_fusion.2), channel_id=1, source_target_pairs={{0,8},{4,12},{8,0},{12,4},{1,9},{5,13},{9,1},{13,5},{2,10},{6,14},... | collective-permute-start | bytes 589832 | tf_op jit(solution)/shard_map/ppermute | solution.py:296
  6.3 10.0 %collective-permute-start.1 = (bf16[160,768]{1,0:T(8,128)(2,1)S(1)}, bf16[160,768]{1,0:T(8,128)(2,1)S(1)}, u32[]{:S(2)}, u32[]{:S(2)}) collective-permute-start(bf16[160,768]{1,0:T(8,128)(2,1)S(1)} %get-tuple-element.37), channel_id=1, source_target_pairs={{0,8},{4,12},{8,0},{12,4},{1,9},{5,13},{9,1},{13,5},{2,10},{6,14},... | collective-permute-start | bytes 737288 | tf_op jit(solution)/shard_map/ppermute | solution.py:296
  6.4 1.9 %copy-start = (bf16[2048,768]{1,0:T(8,128)(2,1)S(1)}, bf16[2048,768]{1,0:T(8,128)(2,1)}, u32[]{:S(2)}) copy-start(bf16[2048,768]{1,0:T(8,128)(2,1)} %values_ref.1) | copy-start | bytes 9437188
  8.3 1.1 %copy-start.1 = (bf16[1,512,768]{2,1,0:T(8,128)(2,1)S(1)}, bf16[1,512,768]{2,1,0:T(8,128)(2,1)}, u32[]{:S(2)}) copy-start(bf16[1,512,768]{2,1,0:T(8,128)(2,1)} %param.4) | copy-start | bytes 2359300
  9.3 3.8 %copy-start.2 = (bf16[1,128,768]{2,1,0:T(8,128)(2,1)S(1)}, bf16[1,128,768]{2,1,0:T(8,128)(2,1)}, u32[]{:S(2)}) copy-start(bf16[1,128,768]{2,1,0:T(8,128)(2,1)} %param.5) | copy-start | bytes 589828
  14.1 2.3 %collective-permute-start.6 = (bf16[128,768]{1,0:T(8,128)(2,1)S(1)}, bf16[128,768]{1,0:T(8,128)(2,1)S(1)}, u32[]{:S(2)}, u32[]{:S(2)}) collective-permute-start(bf16[128,768]{1,0:T(8,128)(2,1)S(1)} %collective-permute-done.5.refs_0_), channel_id=1, source_target_pairs={{0,4},{4,0},{8,12},{12,8},{1,5},{5,1},{9,13},{13,9},{2,6},{6,2},{1... | collective-permute-start | bytes 589832 | tf_op jit(solution)/shard_map/ppermute | solution.py:296
  14.2 8.6 %collective-permute-start.8 = (bf16[160,768]{1,0:T(8,128)(2,1)S(1)}, bf16[160,768]{1,0:T(8,128)(2,1)S(1)}, u32[]{:S(2)}, u32[]{:S(2)}) collective-permute-start(bf16[160,768]{1,0:T(8,128)(2,1)S(1)} %get-tuple-element.36), channel_id=1, source_target_pairs={{0,8},{4,12},{8,0},{12,4},{1,9},{5,13},{9,1},{13,5},{2,10},{6,14},... | collective-permute-start | bytes 737288 | tf_op jit(solution)/shard_map/ppermute | solution.py:296
  16.3 8.7 %collective-permute-start.4 = (bf16[160,768]{1,0:T(8,128)(2,1)S(1)}, bf16[160,768]{1,0:T(8,128)(2,1)S(1)}, u32[]{:S(2)}, u32[]{:S(2)}) collective-permute-start(bf16[160,768]{1,0:T(8,128)(2,1)S(1)} %collective-permute-done.1.refs_0_), channel_id=1, source_target_pairs={{0,4},{4,0},{8,12},{12,8},{1,5},{5,1},{9,13},{13,9},{2,6},{6,2},{1... | collective-permute-start | bytes 737288 | tf_op jit(solution)/shard_map/ppermute | solution.py:296
  22.8 5.8 %collective-permute-start.9 = (bf16[160,768]{1,0:T(8,128)(2,1)S(1)}, bf16[160,768]{1,0:T(8,128)(2,1)S(1)}, u32[]{:S(2)}, u32[]{:S(2)}) collective-permute-start(bf16[160,768]{1,0:T(8,128)(2,1)S(1)} %collective-permute-done.8.refs_0_), channel_id=1, source_target_pairs={{0,4},{4,0},{8,12},{12,8},{1,5},{5,1},{9,13},{13,9},{2,6},{6,2},{1... | collective-permute-start | bytes 737288 | tf_op jit(solution)/shard_map/ppermute | solution.py:296
  22.9 5.7 %collective-permute-start = (bf16[64,768]{1,0:T(8,128)(2,1)S(1)}, bf16[64,768]{1,0:T(8,128)(2,1)S(1)}, u32[]{:S(2)}, u32[]{:S(2)}) collective-permute-start(bf16[64,768]{1,0:T(8,128)(2,1)S(1)} %slice_bitcast_fusion.3), channel_id=1, source_target_pairs={{0,8},{4,12},{8,0},{12,4},{1,9},{5,13},{9,1},{13,5},{2,10},{6,14},... | collective-permute-start | bytes 294920 | tf_op jit(solution)/shard_map/ppermute | solution.py:296
  24.7 7.7 %collective-permute-start.13 = (bf16[128,768]{1,0:T(8,128)(2,1)S(1)}, bf16[128,768]{1,0:T(8,128)(2,1)S(1)}, u32[]{:S(2)}, u32[]{:S(2)}) collective-permute-start(bf16[128,768]{1,0:T(8,128)(2,1)S(1)} %bitcast.15), channel_id=1, source_target_pairs={{0,8},{4,12},{8,0},{12,4},{1,9},{5,13},{9,1},{13,5},{2,10},{6,14},... | collective-permute-start | bytes 589832 | tf_op jit(solution)/shard_map/ppermute | solution.py:296
  28.6 1.3 %collective-permute-start.7 = (bf16[64,768]{1,0:T(8,128)(2,1)S(1)}, bf16[64,768]{1,0:T(8,128)(2,1)S(1)}, u32[]{:S(2)}, u32[]{:S(2)}) collective-permute-start(bf16[64,768]{1,0:T(8,128)(2,1)S(1)} %collective-permute-done.refs_0_), channel_id=1, source_target_pairs={{0,4},{4,0},{8,12},{12,8},{1,5},{5,1},{9,13},{13,9},{2,6},{6,2},{1... | collective-permute-start | bytes 294920 | tf_op jit(solution)/shard_map/ppermute | solution.py:296
  32.3 6.9 %collective-permute-start.14 = (bf16[128,768]{1,0:T(8,128)(2,1)S(1)}, bf16[128,768]{1,0:T(8,128)(2,1)S(1)}, u32[]{:S(2)}, u32[]{:S(2)}) collective-permute-start(bf16[128,768]{1,0:T(8,128)(2,1)S(1)} %collective-permute-done.13.refs_0_), channel_id=1, source_target_pairs={{0,4},{4,0},{8,12},{12,8},{1,5},{5,1},{9,13},{13,9},{2,6},{6,2},{1... | collective-permute-start | bytes 589832 | tf_op jit(solution)/shard_map/ppermute | solution.py:296
  32.3 8.1 %collective-permute-start.10 = (f32[1,2048]{1,0:T(1,128)S(1)}, f32[1,2048]{1,0:T(1,128)S(1)}, u32[]{:S(2)}, u32[]{:S(2)}) collective-permute-start(f32[1,2048]{1,0:T(1,128)S(1)} %bank.9.total_ref), channel_id=1, source_target_pairs={{0,1},{1,2},{2,3},{3,0},{4,5},{5,6},{6,7},{7,4},{8,9},{9,10},{10,1... | collective-permute-start | bytes 24584 | tf_op jit(solution)/shard_map/ppermute | solution.py:327
  34.1 6.4 %collective-permute-start.11 = (f32[1,2048]{1,0:T(1,128)S(1)}, f32[1,2048]{1,0:T(1,128)S(1)}, u32[]{:S(2)}, u32[]{:S(2)}) collective-permute-start(f32[1,2048]{1,0:T(1,128)S(1)} %bank.9.total_ref), channel_id=1, source_target_pairs={{0,2},{1,3},{2,0},{3,1},{4,6},{5,7},{6,4},{7,5},{8,10},{9,11},{10,... | collective-permute-start | bytes 24584 | tf_op jit(solution)/shard_map/ppermute | solution.py:327
  36.7 3.8 %collective-permute-start.12 = (f32[1,2048]{1,0:T(1,128)S(1)}, f32[1,2048]{1,0:T(1,128)S(1)}, u32[]{:S(2)}, u32[]{:S(2)}) collective-permute-start(f32[1,2048]{1,0:T(1,128)S(1)} %bank.9.total_ref), channel_id=1, source_target_pairs={{0,3},{1,0},{2,1},{3,2},{4,7},{5,4},{6,5},{7,6},{8,11},{9,8},{10,9... | collective-permute-start | bytes 24584 | tf_op jit(solution)/shard_map/ppermute | solution.py:327
  40.9 2.5 %collective-permute-start.15 = (f32[4,128]{1,0:T(4,128)S(1)}, f32[4,128]{1,0:T(4,128)S(1)}, u32[]{:S(2)}, u32[]{:S(2)}) collective-permute-start(f32[4,128]{1,0:T(4,128)S(1)} %get-tuple-element.30.refs_0_), channel_id=1, source_target_pairs={{0,4},{4,0},{8,12},{12,8},{1,5},{5,1},{9,13},{13,9},{2,6},{6,2},{1... | collective-permute-start | bytes 6152 | tf_op jit(solution)/shard_map/ppermute | solution.py:296
  41.0 3.7 %collective-permute-start.16 = (f32[4,128]{1,0:T(4,128)S(1)}, f32[4,128]{1,0:T(4,128)S(1)}, u32[]{:S(2)}, u32[]{:S(2)}) collective-permute-start(f32[4,128]{1,0:T(4,128)S(1)} %get-tuple-element.30.refs_0_), channel_id=1, source_target_pairs={{0,8},{4,12},{8,0},{12,4},{1,9},{5,13},{9,1},{13,5},{2,10},{6,14},... | collective-permute-start | bytes 6152 | tf_op jit(solution)/shard_map/ppermute | solution.py:296
  42.6 3.0 %collective-permute-start.17 = (f32[4,128]{1,0:T(4,128)S(1)}, f32[4,128]{1,0:T(4,128)S(1)}, u32[]{:S(2)}, u32[]{:S(2)}) collective-permute-start(f32[4,128]{1,0:T(4,128)S(1)} %get-tuple-element.30.refs_0_), channel_id=1, source_target_pairs={{0,12},{4,8},{8,4},{12,0},{1,13},{5,9},{9,5},{13,1},{2,14},{6,10},... | collective-permute-start | bytes 6152 | tf_op jit(solution)/shard_map/ppermute | solution.py:296

commit v3 on v2

--- a/solution.py
+++ b/solution.py
@@ -29,18 +29,20 @@
 
 def inner(rows, columns):
     return lax.dot_general(
-        rows, columns, (((1,), (1,)), ((), ())), preferred_element_type=jnp.float32
+        rows, columns, (((1,), (0,)), ((), ())), preferred_element_type=jnp.float32
     )
 
 
 def unit_kernel(values_ref, unit_ref):
-    unit_ref[...] = unit_rows(values_ref[...])
+    step = math.gcd(values_ref.shape[0], 256)
+    for start in range(0, values_ref.shape[0], step):
+        unit_ref[:, start : start + step] = unit_rows(values_ref[start : start + step, :]).T
 
 
 def unit_call(values):
     return pl.pallas_call(
         unit_kernel,
-        out_shape=jax.ShapeDtypeStruct(values.shape, jnp.bfloat16),
+        out_shape=jax.ShapeDtypeStruct(values.shape[::-1], jnp.bfloat16),
         in_specs=[VMEM],
         out_specs=VMEM,
         compiler_params=params(16),
@@ -60,8 +62,8 @@
     )
     units = [unit_rows(block[...]) for block in blocks]
     unit = jnp.concatenate(units, axis=0) if count > 1 else units[0]
-    for start in range(0, gallery_ref.shape[0], tile):
-        scores = inner(unit, gallery_ref[start : start + tile, :])
+    for start in range(0, gallery_ref.shape[1], tile):
+        scores = inner(unit, gallery_ref[:, start : start + tile])
         total = jnp.sum(jnp.exp2(scores * (sharpness * LOG2E)), axis=0, keepdims=True)
         for other in earlier:
             total = total + other[:, start : start + tile]
@@ -69,7 +71,7 @@
 
 
 def bank_call(blocks, gallery_unit, earlier=()):
-    columns, depth = gallery_unit.shape
+    depth, columns = gallery_unit.shape
     rows = sum(block.shape[0] for block in blocks)
     tile = math.gcd(columns, 256)
     return pl.pallas_call(
@@ -91,14 +93,14 @@
     blocks, gallery_ref, (score_ref, power_ref) = refs[:count], refs[count], refs[-2:]
     units = [unit_rows(block[...]) for block in blocks]
     unit = jnp.concatenate(units, axis=0) if count > 1 else units[0]
-    for start in range(0, gallery_ref.shape[0], tile):
-        scores = inner(unit, gallery_ref[start : start + tile, :])
+    for start in range(0, gallery_ref.shape[1], tile):
+        scores = inner(unit, gallery_ref[:, start : start + tile])
         score_ref[:, start : start + tile] = scores * sharpness
         power_ref[:, start : start + tile] = jnp.exp2(scores * (sharpness * LOG2E))
 
 
 def test_call(blocks, gallery_unit):
-    columns, depth = gallery_unit.shape
+    depth, columns = gallery_unit.shape
     rows = sum(block.shape[0] for block in blocks)
     tile = math.gcd(columns, 256)
     shape = jax.ShapeDtypeStruct((rows, columns), jnp.float32)
@@ -310,12 +312,13 @@
         near_tests.append(shift(test, 0, 1))
     gallery_unit = unit_call(gallery)
     total = bank_call(near, gallery_unit)
+    summed = total
     tables = [test_call(near_tests, after(gallery_unit, total))]
     total = after(total, tables[0][0])
 
-    behind = [total, total]
-    for block in crossed:
-        blocks = [after(block, behind[-2])]
+    behind = [total]
+    for index, block in enumerate(crossed):
+        blocks = [after(block, behind[index // 2 * 2] if index > 1 else summed)]
         if core == 2:
             blocks.append(shift(blocks[0], 0, 1))
         behind.append(bank_call(blocks, gallery_unit, [behind[-1]]))

time: 48.2 us -> 49.1 us (1.019)
  waiting for transfers between devices: 11.1 us -> 13.5 us
  Pallas kernels: 16.2 us -> 15.4 us
  starting transfers between devices: 15.8 us -> 15.3 us
    ppermute x15, waiting for transfers between devices: 11.1 us -> 12.6 us  [shift(): return lax.ppermute(value, 'gal', moves)]
    pallas_call x3, Pallas kernels: 3.47 us -> 2.42 us  [test_call(): pl.pallas_call(functools.partial(test_kernel, len(blocks), tile), out_sha...]
    ppermute x3, waiting for transfers between devices: 0.01 us -> 0.92 us  [per_device(): lax.ppermute(total, 'qb', [(i, (i + s) % groups) for i in range(groups)])]
    pallas_call x1, Pallas kernels: 0.97 us -> 1.67 us  [unit_call(): pl.pallas_call(unit_kernel, out_shape=jax.ShapeDtypeStruct(values.shape[:...]
  transfers between devices with their start and end apart: 18 -> 18, of which waited for: 5 -> 7; matrix products, arithmetic and copies ran while one was open for 4% -> 4% of each run, Pallas kernels for 28% -> 26%
where the time goes in v3:
time: 49.1 us; the launch traced here: 48.9 us
  Pallas kernels  15.4 us (31%)
  starting transfers between devices  15.3 us (31%)
  waiting for transfers between devices  13.5 us (27%)
  local copies, waits for them, and re-layouts  3.93 us (8%)
  between operations  0.84 us (2%)
    ppermute x15, waiting for transfers between devices, shift(): return lax.ppermute(value, 'gal', moves)  12.6 us
    ppermute x15, starting transfers between devices, shift(): return lax.ppermute(value, 'gal', moves)  9.55 us
    pallas_call x5, Pallas kernels, bank_call(): pl.pallas_call(functools.partial(bank_kernel, len(blocks), tile), out_sha...  7.96 us
    ppermute x3, starting transfers between devices, per_device(): lax.ppermute(total, 'qb', [(i, (i + s) % groups) for i in range(groups)])  5.73 us
    pallas_call x3, Pallas kernels, test_call(): pl.pallas_call(functools.partial(test_kernel, len(blocks), tile), out_sha...  2.42 us
    pallas_call x1, Pallas kernels, out_call(): pl.pallas_call(functools.partial(out_kernel, origins, orders, pairs, core...  2.34 us
    slice x3, local copies, waits for them, and re-layouts, per_device(): lax.slice_in_dim(bank, s, s + n, axis=0)  2.04 us
    unnamed x6, local copies, waits for them, and re-layouts  1.89 us
  transfers between devices with their start and end apart: 18, of which 7 were waited for; matrix products, arithmetic and copies ran while one was open for 4% of the time, Pallas kernels for 26%

profile of v3, /device:TPU:0, one launch (start us, length us, event | category | flops | bytes accessed | tf_op | source)
XLA Modules:
  0.0 48.9 jit_solution(3888782051902683498)
XLA Ops:
  0.6 0.6 %collective-permute-start.2 = (bf16[512,768]{1,0:T(8,128)(2,1)}, bf16[512,768]{1,0:T(8,128)(2,1)S(1)}, u32[]{:S(2)}, u32[]{:S(2)}) collective-permute-start(bf16[512,768]{1,0:T(8,128)(2,1)} %bitcast.11), channel_id=1, source_target_pairs={{0,4},{4,0},{8,12},{12,8},{1,5},{5,1},{9,13},{13,9},{2,6},{6,2},{1... | collective-permute-start | bytes 2359304 | tf_op jit(solution)/shard_map/ppermute | solution.py:298
  1.2 0.1 collective-permute-start.6
  1.3 0.9 %slice_bitcast_fusion.2 = bf16[128,768]{1,0:T(8,128)(2,1)S(1)} fusion(bf16[1,512,768]{2,1,0:T(8,128)(2,1)} %param.4), kind=kLoop, calls=%fused_computation.2 | loop fusion | bytes 393216 | tf_op jit(solution)/shard_map/slice | solution.py:302
  2.2 3.0 %collective-permute-start.4 = (bf16[128,768]{1,0:T(8,128)(2,1)S(1)}, bf16[128,768]{1,0:T(8,128)(2,1)S(1)}, u32[]{:S(2)}, u32[]{:S(2)}) collective-permute-start(bf16[128,768]{1,0:T(8,128)(2,1)S(1)} %slice_bitcast_fusion.2), channel_id=1, source_target_pairs={{0,8},{4,12},{8,0},{12,4},{1,9},{5,13},{9,1},{13,5},{2,10},{6,14},... | collective-permute-start | bytes 589832 | tf_op jit(solution)/shard_map/ppermute | solution.py:298
  5.2 1.1 %slice_bitcast_fusion = (bf16[160,768]{1,0:T(8,128)(2,1)S(1)}, bf16[160,768]{1,0:T(8,128)(2,1)S(1)}) fusion(bf16[1,512,768]{2,1,0:T(8,128)(2,1)} %param.4), kind=kLoop, calls=%fused_computation | loop fusion | bytes 983040 | tf_op jit(solution)/shard_map/slice | solution.py:302
  6.3 0.1 collective-permute-start.1
  6.4 1.9 %copy-done = bf16[2048,768]{1,0:T(8,128)(2,1)S(1)} copy-done((bf16[2048,768]{1,0:T(8,128)(2,1)S(1)}, bf16[2048,768]{1,0:T(8,128)(2,1)}, u32[]{:S(2)}) %copy-start) | copy-done | bytes 3145752
  8.3 1.7 %unit.1.refs_2_.refs_1_ = bf16[768,2048]{1,0:T(8,128)(2,1)S(1)} custom-call(bf16[2048,768]{1,0:T(8,128)(2,1)S(1)} %copy-done), custom_call_target="tpu_custom_call" | custom-call | flops 6291456 | bytes 6291456 | tf_op jit(solution)/shard_map/unit/pallas_call | solution.py:43
  10.0 0.0 copy-start.2
  10.0 0.0 collective-permute-done.2.refs_1_
  10.0 3.6 %bank.5.refs_3_ = f32[1,2048]{1,0:T(1,128)S(1)} custom-call(bf16[512,768]{1,0:T(8,128)(2,1)S(1)} %bitcast.12, bf16[512,768]{1,0:T(8,128)(2,1)S(1)} %collective-permute-done.2.refs_1_, bf16[768,2048]{1,0:T(8,128)(2,1)S(1)} %unit.1.refs_2_.refs_1_), custom_call_target="tpu_custom_call" | custom-call | flops 3221225472 | bytes 4718592 | tf_op jit(solution)/shard_map/bank/pallas_call | solution.py:77
  13.6 0.0 collective-permute-done.4.refs_0_
  13.6 0.1 collective-permute-start.5
  13.7 1.9 %collective-permute-done.1.refs_0_ = bf16[160,768]{1,0:T(8,128)(2,1)S(1)} collective-permute-done((bf16[160,768]{1,0:T(8,128)(2,1)S(1)}, bf16[160,768]{1,0:T(8,128)(2,1)S(1)}, u32[]{:S(2)}, u32[]{:S(2)}) %collective-permute-start.1) | collective-permute-done | bytes 245792 | tf_op jit(solution)/shard_map/ppermute | solution.py:298
  15.6 0.0 collective-permute-start.3
  15.6 1.7 %collective-permute-start.8 = (bf16[160,768]{1,0:T(8,128)(2,1)S(1)}, bf16[160,768]{1,0:T(8,128)(2,1)S(1)}, u32[]{:S(2)}, u32[]{:S(2)}) collective-permute-start(bf16[160,768]{1,0:T(8,128)(2,1)S(1)} %get-tuple-element.36), channel_id=1, source_target_pairs={{0,8},{4,12},{8,0},{12,4},{1,9},{5,13},{9,1},{13,5},{2,10},{6,14},... | collective-permute-start | bytes 737288 | tf_op jit(solution)/shard_map/ppermute | solution.py:298
  17.4 0.0 collective-permute-done.6.refs_1_
  17.4 1.1 %test.3 = (f32[256,2048]{1,0:T(8,128)S(1)}, f32[256,2048]{1,0:T(8,128)S(1)}) custom-call(bf16[128,768]{1,0:T(8,128)(2,1)S(1)} %bitcast.14, bf16[128,768]{1,0:T(8,128)(2,1)S(1)} %collective-permute-done.6.refs_1_, bf16[768,2048]{1,0:T(8,128)(2,1)S(1)} %unit.1.refs_2_.refs_1_), custom_call_target="tpu_custom_call" | custom-call | flops 805306368 | bytes 7733248 | tf_op jit(solution)/shard_map/test/pallas_call | solution.py:107
  18.5 0.0 collective-permute-done.5.refs_1_
  18.5 1.1 %bank.6.refs_3_ = f32[1,2048]{1,0:T(1,128)S(1)} custom-call(bf16[128,768]{1,0:T(8,128)(2,1)S(1)} %collective-permute-done.4.refs_0_, bf16[128,768]{1,0:T(8,128)(2,1)S(1)} %collective-permute-done.5.refs_1_, bf16[768,2048]{1,0:T(8,128)(2,1)S(1)} %unit.1.refs_2_.refs_1_, f32[1,2048]{1,0:T(1,128)S(1)} %bank.5.refs_3_), custom_call_target="tpu_custom_call" | custom-call | flops 805306368 | bytes 3538944 | tf_op jit(solution)/shard_map/bank/pallas_call | solution.py:77
  19.6 0.0 collective-permute-done.3.refs_1_
  19.6 1.3 %bank.7.refs_3_ = f32[1,2048]{1,0:T(1,128)S(1)} custom-call(bf16[160,768]{1,0:T(8,128)(2,1)S(1)} %collective-permute-done.1.refs_0_, bf16[160,768]{1,0:T(8,128)(2,1)S(1)} %collective-permute-done.3.refs_1_, bf16[768,2048]{1,0:T(8,128)(2,1)S(1)} %unit.1.refs_2_.refs_1_, f32[1,2048]{1,0:T(1,128)S(1)} %bank.6.refs_3_), custom_call_target="tpu_custom_call" | custom-call | flops 1006632960 | bytes 3637248 | tf_op jit(solution)/shard_map/bank/pallas_call | solution.py:77
  20.9 3.1 %collective-permute-done.8.refs_0_ = bf16[160,768]{1,0:T(8,128)(2,1)S(1)} collective-permute-done((bf16[160,768]{1,0:T(8,128)(2,1)S(1)}, bf16[160,768]{1,0:T(8,128)(2,1)S(1)}, u32[]{:S(2)}, u32[]{:S(2)}) %collective-permute-start.8) | collective-permute-done | bytes 245792 | tf_op jit(solution)/shard_map/ppermute | solution.py:298
  24.0 0.0 collective-permute-start.9
  24.0 1.8 %collective-permute-start = (bf16[64,768]{1,0:T(8,128)(2,1)S(1)}, bf16[64,768]{1,0:T(8,128)(2,1)S(1)}, u32[]{:S(2)}, u32[]{:S(2)}) collective-permute-start(bf16[64,768]{1,0:T(8,128)(2,1)S(1)} %slice_bitcast_fusion.3), channel_id=1, source_target_pairs={{0,8},{4,12},{8,0},{12,4},{1,9},{5,13},{9,1},{13,5},{2,10},{6,14},... | collective-permute-start | bytes 294920 | tf_op jit(solution)/shard_map/ppermute | solution.py:298
  25.8 0.3 collective-permute-start.13
  26.1 3.6 %collective-permute-done.refs_0_ = bf16[64,768]{1,0:T(8,128)(2,1)S(1)} collective-permute-done((bf16[64,768]{1,0:T(8,128)(2,1)S(1)}, bf16[64,768]{1,0:T(8,128)(2,1)S(1)}, u32[]{:S(2)}, u32[]{:S(2)}) %collective-permute-start) | collective-permute-done | bytes 98336 | tf_op jit(solution)/shard_map/ppermute | solution.py:298
  29.7 0.0 collective-permute-start.7
  29.7 0.0 collective-permute-done.9.refs_1_
  29.7 1.3 %bank.8.refs_3_ = f32[1,2048]{1,0:T(1,128)S(1)} custom-call(bf16[160,768]{1,0:T(8,128)(2,1)S(1)} %collective-permute-done.8.refs_0_, bf16[160,768]{1,0:T(8,128)(2,1)S(1)} %collective-permute-done.9.refs_1_, bf16[768,2048]{1,0:T(8,128)(2,1)S(1)} %unit.1.refs_2_.refs_1_, f32[1,2048]{1,0:T(1,128)S(1)} %bank.7.refs_3_), custom_call_target="tpu_custom_call" | custom-call | flops 1006632960 | bytes 3637248 | tf_op jit(solution)/shard_map/bank/pallas_call | solution.py:77
  31.0 0.0 collective-permute-done.7.refs_1_
  31.1 0.7 %bank.9.total_ref = f32[1,2048]{1,0:T(1,128)S(1)} custom-call(bf16[64,768]{1,0:T(8,128)(2,1)S(1)} %collective-permute-done.refs_0_, bf16[64,768]{1,0:T(8,128)(2,1)S(1)} %collective-permute-done.7.refs_1_, bf16[768,2048]{1,0:T(8,128)(2,1)S(1)} %unit.1.refs_2_.refs_1_, f32[1,2048]{1,0:T(1,128)S(1)} %bank.8.refs_3_), custom_call_target="tpu_custom_call" | custom-call | flops 402653184 | bytes 3342336 | tf_op jit(solution)/shard_map/bank/pallas_call | solution.py:77
  31.8 1.7 %collective-permute-done.13.refs_0_ = bf16[128,768]{1,0:T(8,128)(2,1)S(1)} collective-permute-done((bf16[128,768]{1,0:T(8,128)(2,1)S(1)}, bf16[128,768]{1,0:T(8,128)(2,1)S(1)}, u32[]{:S(2)}, u32[]{:S(2)}) %collective-permute-start.13) | collective-permute-done | bytes 196640 | tf_op jit(solution)/shard_map/ppermute | solution.py:298
  33.5 1.8 %collective-permute-start.10 = (f32[1,2048]{1,0:T(1,128)S(1)}, f32[1,2048]{1,0:T(1,128)S(1)}, u32[]{:S(2)}, u32[]{:S(2)}) collective-permute-start(f32[1,2048]{1,0:T(1,128)S(1)} %bank.9.total_ref), channel_id=1, source_target_pairs={{0,1},{1,2},{2,3},{3,0},{4,5},{5,6},{6,7},{7,4},{8,9},{9,10},{10,1... | collective-permute-start | bytes 24584 | tf_op jit(solution)/shard_map/ppermute | solution.py:330
  35.3 2.6 %collective-permute-start.11 = (f32[1,2048]{1,0:T(1,128)S(1)}, f32[1,2048]{1,0:T(1,128)S(1)}, u32[]{:S(2)}, u32[]{:S(2)}) collective-permute-start(f32[1,2048]{1,0:T(1,128)S(1)} %bank.9.total_ref), channel_id=1, source_target_pairs={{0,2},{1,3},{2,0},{3,1},{4,6},{5,7},{6,4},{7,5},{8,10},{9,11},{10,... | collective-permute-start | bytes 24584 | tf_op jit(solution)/shard_map/ppermute | solution.py:330
  37.9 1.3 %collective-permute-start.12 = (f32[1,2048]{1,0:T(1,128)S(1)}, f32[1,2048]{1,0:T(1,128)S(1)}, u32[]{:S(2)}, u32[]{:S(2)}) collective-permute-start(f32[1,2048]{1,0:T(1,128)S(1)} %bank.9.total_ref), channel_id=1, source_target_pairs={{0,3},{1,0},{2,1},{3,2},{4,7},{5,4},{6,5},{7,6},{8,11},{9,8},{10,9... | collective-permute-start | bytes 24584 | tf_op jit(solution)/shard_map/ppermute | solution.py:330
  39.2 0.7 %test.4 = (f32[128,2048]{1,0:T(8,128)S(1)}, f32[128,2048]{1,0:T(8,128)S(1)}) custom-call(bf16[128,768]{1,0:T(8,128)(2,1)S(1)} %collective-permute-done.13.refs_0_, bf16[768,2048]{1,0:T(8,128)(2,1)S(1)} %unit.1.refs_2_.refs_1_), custom_call_target="tpu_custom_call" | custom-call | flops 402653184 | bytes 5439488 | tf_op jit(solution)/shard_map/test/pallas_call | solution.py:107
  39.9 0.0 collective-permute-done.14.refs_0_
  39.9 0.7 %test.5 = (f32[128,2048]{1,0:T(8,128)S(1)}, f32[128,2048]{1,0:T(8,128)S(1)}) custom-call(bf16[128,768]{1,0:T(8,128)(2,1)S(1)} %collective-permute-done.14.refs_0_, bf16[768,2048]{1,0:T(8,128)(2,1)S(1)} %unit.1.refs_2_.refs_1_), custom_call_target="tpu_custom_call" | custom-call | flops 402653184 | bytes 5439488 | tf_op jit(solution)/shard_map/test/pallas_call | solution.py:107
  40.6 0.9 %collective-permute-done.12.refs_3_ = f32[1,2048]{1,0:T(1,128)S(1)} collective-permute-done((f32[1,2048]{1,0:T(1,128)S(1)}, f32[1,2048]{1,0:T(1,128)S(1)}, u32[]{:S(2)}, u32[]{:S(2)}) %collective-permute-start.12) | collective-permute-done | bytes 8224 | tf_op jit(solution)/shard_map/ppermute | solution.py:330
  41.5 0.4 rows.1
  41.9 0.1 collective-permute-start.15
  42.0 1.6 %collective-permute-start.16 = (f32[4,128]{1,0:T(4,128)S(1)}, f32[4,128]{1,0:T(4,128)S(1)}, u32[]{:S(2)}, u32[]{:S(2)}) collective-permute-start(f32[4,128]{1,0:T(4,128)S(1)} %get-tuple-element.30.refs_0_), channel_id=1, source_target_pairs={{0,8},{4,12},{8,0},{12,4},{1,9},{5,13},{9,1},{13,5},{2,10},{6,14},... | collective-permute-start | bytes 6152 | tf_op jit(solution)/shard_map/ppermute | solution.py:298
  43.6 0.3 collective-permute-start.17
  43.8 0.6 %logs.1 = (f32[1,2048]{1,0:T(1,128)S(1)}, f32[1,2048]{1,0:T(1,128)}) custom-call(f32[1,2048]{1,0:T(1,128)S(1)} %get-tuple-element.33.total_ref), custom_call_target="tpu_custom_call" | custom-call | flops 2048 | bytes 24576 | tf_op jit(solution)/shard_map/logs/pallas_call | solution.py:191
  44.5 1.2 %collective-permute-done.16.refs_2_ = f32[4,128]{1,0:T(4,128)S(1)} collective-permute-done((f32[4,128]{1,0:T(4,128)S(1)}, f32[4,128]{1,0:T(4,128)S(1)}, u32[]{:S(2)}, u32[]{:S(2)}) %collective-permute-start.16) | collective-permute-done | bytes 2080 | tf_op jit(solution)/shard_map/ppermute | solution.py:298
  45.7 0.9 %collective-permute-done.17.refs_3_ = f32[4,128]{1,0:T(4,128)S(1)} collective-permute-done((f32[4,128]{1,0:T(4,128)S(1)}, f32[4,128]{1,0:T(4,128)S(1)}, u32[]{:S(2)}, u32[]{:S(2)}) %collective-permute-start.17) | collective-permute-done | bytes 2080 | tf_op jit(solution)/shard_map/ppermute | solution.py:298
  46.6 2.3 %out.1 = f32[512,2048]{1,0:T(8,128)} custom-call(f32[4,128]{1,0:T(4,128)S(1)} %get-tuple-element.30.refs_0_, f32[4,128]{1,0:T(4,128)S(1)} %collective-permute-done.15.refs_1_, f32[4,128]{1,0:T(4,128)S(1)} %collective-permute-done.16.refs_2_, f32[4,128]{1,0:T(4,128)S(1)} %collective-permute-done.17.refs_3_, f32[256,2048]{1,0:T(8,128)S(1)} %get-tuple-element.22.refs_4_, ...), custom_call_target="tpu_custom_call" | custom-call | flops 3145728 | bytes 8388608 | tf_op jit(solution)/shard_map/out/pallas_call | solution.py:256
  (10 shorter events, 0.0 us)
Async XLA Ops:
  0.6 9.3 %collective-permute-start.2 = (bf16[512,768]{1,0:T(8,128)(2,1)}, bf16[512,768]{1,0:T(8,128)(2,1)S(1)}, u32[]{:S(2)}, u32[]{:S(2)}) collective-permute-start(bf16[512,768]{1,0:T(8,128)(2,1)} %bitcast.11), channel_id=1, source_target_pairs={{0,4},{4,0},{8,12},{12,8},{1,5},{5,1},{9,13},{13,9},{2,6},{6,2},{1... | collective-permute-start | bytes 2359304 | tf_op jit(solution)/shard_map/ppermute | solution.py:298
  1.2 16.2 %collective-permute-start.6 = (bf16[128,768]{1,0:T(8,128)(2,1)}, bf16[128,768]{1,0:T(8,128)(2,1)S(1)}, u32[]{:S(2)}, u32[]{:S(2)}) collective-permute-start(bf16[128,768]{1,0:T(8,128)(2,1)} %bitcast.13), channel_id=1, source_target_pairs={{0,4},{4,0},{8,12},{12,8},{1,5},{5,1},{9,13},{13,9},{2,6},{6,2},{1... | collective-permute-start | bytes 589832 | tf_op jit(solution)/shard_map/ppermute | solution.py:298
  2.2 11.4 %collective-permute-start.4 = (bf16[128,768]{1,0:T(8,128)(2,1)S(1)}, bf16[128,768]{1,0:T(8,128)(2,1)S(1)}, u32[]{:S(2)}, u32[]{:S(2)}) collective-permute-start(bf16[128,768]{1,0:T(8,128)(2,1)S(1)} %slice_bitcast_fusion.2), channel_id=1, source_target_pairs={{0,8},{4,12},{8,0},{12,4},{1,9},{5,13},{9,1},{13,5},{2,10},{6,14},... | collective-permute-start | bytes 589832 | tf_op jit(solution)/shard_map/ppermute | solution.py:298
  6.3 9.3 %collective-permute-start.1 = (bf16[160,768]{1,0:T(8,128)(2,1)S(1)}, bf16[160,768]{1,0:T(8,128)(2,1)S(1)}, u32[]{:S(2)}, u32[]{:S(2)}) collective-permute-start(bf16[160,768]{1,0:T(8,128)(2,1)S(1)} %get-tuple-element.37), channel_id=1, source_target_pairs={{0,8},{4,12},{8,0},{12,4},{1,9},{5,13},{9,1},{13,5},{2,10},{6,14},... | collective-permute-start | bytes 737288 | tf_op jit(solution)/shard_map/ppermute | solution.py:298
  6.4 1.9 %copy-start = (bf16[2048,768]{1,0:T(8,128)(2,1)S(1)}, bf16[2048,768]{1,0:T(8,128)(2,1)}, u32[]{:S(2)}) copy-start(bf16[2048,768]{1,0:T(8,128)(2,1)} %values_ref.1) | copy-start | bytes 9437188
  8.3 1.7 %copy-start.1 = (bf16[1,512,768]{2,1,0:T(8,128)(2,1)S(1)}, bf16[1,512,768]{2,1,0:T(8,128)(2,1)}, u32[]{:S(2)}) copy-start(bf16[1,512,768]{2,1,0:T(8,128)(2,1)} %param.4) | copy-start | bytes 2359300
  10.0 7.4 %copy-start.2 = (bf16[1,128,768]{2,1,0:T(8,128)(2,1)S(1)}, bf16[1,128,768]{2,1,0:T(8,128)(2,1)}, u32[]{:S(2)}) copy-start(bf16[1,128,768]{2,1,0:T(8,128)(2,1)} %param.5) | copy-start | bytes 589828
  13.6 4.8 %collective-permute-start.5 = (bf16[128,768]{1,0:T(8,128)(2,1)S(1)}, bf16[128,768]{1,0:T(8,128)(2,1)S(1)}, u32[]{:S(2)}, u32[]{:S(2)}) collective-permute-start(bf16[128,768]{1,0:T(8,128)(2,1)S(1)} %collective-permute-done.4.refs_0_), channel_id=1, source_target_pairs={{0,4},{4,0},{8,12},{12,8},{1,5},{5,1},{9,13},{13,9},{2,6},{6,2},{1... | collective-permute-start | bytes 589832 | tf_op jit(solution)/shard_map/ppermute | solution.py:298
  15.6 4.0 %collective-permute-start.3 = (bf16[160,768]{1,0:T(8,128)(2,1)S(1)}, bf16[160,768]{1,0:T(8,128)(2,1)S(1)}, u32[]{:S(2)}, u32[]{:S(2)}) collective-permute-start(bf16[160,768]{1,0:T(8,128)(2,1)S(1)} %collective-permute-done.1.refs_0_), channel_id=1, source_target_pairs={{0,4},{4,0},{8,12},{12,8},{1,5},{5,1},{9,13},{13,9},{2,6},{6,2},{1... | collective-permute-start | bytes 737288 | tf_op jit(solution)/shard_map/ppermute | solution.py:298
  15.6 8.4 %collective-permute-start.8 = (bf16[160,768]{1,0:T(8,128)(2,1)S(1)}, bf16[160,768]{1,0:T(8,128)(2,1)S(1)}, u32[]{:S(2)}, u32[]{:S(2)}) collective-permute-start(bf16[160,768]{1,0:T(8,128)(2,1)S(1)} %get-tuple-element.36), channel_id=1, source_target_pairs={{0,8},{4,12},{8,0},{12,4},{1,9},{5,13},{9,1},{13,5},{2,10},{6,14},... | collective-permute-start | bytes 737288 | tf_op jit(solution)/shard_map/ppermute | solution.py:298
  24.0 5.8 %collective-permute-start.9 = (bf16[160,768]{1,0:T(8,128)(2,1)S(1)}, bf16[160,768]{1,0:T(8,128)(2,1)S(1)}, u32[]{:S(2)}, u32[]{:S(2)}) collective-permute-start(bf16[160,768]{1,0:T(8,128)(2,1)S(1)} %collective-permute-done.8.refs_0_), channel_id=1, source_target_pairs={{0,4},{4,0},{8,12},{12,8},{1,5},{5,1},{9,13},{13,9},{2,6},{6,2},{1... | collective-permute-start | bytes 737288 | tf_op jit(solution)/shard_map/ppermute | solution.py:298
  24.0 5.7 %collective-permute-start = (bf16[64,768]{1,0:T(8,128)(2,1)S(1)}, bf16[64,768]{1,0:T(8,128)(2,1)S(1)}, u32[]{:S(2)}, u32[]{:S(2)}) collective-permute-start(bf16[64,768]{1,0:T(8,128)(2,1)S(1)} %slice_bitcast_fusion.3), channel_id=1, source_target_pairs={{0,8},{4,12},{8,0},{12,4},{1,9},{5,13},{9,1},{13,5},{2,10},{6,14},... | collective-permute-start | bytes 294920 | tf_op jit(solution)/shard_map/ppermute | solution.py:298
  25.8 7.7 %collective-permute-start.13 = (bf16[128,768]{1,0:T(8,128)(2,1)S(1)}, bf16[128,768]{1,0:T(8,128)(2,1)S(1)}, u32[]{:S(2)}, u32[]{:S(2)}) collective-permute-start(bf16[128,768]{1,0:T(8,128)(2,1)S(1)} %bitcast.15), channel_id=1, source_target_pairs={{0,8},{4,12},{8,0},{12,4},{1,9},{5,13},{9,1},{13,5},{2,10},{6,14},... | collective-permute-start | bytes 589832 | tf_op jit(solution)/shard_map/ppermute | solution.py:298
  29.7 1.3 %collective-permute-start.7 = (bf16[64,768]{1,0:T(8,128)(2,1)S(1)}, bf16[64,768]{1,0:T(8,128)(2,1)S(1)}, u32[]{:S(2)}, u32[]{:S(2)}) collective-permute-start(bf16[64,768]{1,0:T(8,128)(2,1)S(1)} %collective-permute-done.refs_0_), channel_id=1, source_target_pairs={{0,4},{4,0},{8,12},{12,8},{1,5},{5,1},{9,13},{13,9},{2,6},{6,2},{1... | collective-permute-start | bytes 294920 | tf_op jit(solution)/shard_map/ppermute | solution.py:298
  33.5 6.4 %collective-permute-start.14 = (bf16[128,768]{1,0:T(8,128)(2,1)S(1)}, bf16[128,768]{1,0:T(8,128)(2,1)S(1)}, u32[]{:S(2)}, u32[]{:S(2)}) collective-permute-start(bf16[128,768]{1,0:T(8,128)(2,1)S(1)} %collective-permute-done.13.refs_0_), channel_id=1, source_target_pairs={{0,4},{4,0},{8,12},{12,8},{1,5},{5,1},{9,13},{13,9},{2,6},{6,2},{1... | collective-permute-start | bytes 589832 | tf_op jit(solution)/shard_map/ppermute | solution.py:298
  33.5 7.1 %collective-permute-start.10 = (f32[1,2048]{1,0:T(1,128)S(1)}, f32[1,2048]{1,0:T(1,128)S(1)}, u32[]{:S(2)}, u32[]{:S(2)}) collective-permute-start(f32[1,2048]{1,0:T(1,128)S(1)} %bank.9.total_ref), channel_id=1, source_target_pairs={{0,1},{1,2},{2,3},{3,0},{4,5},{5,6},{6,7},{7,4},{8,9},{9,10},{10,1... | collective-permute-start | bytes 24584 | tf_op jit(solution)/shard_map/ppermute | solution.py:330
  35.3 5.3 %collective-permute-start.11 = (f32[1,2048]{1,0:T(1,128)S(1)}, f32[1,2048]{1,0:T(1,128)S(1)}, u32[]{:S(2)}, u32[]{:S(2)}) collective-permute-start(f32[1,2048]{1,0:T(1,128)S(1)} %bank.9.total_ref), channel_id=1, source_target_pairs={{0,2},{1,3},{2,0},{3,1},{4,6},{5,7},{6,4},{7,5},{8,10},{9,11},{10,... | collective-permute-start | bytes 24584 | tf_op jit(solution)/shard_map/ppermute | solution.py:330
  37.9 3.7 %collective-permute-start.12 = (f32[1,2048]{1,0:T(1,128)S(1)}, f32[1,2048]{1,0:T(1,128)S(1)}, u32[]{:S(2)}, u32[]{:S(2)}) collective-permute-start(f32[1,2048]{1,0:T(1,128)S(1)} %bank.9.total_ref), channel_id=1, source_target_pairs={{0,3},{1,0},{2,1},{3,2},{4,7},{5,4},{6,5},{7,6},{8,11},{9,8},{10,9... | collective-permute-start | bytes 24584 | tf_op jit(solution)/shard_map/ppermute | solution.py:330
  41.9 2.5 %collective-permute-start.15 = (f32[4,128]{1,0:T(4,128)S(1)}, f32[4,128]{1,0:T(4,128)S(1)}, u32[]{:S(2)}, u32[]{:S(2)}) collective-permute-start(f32[4,128]{1,0:T(4,128)S(1)} %get-tuple-element.30.refs_0_), channel_id=1, source_target_pairs={{0,4},{4,0},{8,12},{12,8},{1,5},{5,1},{9,13},{13,9},{2,6},{6,2},{1... | collective-permute-start | bytes 6152 | tf_op jit(solution)/shard_map/ppermute | solution.py:298
  42.0 3.7 %collective-permute-start.16 = (f32[4,128]{1,0:T(4,128)S(1)}, f32[4,128]{1,0:T(4,128)S(1)}, u32[]{:S(2)}, u32[]{:S(2)}) collective-permute-start(f32[4,128]{1,0:T(4,128)S(1)} %get-tuple-element.30.refs_0_), channel_id=1, source_target_pairs={{0,8},{4,12},{8,0},{12,4},{1,9},{5,13},{9,1},{13,5},{2,10},{6,14},... | collective-permute-start | bytes 6152 | tf_op jit(solution)/shard_map/ppermute | solution.py:298
  43.6 3.0 %collective-permute-start.17 = (f32[4,128]{1,0:T(4,128)S(1)}, f32[4,128]{1,0:T(4,128)S(1)}, u32[]{:S(2)}, u32[]{:S(2)}) collective-permute-start(f32[4,128]{1,0:T(4,128)S(1)} %get-tuple-element.30.refs_0_), channel_id=1, source_target_pairs={{0,12},{4,8},{8,4},{12,0},{1,13},{5,9},{9,5},{13,1},{2,14},{6,10},... | collective-permute-start | bytes 6152 | tf_op jit(solution)/shard_map/ppermute | solution.py:298

commit v4 on v3

--- a/solution.py
+++ b/solution.py
@@ -33,24 +33,69 @@
     )
 
 
-def unit_kernel(values_ref, unit_ref):
-    step = math.gcd(values_ref.shape[0], 256)
-    for start in range(0, values_ref.shape[0], step):
-        unit_ref[:, start : start + step] = unit_rows(values_ref[start : start + step, :]).T
+def cut_kernel(starts, source_ref, *refs):
+    outs, sems = refs[:-1], refs[-1]
+    copies = [
+        pltpu.make_async_copy(source_ref.at[pl.ds(start, out.shape[0])], out, sems.at[index])
+        for index, (start, out) in enumerate(zip(starts, outs))
+    ]
+    for copy in copies:
+        copy.start()
+    for copy in copies:
+        copy.wait()
+
+
+def cut_call(source, starts, sizes):
+    shapes = [jax.ShapeDtypeStruct((size, source.shape[1]), source.dtype) for size in sizes]
+    return pl.pallas_call(
+        functools.partial(cut_kernel, starts),
+        out_shape=shapes,
+        in_specs=[pl.BlockSpec(memory_space=pltpu.HBM)],
+        out_specs=[VMEM] * len(sizes),
+        scratch_shapes=[pltpu.SemaphoreType.DMA((len(sizes),))],
+        compiler_params=params(4),
+        name="cut",
+        cost_estimate=pl.CostEstimate(
+            flops=0, bytes_accessed=4 * sum(sizes) * source.shape[1], transcendentals=0
+        ),
+    )(source)
+
+
+def unit_kernel(step, values_ref, unit_ref, stage, sems):
+    rows = values_ref.shape[0]
+    copies = [
+        pltpu.make_async_copy(
+            values_ref.at[pl.ds(start, step)], stage.at[pl.ds(start, step)], sems.at[start // step]
+        )
+        for start in range(0, rows, step)
+    ]
+    ahead = 3
+    for copy in copies[:ahead]:
+        copy.start()
+    for index, start in enumerate(range(0, rows, step)):
+        copies[index].wait()
+        if index + ahead < len(copies):
+            copies[index + ahead].start()
+        unit_ref[:, start : start + step] = unit_rows(stage[start : start + step, :]).T
 
 
 def unit_call(values):
-    return pl.pallas_call(
-        unit_kernel,
+    step = math.gcd(values.shape[0], 256)
+    return pl.pallas_call(
+        functools.partial(unit_kernel, step),
         out_shape=jax.ShapeDtypeStruct(values.shape[::-1], jnp.bfloat16),
-        in_specs=[VMEM],
+        in_specs=[pl.BlockSpec(memory_space=pltpu.HBM)],
         out_specs=VMEM,
+        scratch_shapes=[
+            pltpu.VMEM(values.shape, values.dtype),
+            pltpu.SemaphoreType.DMA((values.shape[0] // step,)),
+        ],
         compiler_params=params(16),
         name="unit",
         cost_estimate=pl.CostEstimate(
             flops=4 * values.size, bytes_accessed=4 * values.size, transcendentals=values.shape[0]
         ),
-    )(values)
+    )(pltpu.with_memory_space_constraint(values, pltpu.HBM))
 
 
 def bank_kernel(count, tile, *refs):
@@ -277,10 +322,7 @@
 def chunk_sizes(rows):
     if rows % 128:
         return [rows]
-    first, last = rows // 4, rows // 8
-    middle = rows - first - last
-    half = (middle // 2 + 15) // 16 * 16
-    return [first, half, middle - half, last]
+    return [rows * part // 32 for part in (8, 12, 8, 4)]
 
 
 def per_device(gallery, querybank, test_queries):
@@ -299,14 +341,16 @@
 
     sizes = chunk_sizes(bank.shape[0])
     starts = [sum(sizes[:i]) for i in range(len(sizes))]
-    chunks = [lax.slice_in_dim(bank, s, s + n, axis=0) for s, n in zip(starts, sizes)]
+    chunks = cut_call(bank, starts[:1], sizes[:1])
+    if len(sizes) > 1:
+        chunks += cut_call(bank, starts[1:], sizes[1:])
 
     crossed = []
     for chunk in chunks:
         crossed += [shift(chunk, pair, 0) for pair in range(1, pairs)]
     test_crossed = [shift(test, pair, 0) for pair in range(1, pairs)]
 
-    near, near_tests = [bank], [test]
+    near, near_tests = [*chunks], [test]
     if core == 2:
         near.append(shift(bank, 0, 1))
         near_tests.append(shift(test, 0, 1))
@@ -318,7 +362,7 @@
 
     behind = [total]
     for index, block in enumerate(crossed):
-        blocks = [after(block, behind[index // 2 * 2] if index > 1 else summed)]
+        blocks = [after(block, behind[index // 2 * 2] if index else summed)]
         if core == 2:
             blocks.append(shift(blocks[0], 0, 1))
         behind.append(bank_call(blocks, gallery_unit, [behind[-1]]))

time: 49.1 us -> 49.5 us (level)
  Pallas kernels: 15.4 us -> 18.2 us
  local copies, waits for them, and re-layouts: 3.93 us -> 1.14 us
    pallas_call x1 -> x3, Pallas kernels: 1.67 us -> 4.41 us  [the longest x1 3.72 us: unit_call(): pl.pallas_call(functools.partial(unit_kernel, step), out_shape=jax.ShapeD...]
    slice x3 -> x0, local copies, waits for them, and re-layouts: 2.04 us -> none  [per_device(): lax.slice_in_dim(bank, s, s + n, axis=0)]
    unnamed x6 -> x4, local copies, waits for them, and re-layouts: 1.89 us -> 1.14 us
  transfers between devices with their start and end apart: 18 -> 18, of which waited for: 7 -> 8; matrix products, arithmetic and copies ran while one was open for 4% -> 0% of each run, Pallas kernels for 26% -> 31%
where the time goes in v4:
time: 49.5 us; the launch traced here: 49.3 us
  Pallas kernels  18.2 us (37%)
  starting transfers between devices  15.7 us (32%)
  waiting for transfers between devices  13.5 us (27%)
  local copies, waits for them, and re-layouts  1.14 us (2%)
  between operations  0.82 us (2%)
    ppermute x15, waiting for transfers between devices, shift(): return lax.ppermute(value, 'gal', moves)  12.6 us
    ppermute x15, starting transfers between devices, shift(): return lax.ppermute(value, 'gal', moves)  9.92 us
    pallas_call x5, Pallas kernels, bank_call(): pl.pallas_call(functools.partial(bank_kernel, len(blocks), tile), out_sha...  7.98 us
    ppermute x3, starting transfers between devices, per_device(): lax.ppermute(total, 'qb', [(i, (i + s) % groups) for i in range(groups)])  5.73 us
    pallas_call x1, Pallas kernels, unit_call(): pl.pallas_call(functools.partial(unit_kernel, step), out_shape=jax.ShapeD...  3.72 us
    pallas_call x3, Pallas kernels, test_call(): pl.pallas_call(functools.partial(test_kernel, len(blocks), tile), out_sha...  2.43 us
    pallas_call x1, Pallas kernels, out_call(): pl.pallas_call(functools.partial(out_kernel, origins, orders, pairs, core...  2.34 us
    unnamed x4, local copies, waits for them, and re-layouts  1.14 us
  transfers between devices with their start and end apart: 18, of which 8 were waited for; matrix products, arithmetic and copies ran while one was open for 0% of the time, Pallas kernels for 31%

profile of v4, /device:TPU:0, one launch (start us, length us, event | category | flops | bytes accessed | tf_op | source)
XLA Modules:
  0.0 49.3 jit_solution(15803117422231328190)
XLA Ops:
  0.6 0.6 %collective-permute-start.2 = (bf16[512,768]{1,0:T(8,128)(2,1)}, bf16[512,768]{1,0:T(8,128)(2,1)S(1)}, u32[]{:S(2)}, u32[]{:S(2)}) collective-permute-start(bf16[512,768]{1,0:T(8,128)(2,1)} %bitcast.3), channel_id=1, source_target_pairs={{0,4},{4,0},{8,12},{12,8},{1,5},{5,1},{9,13},{13,9},{2,6},{6,2},{1... | collective-permute-start | bytes 2359304 | tf_op jit(solution)/shard_map/ppermute | solution.py:340
  1.2 0.1 collective-permute-start.3
  1.3 1.1 %copy-done = bf16[1,512,768]{2,1,0:T(8,128)(2,1)S(1)} copy-done((bf16[1,512,768]{2,1,0:T(8,128)(2,1)S(1)}, bf16[1,512,768]{2,1,0:T(8,128)(2,1)}, u32[]{:S(2)}) %copy-start) | copy-done | bytes 786456
  2.4 0.2 cut.3.refs_0_
  2.6 3.0 %collective-permute-start.5 = (bf16[128,768]{1,0:T(8,128)(2,1)S(1)}, bf16[128,768]{1,0:T(8,128)(2,1)S(1)}, u32[]{:S(2)}, u32[]{:S(2)}) collective-permute-start(bf16[128,768]{1,0:T(8,128)(2,1)S(1)} %cut.3.refs_0_), channel_id=1, source_target_pairs={{0,8},{4,12},{8,0},{12,4},{1,9},{5,13},{9,1},{13,5},{2,10},{6,14},... | collective-permute-start | bytes 589832 | tf_op jit(solution)/shard_map/ppermute | solution.py:340
  5.6 0.5 cut.2
  6.1 0.1 collective-permute-start.1
  6.2 3.7 %unit.1.refs_5_.refs_2_.refs_1_ = bf16[768,2048]{1,0:T(8,128)(2,1)S(1)} custom-call(bf16[2048,768]{1,0:T(8,128)(2,1)} %values_ref.1), custom_call_target="tpu_custom_call" | custom-call | flops 6291456 | bytes 6291456 | tf_op jit(solution)/shard_map/unit/pallas_call | solution.py:84
  9.9 0.0 collective-permute-done.2.refs_4_
  9.9 0.0 copy-start.1
  9.9 3.6 %bank.5.refs_3_ = f32[1,2048]{1,0:T(1,128)S(1)} custom-call(bf16[128,768]{1,0:T(8,128)(2,1)S(1)} %cut.3.refs_0_, bf16[192,768]{1,0:T(8,128)(2,1)S(1)} %get-tuple-element.23.refs_1_, bf16[128,768]{1,0:T(8,128)(2,1)S(1)} %get-tuple-element.24.refs_2_, bf16[64,768]{1,0:T(8,128)(2,1)S(1)} %get-tuple-element.22.refs_3_, ...), custom_call_target="tpu_custom_call" | custom-call | flops 3221225472 | bytes 4718592 | tf_op jit(solution)/shard_map/bank/pallas_call | solution.py:122
  13.6 0.0 collective-permute-done.3.refs_1_
  13.6 1.1 %test.3 = (f32[256,2048]{1,0:T(8,128)S(1)}, f32[256,2048]{1,0:T(8,128)S(1)}) custom-call(bf16[128,768]{1,0:T(8,128)(2,1)S(1)} %bitcast.7, bf16[128,768]{1,0:T(8,128)(2,1)S(1)} %collective-permute-done.3.refs_1_, bf16[768,2048]{1,0:T(8,128)(2,1)S(1)} %unit.1.refs_5_.refs_2_.refs_1_), custom_call_target="tpu_custom_call" | custom-call | flops 805306368 | bytes 7733248 | tf_op jit(solution)/shard_map/test/pallas_call | solution.py:152
  14.7 2.4 %collective-permute-done.1.refs_0_ = bf16[192,768]{1,0:T(8,128)(2,1)S(1)} collective-permute-done((bf16[192,768]{1,0:T(8,128)(2,1)S(1)}, bf16[192,768]{1,0:T(8,128)(2,1)S(1)}, u32[]{:S(2)}, u32[]{:S(2)}) %collective-permute-start.1) | collective-permute-done | bytes 294944 | tf_op jit(solution)/shard_map/ppermute | solution.py:340
  17.1 0.0 collective-permute-start.4
  17.1 0.0 collective-permute-done.5.refs_0_
  17.1 0.5 %collective-permute-start.6 = (bf16[128,768]{1,0:T(8,128)(2,1)S(1)}, bf16[128,768]{1,0:T(8,128)(2,1)S(1)}, u32[]{:S(2)}, u32[]{:S(2)}) collective-permute-start(bf16[128,768]{1,0:T(8,128)(2,1)S(1)} %collective-permute-done.5.refs_0_), channel_id=1, source_target_pairs={{0,4},{4,0},{8,12},{12,8},{1,5},{5,1},{9,13},{13,9},{2,6},{6,2},{1... | collective-permute-start | bytes 589832 | tf_op jit(solution)/shard_map/ppermute | solution.py:340
  17.6 1.7 %collective-permute-start.8 = (bf16[128,768]{1,0:T(8,128)(2,1)S(1)}, bf16[128,768]{1,0:T(8,128)(2,1)S(1)}, u32[]{:S(2)}, u32[]{:S(2)}) collective-permute-start(bf16[128,768]{1,0:T(8,128)(2,1)S(1)} %get-tuple-element.24.refs_2_), channel_id=1, source_target_pairs={{0,8},{4,12},{8,0},{12,4},{1,9},{5,13},{9,1},{13,5},{2,10},{6,14},... | collective-permute-start | bytes 589832 | tf_op jit(solution)/shard_map/ppermute | solution.py:340
  19.4 0.0 collective-permute-done.6.refs_1_
  19.4 1.1 %bank.6.refs_3_ = f32[1,2048]{1,0:T(1,128)S(1)} custom-call(bf16[128,768]{1,0:T(8,128)(2,1)S(1)} %collective-permute-done.5.refs_0_, bf16[128,768]{1,0:T(8,128)(2,1)S(1)} %collective-permute-done.6.refs_1_, bf16[768,2048]{1,0:T(8,128)(2,1)S(1)} %unit.1.refs_5_.refs_2_.refs_1_, f32[1,2048]{1,0:T(1,128)S(1)} %bank.5.refs_3_), custom_call_target="tpu_custom_call" | custom-call | flops 805306368 | bytes 3538944 | tf_op jit(solution)/shard_map/bank/pallas_call | solution.py:122
  20.5 0.0 collective-permute-done.4.refs_1_
  20.5 1.5 %bank.7.refs_3_ = f32[1,2048]{1,0:T(1,128)S(1)} custom-call(bf16[192,768]{1,0:T(8,128)(2,1)S(1)} %collective-permute-done.1.refs_0_, bf16[192,768]{1,0:T(8,128)(2,1)S(1)} %collective-permute-done.4.refs_1_, bf16[768,2048]{1,0:T(8,128)(2,1)S(1)} %unit.1.refs_5_.refs_2_.refs_1_, f32[1,2048]{1,0:T(1,128)S(1)} %bank.6.refs_3_), custom_call_target="tpu_custom_call" | custom-call | flops 1207959552 | bytes 3735552 | tf_op jit(solution)/shard_map/bank/pallas_call | solution.py:122
  22.0 2.4 %collective-permute-done.8.refs_0_ = bf16[128,768]{1,0:T(8,128)(2,1)S(1)} collective-permute-done((bf16[128,768]{1,0:T(8,128)(2,1)S(1)}, bf16[128,768]{1,0:T(8,128)(2,1)S(1)}, u32[]{:S(2)}, u32[]{:S(2)}) %collective-permute-start.8) | collective-permute-done | bytes 196640 | tf_op jit(solution)/shard_map/ppermute | solution.py:340
  24.4 0.0 collective-permute-start.9
  24.4 1.7 %collective-permute-start = (bf16[64,768]{1,0:T(8,128)(2,1)S(1)}, bf16[64,768]{1,0:T(8,128)(2,1)S(1)}, u32[]{:S(2)}, u32[]{:S(2)}) collective-permute-start(bf16[64,768]{1,0:T(8,128)(2,1)S(1)} %get-tuple-element.22.refs_3_), channel_id=1, source_target_pairs={{0,8},{4,12},{8,0},{12,4},{1,9},{5,13},{9,1},{13,5},{2,10},{6,14},... | collective-permute-start | bytes 294920 | tf_op jit(solution)/shard_map/ppermute | solution.py:340
  26.2 0.3 collective-permute-start.13
  26.5 3.6 %collective-permute-done.refs_0_ = bf16[64,768]{1,0:T(8,128)(2,1)S(1)} collective-permute-done((bf16[64,768]{1,0:T(8,128)(2,1)S(1)}, bf16[64,768]{1,0:T(8,128)(2,1)S(1)}, u32[]{:S(2)}, u32[]{:S(2)}) %collective-permute-start) | collective-permute-done | bytes 98336 | tf_op jit(solution)/shard_map/ppermute | solution.py:340
  30.1 0.0 collective-permute-done.9.refs_1_
  30.1 1.1 %bank.8.refs_3_ = f32[1,2048]{1,0:T(1,128)S(1)} custom-call(bf16[128,768]{1,0:T(8,128)(2,1)S(1)} %collective-permute-done.8.refs_0_, bf16[128,768]{1,0:T(8,128)(2,1)S(1)} %collective-permute-done.9.refs_1_, bf16[768,2048]{1,0:T(8,128)(2,1)S(1)} %unit.1.refs_5_.refs_2_.refs_1_, f32[1,2048]{1,0:T(1,128)S(1)} %bank.7.refs_3_), custom_call_target="tpu_custom_call" | custom-call | flops 805306368 | bytes 3538944 | tf_op jit(solution)/shard_map/bank/pallas_call | solution.py:122
  31.2 0.2 collective-permute-done.7.refs_1_
  31.4 0.7 %bank.9.total_ref = f32[1,2048]{1,0:T(1,128)S(1)} custom-call(bf16[64,768]{1,0:T(8,128)(2,1)S(1)} %collective-permute-done.refs_0_, bf16[64,768]{1,0:T(8,128)(2,1)S(1)} %collective-permute-done.7.refs_1_, bf16[768,2048]{1,0:T(8,128)(2,1)S(1)} %unit.1.refs_5_.refs_2_.refs_1_, f32[1,2048]{1,0:T(1,128)S(1)} %bank.8.refs_3_), custom_call_target="tpu_custom_call" | custom-call | flops 402653184 | bytes 3342336 | tf_op jit(solution)/shard_map/bank/pallas_call | solution.py:122
  32.1 1.8 %collective-permute-done.13.refs_0_ = bf16[128,768]{1,0:T(8,128)(2,1)S(1)} collective-permute-done((bf16[128,768]{1,0:T(8,128)(2,1)S(1)}, bf16[128,768]{1,0:T(8,128)(2,1)S(1)}, u32[]{:S(2)}, u32[]{:S(2)}) %collective-permute-start.13) | collective-permute-done | bytes 196640 | tf_op jit(solution)/shard_map/ppermute | solution.py:340
  33.9 1.8 %collective-permute-start.10 = (f32[1,2048]{1,0:T(1,128)S(1)}, f32[1,2048]{1,0:T(1,128)S(1)}, u32[]{:S(2)}, u32[]{:S(2)}) collective-permute-start(f32[1,2048]{1,0:T(1,128)S(1)} %bank.9.total_ref), channel_id=1, source_target_pairs={{0,1},{1,2},{2,3},{3,0},{4,5},{5,6},{6,7},{7,4},{8,9},{9,10},{10,1... | collective-permute-start | bytes 24584 | tf_op jit(solution)/shard_map/ppermute | solution.py:374
  35.7 2.6 %collective-permute-start.11 = (f32[1,2048]{1,0:T(1,128)S(1)}, f32[1,2048]{1,0:T(1,128)S(1)}, u32[]{:S(2)}, u32[]{:S(2)}) collective-permute-start(f32[1,2048]{1,0:T(1,128)S(1)} %bank.9.total_ref), channel_id=1, source_target_pairs={{0,2},{1,3},{2,0},{3,1},{4,6},{5,7},{6,4},{7,5},{8,10},{9,11},{10,... | collective-permute-start | bytes 24584 | tf_op jit(solution)/shard_map/ppermute | solution.py:374
  38.2 1.3 %collective-permute-start.12 = (f32[1,2048]{1,0:T(1,128)S(1)}, f32[1,2048]{1,0:T(1,128)S(1)}, u32[]{:S(2)}, u32[]{:S(2)}) collective-permute-start(f32[1,2048]{1,0:T(1,128)S(1)} %bank.9.total_ref), channel_id=1, source_target_pairs={{0,3},{1,0},{2,1},{3,2},{4,7},{5,4},{6,5},{7,6},{8,11},{9,8},{10,9... | collective-permute-start | bytes 24584 | tf_op jit(solution)/shard_map/ppermute | solution.py:374
  39.6 0.7 %test.4 = (f32[128,2048]{1,0:T(8,128)S(1)}, f32[128,2048]{1,0:T(8,128)S(1)}) custom-call(bf16[128,768]{1,0:T(8,128)(2,1)S(1)} %collective-permute-done.13.refs_0_, bf16[768,2048]{1,0:T(8,128)(2,1)S(1)} %unit.1.refs_5_.refs_2_.refs_1_), custom_call_target="tpu_custom_call" | custom-call | flops 402653184 | bytes 5439488 | tf_op jit(solution)/shard_map/test/pallas_call | solution.py:152
  40.3 0.0 collective-permute-done.14.refs_0_
  40.3 0.7 %test.5 = (f32[128,2048]{1,0:T(8,128)S(1)}, f32[128,2048]{1,0:T(8,128)S(1)}) custom-call(bf16[128,768]{1,0:T(8,128)(2,1)S(1)} %collective-permute-done.14.refs_0_, bf16[768,2048]{1,0:T(8,128)(2,1)S(1)} %unit.1.refs_5_.refs_2_.refs_1_), custom_call_target="tpu_custom_call" | custom-call | flops 402653184 | bytes 5439488 | tf_op jit(solution)/shard_map/test/pallas_call | solution.py:152
  41.0 0.0 collective-permute-done.10.refs_1_
  41.0 0.9 %collective-permute-done.12.refs_3_ = f32[1,2048]{1,0:T(1,128)S(1)} collective-permute-done((f32[1,2048]{1,0:T(1,128)S(1)}, f32[1,2048]{1,0:T(1,128)S(1)}, u32[]{:S(2)}, u32[]{:S(2)}) %collective-permute-start.12) | collective-permute-done | bytes 8224 | tf_op jit(solution)/shard_map/ppermute | solution.py:374
  41.9 0.4 rows.1
  42.3 0.1 collective-permute-start.15
  42.4 1.6 %collective-permute-start.16 = (f32[4,128]{1,0:T(4,128)S(1)}, f32[4,128]{1,0:T(4,128)S(1)}, u32[]{:S(2)}, u32[]{:S(2)}) collective-permute-start(f32[4,128]{1,0:T(4,128)S(1)} %get-tuple-element.36.refs_0_), channel_id=1, source_target_pairs={{0,8},{4,12},{8,0},{12,4},{1,9},{5,13},{9,1},{13,5},{2,10},{6,14},... | collective-permute-start | bytes 6152 | tf_op jit(solution)/shard_map/ppermute | solution.py:340
  44.0 0.3 collective-permute-start.17
  44.2 0.6 %logs.1 = (f32[1,2048]{1,0:T(1,128)S(1)}, f32[1,2048]{1,0:T(1,128)}) custom-call(f32[1,2048]{1,0:T(1,128)S(1)} %get-tuple-element.39.total_ref), custom_call_target="tpu_custom_call" | custom-call | flops 2048 | bytes 24576 | tf_op jit(solution)/shard_map/logs/pallas_call | solution.py:236
  44.8 1.2 %collective-permute-done.16.refs_2_ = f32[4,128]{1,0:T(4,128)S(1)} collective-permute-done((f32[4,128]{1,0:T(4,128)S(1)}, f32[4,128]{1,0:T(4,128)S(1)}, u32[]{:S(2)}, u32[]{:S(2)}) %collective-permute-start.16) | collective-permute-done | bytes 2080 | tf_op jit(solution)/shard_map/ppermute | solution.py:340
  46.0 0.9 %collective-permute-done.17.refs_3_ = f32[4,128]{1,0:T(4,128)S(1)} collective-permute-done((f32[4,128]{1,0:T(4,128)S(1)}, f32[4,128]{1,0:T(4,128)S(1)}, u32[]{:S(2)}, u32[]{:S(2)}) %collective-permute-start.17) | collective-permute-done | bytes 2080 | tf_op jit(solution)/shard_map/ppermute | solution.py:340
  47.0 2.3 %out.1 = f32[512,2048]{1,0:T(8,128)} custom-call(f32[4,128]{1,0:T(4,128)S(1)} %get-tuple-element.36.refs_0_, f32[4,128]{1,0:T(4,128)S(1)} %collective-permute-done.15.refs_1_, f32[4,128]{1,0:T(4,128)S(1)} %collective-permute-done.16.refs_2_, f32[4,128]{1,0:T(4,128)S(1)} %collective-permute-done.17.refs_3_, f32[256,2048]{1,0:T(8,128)S(1)} %get-tuple-element.26.refs_4_, ...), custom_call_target="tpu_custom_call" | custom-call | flops 3145728 | bytes 8388608 | tf_op jit(solution)/shard_map/out/pallas_call | solution.py:301
  (7 shorter events, 0.0 us)
Async XLA Ops:
  0.6 9.3 %collective-permute-start.2 = (bf16[512,768]{1,0:T(8,128)(2,1)}, bf16[512,768]{1,0:T(8,128)(2,1)S(1)}, u32[]{:S(2)}, u32[]{:S(2)}) collective-permute-start(bf16[512,768]{1,0:T(8,128)(2,1)} %bitcast.3), channel_id=1, source_target_pairs={{0,4},{4,0},{8,12},{12,8},{1,5},{5,1},{9,13},{13,9},{2,6},{6,2},{1... | collective-permute-start | bytes 2359304 | tf_op jit(solution)/shard_map/ppermute | solution.py:340
  1.2 12.4 %collective-permute-start.3 = (bf16[128,768]{1,0:T(8,128)(2,1)}, bf16[128,768]{1,0:T(8,128)(2,1)S(1)}, u32[]{:S(2)}, u32[]{:S(2)}) collective-permute-start(bf16[128,768]{1,0:T(8,128)(2,1)} %bitcast.6), channel_id=1, source_target_pairs={{0,4},{4,0},{8,12},{12,8},{1,5},{5,1},{9,13},{13,9},{2,6},{6,2},{1... | collective-permute-start | bytes 589832 | tf_op jit(solution)/shard_map/ppermute | solution.py:340
  1.3 1.1 %copy-start = (bf16[1,512,768]{2,1,0:T(8,128)(2,1)S(1)}, bf16[1,512,768]{2,1,0:T(8,128)(2,1)}, u32[]{:S(2)}) copy-start(bf16[1,512,768]{2,1,0:T(8,128)(2,1)} %param.4) | copy-start | bytes 2359300
  2.6 14.5 %collective-permute-start.5 = (bf16[128,768]{1,0:T(8,128)(2,1)S(1)}, bf16[128,768]{1,0:T(8,128)(2,1)S(1)}, u32[]{:S(2)}, u32[]{:S(2)}) collective-permute-start(bf16[128,768]{1,0:T(8,128)(2,1)S(1)} %cut.3.refs_0_), channel_id=1, source_target_pairs={{0,8},{4,12},{8,0},{12,4},{1,9},{5,13},{9,1},{13,5},{2,10},{6,14},... | collective-permute-start | bytes 589832 | tf_op jit(solution)/shard_map/ppermute | solution.py:340
  6.1 11.0 %collective-permute-start.1 = (bf16[192,768]{1,0:T(8,128)(2,1)S(1)}, bf16[192,768]{1,0:T(8,128)(2,1)S(1)}, u32[]{:S(2)}, u32[]{:S(2)}) collective-permute-start(bf16[192,768]{1,0:T(8,128)(2,1)S(1)} %get-tuple-element.23.refs_1_), channel_id=1, source_target_pairs={{0,8},{4,12},{8,0},{12,4},{1,9},{5,13},{9,1},{13,5},{2,10},{6,14},... | collective-permute-start | bytes 884744 | tf_op jit(solution)/shard_map/ppermute | solution.py:340
  9.9 3.6 %copy-start.1 = (bf16[1,128,768]{2,1,0:T(8,128)(2,1)S(1)}, bf16[1,128,768]{2,1,0:T(8,128)(2,1)}, u32[]{:S(2)}) copy-start(bf16[1,128,768]{2,1,0:T(8,128)(2,1)} %param.5) | copy-start | bytes 589828
  17.1 3.4 %collective-permute-start.4 = (bf16[192,768]{1,0:T(8,128)(2,1)S(1)}, bf16[192,768]{1,0:T(8,128)(2,1)S(1)}, u32[]{:S(2)}, u32[]{:S(2)}) collective-permute-start(bf16[192,768]{1,0:T(8,128)(2,1)S(1)} %collective-permute-done.1.refs_0_), channel_id=1, source_target_pairs={{0,4},{4,0},{8,12},{12,8},{1,5},{5,1},{9,13},{13,9},{2,6},{6,2},{1... | collective-permute-start | bytes 884744 | tf_op jit(solution)/shard_map/ppermute | solution.py:340
  17.1 2.3 %collective-permute-start.6 = (bf16[128,768]{1,0:T(8,128)(2,1)S(1)}, bf16[128,768]{1,0:T(8,128)(2,1)S(1)}, u32[]{:S(2)}, u32[]{:S(2)}) collective-permute-start(bf16[128,768]{1,0:T(8,128)(2,1)S(1)} %collective-permute-done.5.refs_0_), channel_id=1, source_target_pairs={{0,4},{4,0},{8,12},{12,8},{1,5},{5,1},{9,13},{13,9},{2,6},{6,2},{1... | collective-permute-start | bytes 589832 | tf_op jit(solution)/shard_map/ppermute | solution.py:340
  17.6 6.8 %collective-permute-start.8 = (bf16[128,768]{1,0:T(8,128)(2,1)S(1)}, bf16[128,768]{1,0:T(8,128)(2,1)S(1)}, u32[]{:S(2)}, u32[]{:S(2)}) collective-permute-start(bf16[128,768]{1,0:T(8,128)(2,1)S(1)} %get-tuple-element.24.refs_2_), channel_id=1, source_target_pairs={{0,8},{4,12},{8,0},{12,4},{1,9},{5,13},{9,1},{13,5},{2,10},{6,14},... | collective-permute-start | bytes 589832 | tf_op jit(solution)/shard_map/ppermute | solution.py:340
  24.4 5.7 %collective-permute-start.9 = (bf16[128,768]{1,0:T(8,128)(2,1)S(1)}, bf16[128,768]{1,0:T(8,128)(2,1)S(1)}, u32[]{:S(2)}, u32[]{:S(2)}) collective-permute-start(bf16[128,768]{1,0:T(8,128)(2,1)S(1)} %collective-permute-done.8.refs_0_), channel_id=1, source_target_pairs={{0,4},{4,0},{8,12},{12,8},{1,5},{5,1},{9,13},{13,9},{2,6},{6,2},{1... | collective-permute-start | bytes 589832 | tf_op jit(solution)/shard_map/ppermute | solution.py:340
  24.4 5.7 %collective-permute-start = (bf16[64,768]{1,0:T(8,128)(2,1)S(1)}, bf16[64,768]{1,0:T(8,128)(2,1)S(1)}, u32[]{:S(2)}, u32[]{:S(2)}) collective-permute-start(bf16[64,768]{1,0:T(8,128)(2,1)S(1)} %get-tuple-element.22.refs_3_), channel_id=1, source_target_pairs={{0,8},{4,12},{8,0},{12,4},{1,9},{5,13},{9,1},{13,5},{2,10},{6,14},... | collective-permute-start | bytes 294920 | tf_op jit(solution)/shard_map/ppermute | solution.py:340
  26.2 7.7 %collective-permute-start.13 = (bf16[128,768]{1,0:T(8,128)(2,1)S(1)}, bf16[128,768]{1,0:T(8,128)(2,1)S(1)}, u32[]{:S(2)}, u32[]{:S(2)}) collective-permute-start(bf16[128,768]{1,0:T(8,128)(2,1)S(1)} %bitcast.8), channel_id=1, source_target_pairs={{0,8},{4,12},{8,0},{12,4},{1,9},{5,13},{9,1},{13,5},{2,10},{6,14},... | collective-permute-start | bytes 589832 | tf_op jit(solution)/shard_map/ppermute | solution.py:340
  30.1 1.3 %collective-permute-start.7 = (bf16[64,768]{1,0:T(8,128)(2,1)S(1)}, bf16[64,768]{1,0:T(8,128)(2,1)S(1)}, u32[]{:S(2)}, u32[]{:S(2)}) collective-permute-start(bf16[64,768]{1,0:T(8,128)(2,1)S(1)} %collective-permute-done.refs_0_), channel_id=1, source_target_pairs={{0,4},{4,0},{8,12},{12,8},{1,5},{5,1},{9,13},{13,9},{2,6},{6,2},{1... | collective-permute-start | bytes 294920 | tf_op jit(solution)/shard_map/ppermute | solution.py:340
  33.9 6.4 %collective-permute-start.14 = (bf16[128,768]{1,0:T(8,128)(2,1)S(1)}, bf16[128,768]{1,0:T(8,128)(2,1)S(1)}, u32[]{:S(2)}, u32[]{:S(2)}) collective-permute-start(bf16[128,768]{1,0:T(8,128)(2,1)S(1)} %collective-permute-done.13.refs_0_), channel_id=1, source_target_pairs={{0,4},{4,0},{8,12},{12,8},{1,5},{5,1},{9,13},{13,9},{2,6},{6,2},{1... | collective-permute-start | bytes 589832 | tf_op jit(solution)/shard_map/ppermute | solution.py:340
  33.9 7.1 %collective-permute-start.10 = (f32[1,2048]{1,0:T(1,128)S(1)}, f32[1,2048]{1,0:T(1,128)S(1)}, u32[]{:S(2)}, u32[]{:S(2)}) collective-permute-start(f32[1,2048]{1,0:T(1,128)S(1)} %bank.9.total_ref), channel_id=1, source_target_pairs={{0,1},{1,2},{2,3},{3,0},{4,5},{5,6},{6,7},{7,4},{8,9},{9,10},{10,1... | collective-permute-start | bytes 24584 | tf_op jit(solution)/shard_map/ppermute | solution.py:374
  35.7 5.3 %collective-permute-start.11 = (f32[1,2048]{1,0:T(1,128)S(1)}, f32[1,2048]{1,0:T(1,128)S(1)}, u32[]{:S(2)}, u32[]{:S(2)}) collective-permute-start(f32[1,2048]{1,0:T(1,128)S(1)} %bank.9.total_ref), channel_id=1, source_target_pairs={{0,2},{1,3},{2,0},{3,1},{4,6},{5,7},{6,4},{7,5},{8,10},{9,11},{10,... | collective-permute-start | bytes 24584 | tf_op jit(solution)/shard_map/ppermute | solution.py:374
  38.2 3.7 %collective-permute-start.12 = (f32[1,2048]{1,0:T(1,128)S(1)}, f32[1,2048]{1,0:T(1,128)S(1)}, u32[]{:S(2)}, u32[]{:S(2)}) collective-permute-start(f32[1,2048]{1,0:T(1,128)S(1)} %bank.9.total_ref), channel_id=1, source_target_pairs={{0,3},{1,0},{2,1},{3,2},{4,7},{5,4},{6,5},{7,6},{8,11},{9,8},{10,9... | collective-permute-start | bytes 24584 | tf_op jit(solution)/shard_map/ppermute | solution.py:374
  42.3 2.5 %collective-permute-start.15 = (f32[4,128]{1,0:T(4,128)S(1)}, f32[4,128]{1,0:T(4,128)S(1)}, u32[]{:S(2)}, u32[]{:S(2)}) collective-permute-start(f32[4,128]{1,0:T(4,128)S(1)} %get-tuple-element.36.refs_0_), channel_id=1, source_target_pairs={{0,4},{4,0},{8,12},{12,8},{1,5},{5,1},{9,13},{13,9},{2,6},{6,2},{1... | collective-permute-start | bytes 6152 | tf_op jit(solution)/shard_map/ppermute | solution.py:340
  42.4 3.7 %collective-permute-start.16 = (f32[4,128]{1,0:T(4,128)S(1)}, f32[4,128]{1,0:T(4,128)S(1)}, u32[]{:S(2)}, u32[]{:S(2)}) collective-permute-start(f32[4,128]{1,0:T(4,128)S(1)} %get-tuple-element.36.refs_0_), channel_id=1, source_target_pairs={{0,8},{4,12},{8,0},{12,4},{1,9},{5,13},{9,1},{13,5},{2,10},{6,14},... | collective-permute-start | bytes 6152 | tf_op jit(solution)/shard_map/ppermute | solution.py:340
  44.0 3.0 %collective-permute-start.17 = (f32[4,128]{1,0:T(4,128)S(1)}, f32[4,128]{1,0:T(4,128)S(1)}, u32[]{:S(2)}, u32[]{:S(2)}) collective-permute-start(f32[4,128]{1,0:T(4,128)S(1)} %get-tuple-element.36.refs_0_), channel_id=1, source_target_pairs={{0,12},{4,8},{8,4},{12,0},{1,13},{5,9},{9,5},{13,1},{2,14},{6,10},... | collective-permute-start | bytes 6152 | tf_op jit(solution)/shard_map/ppermute | solution.py:340

commit v5 on v4

--- a/solution.py
+++ b/solution.py
@@ -69,18 +69,15 @@
         )
         for start in range(0, rows, step)
     ]
-    ahead = 3
-    for copy in copies[:ahead]:
+    for copy in copies:
         copy.start()
-    for index, start in enumerate(range(0, rows, step)):
-        copies[index].wait()
-        if index + ahead < len(copies):
-            copies[index + ahead].start()
+    for start, copy in zip(range(0, rows, step), copies):
+        copy.wait()
         unit_ref[:, start : start + step] = unit_rows(stage[start : start + step, :]).T
 
 
 def unit_call(values):
-    step = math.gcd(values.shape[0], 256)
+    step = math.gcd(values.shape[0], 512)
     return pl.pallas_call(
         functools.partial(unit_kernel, step),
         out_shape=jax.ShapeDtypeStruct(values.shape[::-1], jnp.bfloat16),
@@ -322,7 +319,8 @@
 def chunk_sizes(rows):
     if rows % 128:
         return [rows]
-    return [rows * part // 32 for part in (8, 12, 8, 4)]
+    first, second, last = rows * 11 // 32 // 16 * 16, rows * 11 // 32 // 16 * 16, rows // 8
+    return [first, second, rows - first - second - last, last]
 
 
 def per_device(gallery, querybank, test_queries):

time: 49.5 us -> 49.3 us (level)
  waiting for transfers between devices: 13.5 us -> 14.9 us
  Pallas kernels: 18.2 us -> 17.1 us
  starting transfers between devices: 15.7 us -> 15.2 us
    ppermute x15, waiting for transfers between devices: 12.6 us -> 13.9 us  [shift(): return lax.ppermute(value, 'gal', moves)]
    pallas_call x1, Pallas kernels: 3.72 us -> 3.02 us  [unit_call(): pl.pallas_call(functools.partial(unit_kernel, step), out_shape=jax.ShapeD...]
    ppermute x15, starting transfers between devices: 9.92 us -> 9.42 us  [shift(): return lax.ppermute(value, 'gal', moves)]
  transfers between devices with their start and end apart: 18 -> 18, of which waited for: 8 -> 9; matrix products, arithmetic and copies ran while one was open for 0% -> 0% of each run, Pallas kernels for 31% -> 29%
where the time goes in v5:
time: 49.3 us; the launch traced here: 49.1 us
  Pallas kernels  17.1 us (35%)
  starting transfers between devices  15.2 us (31%)
  waiting for transfers between devices  14.9 us (30%)
  local copies, waits for them, and re-layouts  1.14 us (2%)
  between operations  0.81 us (2%)
    ppermute x15, waiting for transfers between devices, shift(): return lax.ppermute(value, 'gal', moves)  13.9 us
    ppermute x15, starting transfers between devices, shift(): return lax.ppermute(value, 'gal', moves)  9.42 us
    pallas_call x5, Pallas kernels, bank_call(): pl.pallas_call(functools.partial(bank_kernel, len(blocks), tile), out_sha...  7.96 us
    ppermute x3, starting transfers between devices, per_device(): lax.ppermute(total, 'qb', [(i, (i + s) % groups) for i in range(groups)])  5.73 us
    pallas_call x1, Pallas kernels, unit_call(): pl.pallas_call(functools.partial(unit_kernel, step), out_shape=jax.ShapeD...  3.02 us
    pallas_call x3, Pallas kernels, test_call(): pl.pallas_call(functools.partial(test_kernel, len(blocks), tile), out_sha...  2.42 us
    pallas_call x1, Pallas kernels, out_call(): pl.pallas_call(functools.partial(out_kernel, origins, orders, pairs, core...  2.34 us
    unnamed x4, local copies, waits for them, and re-layouts  1.14 us
  transfers between devices with their start and end apart: 18, of which 9 were waited for; matrix products, arithmetic and copies ran while one was open for 0% of the time, Pallas kernels for 29%

profile of v5, /device:TPU:0, one launch (start us, length us, event | category | flops | bytes accessed | tf_op | source)
XLA Modules:
  0.0 49.1 jit_solution(9515431829018084915)
XLA Ops:
  0.6 0.6 %collective-permute-start.2 = (bf16[512,768]{1,0:T(8,128)(2,1)}, bf16[512,768]{1,0:T(8,128)(2,1)S(1)}, u32[]{:S(2)}, u32[]{:S(2)}) collective-permute-start(bf16[512,768]{1,0:T(8,128)(2,1)} %bitcast.3), channel_id=1, source_target_pairs={{0,4},{4,0},{8,12},{12,8},{1,5},{5,1},{9,13},{13,9},{2,6},{6,2},{1... | collective-permute-start | bytes 2359304 | tf_op jit(solution)/shard_map/ppermute | solution.py:338
  1.2 0.1 collective-permute-start.3
  1.3 1.1 %copy-done = bf16[1,512,768]{2,1,0:T(8,128)(2,1)S(1)} copy-done((bf16[1,512,768]{2,1,0:T(8,128)(2,1)S(1)}, bf16[1,512,768]{2,1,0:T(8,128)(2,1)}, u32[]{:S(2)}) %copy-start) | copy-done | bytes 786456
  2.4 3.0 %collective-permute-start.5 = (bf16[176,768]{1,0:T(8,128)(2,1)S(1)}, bf16[176,768]{1,0:T(8,128)(2,1)S(1)}, u32[]{:S(2)}, u32[]{:S(2)}) collective-permute-start(bf16[176,768]{1,0:T(8,128)(2,1)S(1)} %cut.3.refs_0_), channel_id=1, source_target_pairs={{0,8},{4,12},{8,0},{12,4},{1,9},{5,13},{9,1},{13,5},{2,10},{6,14},... | collective-permute-start | bytes 811016 | tf_op jit(solution)/shard_map/ppermute | solution.py:338
  5.4 0.4 cut.2
  5.8 0.1 collective-permute-start.1
  5.9 3.0 %unit.1.refs_5_.refs_2_.refs_1_ = bf16[768,2048]{1,0:T(8,128)(2,1)S(1)} custom-call(bf16[2048,768]{1,0:T(8,128)(2,1)} %values_ref.1), custom_call_target="tpu_custom_call" | custom-call | flops 6291456 | bytes 6291456 | tf_op jit(solution)/shard_map/unit/pallas_call | solution.py:81
  8.9 0.0 collective-permute-done.2.refs_4_
  8.9 0.0 copy-start.1
  9.0 3.6 %bank.5.refs_3_ = f32[1,2048]{1,0:T(1,128)S(1)} custom-call(bf16[176,768]{1,0:T(8,128)(2,1)S(1)} %cut.3.refs_0_, bf16[176,768]{1,0:T(8,128)(2,1)S(1)} %get-tuple-element.23.refs_1_, bf16[96,768]{1,0:T(8,128)(2,1)S(1)} %get-tuple-element.24.refs_2_, bf16[64,768]{1,0:T(8,128)(2,1)S(1)} %get-tuple-element.22.refs_3_, ...), custom_call_target="tpu_custom_call" | custom-call | flops 3221225472 | bytes 4718592 | tf_op jit(solution)/shard_map/bank/pallas_call | solution.py:119
  12.6 0.2 collective-permute-done.5.refs_0_
  12.8 0.0 collective-permute-start.6
  12.8 0.0 collective-permute-done.3.refs_1_
  12.8 1.1 %test.3 = (f32[256,2048]{1,0:T(8,128)S(1)}, f32[256,2048]{1,0:T(8,128)S(1)}) custom-call(bf16[128,768]{1,0:T(8,128)(2,1)S(1)} %bitcast.7, bf16[128,768]{1,0:T(8,128)(2,1)S(1)} %collective-permute-done.3.refs_1_, bf16[768,2048]{1,0:T(8,128)(2,1)S(1)} %unit.1.refs_5_.refs_2_.refs_1_), custom_call_target="tpu_custom_call" | custom-call | flops 805306368 | bytes 7733248 | tf_op jit(solution)/shard_map/test/pallas_call | solution.py:149
  13.9 4.1 %collective-permute-done.1.refs_0_ = bf16[176,768]{1,0:T(8,128)(2,1)S(1)} collective-permute-done((bf16[176,768]{1,0:T(8,128)(2,1)S(1)}, bf16[176,768]{1,0:T(8,128)(2,1)S(1)}, u32[]{:S(2)}, u32[]{:S(2)}) %collective-permute-start.1) | collective-permute-done | bytes 270368 | tf_op jit(solution)/shard_map/ppermute | solution.py:338
  18.0 0.0 collective-permute-start.4
  18.0 1.7 %collective-permute-start.8 = (bf16[96,768]{1,0:T(8,128)(2,1)S(1)}, bf16[96,768]{1,0:T(8,128)(2,1)S(1)}, u32[]{:S(2)}, u32[]{:S(2)}) collective-permute-start(bf16[96,768]{1,0:T(8,128)(2,1)S(1)} %get-tuple-element.24.refs_2_), channel_id=1, source_target_pairs={{0,8},{4,12},{8,0},{12,4},{1,9},{5,13},{9,1},{13,5},{2,10},{6,14},... | collective-permute-start | bytes 442376 | tf_op jit(solution)/shard_map/ppermute | solution.py:338
  19.7 0.0 collective-permute-done.6.refs_1_
  19.7 1.4 %bank.6.refs_3_ = f32[1,2048]{1,0:T(1,128)S(1)} custom-call(bf16[176,768]{1,0:T(8,128)(2,1)S(1)} %collective-permute-done.5.refs_0_, bf16[176,768]{1,0:T(8,128)(2,1)S(1)} %collective-permute-done.6.refs_1_, bf16[768,2048]{1,0:T(8,128)(2,1)S(1)} %unit.1.refs_5_.refs_2_.refs_1_, f32[1,2048]{1,0:T(1,128)S(1)} %bank.5.refs_3_), custom_call_target="tpu_custom_call" | custom-call | flops 1107296256 | bytes 3686400 | tf_op jit(solution)/shard_map/bank/pallas_call | solution.py:119
  21.1 0.0 collective-permute-done.4.refs_1_
  21.1 1.4 %bank.7.refs_3_ = f32[1,2048]{1,0:T(1,128)S(1)} custom-call(bf16[176,768]{1,0:T(8,128)(2,1)S(1)} %collective-permute-done.1.refs_0_, bf16[176,768]{1,0:T(8,128)(2,1)S(1)} %collective-permute-done.4.refs_1_, bf16[768,2048]{1,0:T(8,128)(2,1)S(1)} %unit.1.refs_5_.refs_2_.refs_1_, f32[1,2048]{1,0:T(1,128)S(1)} %bank.6.refs_3_), custom_call_target="tpu_custom_call" | custom-call | flops 1107296256 | bytes 3686400 | tf_op jit(solution)/shard_map/bank/pallas_call | solution.py:119
  22.5 1.7 %collective-permute-done.8.refs_0_ = bf16[96,768]{1,0:T(8,128)(2,1)S(1)} collective-permute-done((bf16[96,768]{1,0:T(8,128)(2,1)S(1)}, bf16[96,768]{1,0:T(8,128)(2,1)S(1)}, u32[]{:S(2)}, u32[]{:S(2)}) %collective-permute-start.8) | collective-permute-done | bytes 147488 | tf_op jit(solution)/shard_map/ppermute | solution.py:338
  24.2 0.0 collective-permute-start.9
  24.2 1.7 %collective-permute-start = (bf16[64,768]{1,0:T(8,128)(2,1)S(1)}, bf16[64,768]{1,0:T(8,128)(2,1)S(1)}, u32[]{:S(2)}, u32[]{:S(2)}) collective-permute-start(bf16[64,768]{1,0:T(8,128)(2,1)S(1)} %get-tuple-element.22.refs_3_), channel_id=1, source_target_pairs={{0,8},{4,12},{8,0},{12,4},{1,9},{5,13},{9,1},{13,5},{2,10},{6,14},... | collective-permute-start | bytes 294920 | tf_op jit(solution)/shard_map/ppermute | solution.py:338
  26.0 0.3 collective-permute-start.13
  26.3 3.6 %collective-permute-done.refs_0_ = bf16[64,768]{1,0:T(8,128)(2,1)S(1)} collective-permute-done((bf16[64,768]{1,0:T(8,128)(2,1)S(1)}, bf16[64,768]{1,0:T(8,128)(2,1)S(1)}, u32[]{:S(2)}, u32[]{:S(2)}) %collective-permute-start) | collective-permute-done | bytes 98336 | tf_op jit(solution)/shard_map/ppermute | solution.py:338
  29.9 0.0 collective-permute-start.7
  29.9 0.0 collective-permute-done.9.refs_1_
  29.9 0.9 %bank.8.refs_3_ = f32[1,2048]{1,0:T(1,128)S(1)} custom-call(bf16[96,768]{1,0:T(8,128)(2,1)S(1)} %collective-permute-done.8.refs_0_, bf16[96,768]{1,0:T(8,128)(2,1)S(1)} %collective-permute-done.9.refs_1_, bf16[768,2048]{1,0:T(8,128)(2,1)S(1)} %unit.1.refs_5_.refs_2_.refs_1_, f32[1,2048]{1,0:T(1,128)S(1)} %bank.7.refs_3_), custom_call_target="tpu_custom_call" | custom-call | flops 603979776 | bytes 3440640 | tf_op jit(solution)/shard_map/bank/pallas_call | solution.py:119
  30.8 0.4 collective-permute-done.7.refs_1_
  31.2 0.7 %bank.9.total_ref = f32[1,2048]{1,0:T(1,128)S(1)} custom-call(bf16[64,768]{1,0:T(8,128)(2,1)S(1)} %collective-permute-done.refs_0_, bf16[64,768]{1,0:T(8,128)(2,1)S(1)} %collective-permute-done.7.refs_1_, bf16[768,2048]{1,0:T(8,128)(2,1)S(1)} %unit.1.refs_5_.refs_2_.refs_1_, f32[1,2048]{1,0:T(1,128)S(1)} %bank.8.refs_3_), custom_call_target="tpu_custom_call" | custom-call | flops 402653184 | bytes 3342336 | tf_op jit(solution)/shard_map/bank/pallas_call | solution.py:119
  31.9 1.8 %collective-permute-done.13.refs_0_ = bf16[128,768]{1,0:T(8,128)(2,1)S(1)} collective-permute-done((bf16[128,768]{1,0:T(8,128)(2,1)S(1)}, bf16[128,768]{1,0:T(8,128)(2,1)S(1)}, u32[]{:S(2)}, u32[]{:S(2)}) %collective-permute-start.13) | collective-permute-done | bytes 196640 | tf_op jit(solution)/shard_map/ppermute | solution.py:338
  33.6 0.0 collective-permute-start.14
  33.7 1.8 %collective-permute-start.10 = (f32[1,2048]{1,0:T(1,128)S(1)}, f32[1,2048]{1,0:T(1,128)S(1)}, u32[]{:S(2)}, u32[]{:S(2)}) collective-permute-start(f32[1,2048]{1,0:T(1,128)S(1)} %bank.9.total_ref), channel_id=1, source_target_pairs={{0,1},{1,2},{2,3},{3,0},{4,5},{5,6},{6,7},{7,4},{8,9},{9,10},{10,1... | collective-permute-start | bytes 24584 | tf_op jit(solution)/shard_map/ppermute | solution.py:372
  35.4 2.6 %collective-permute-start.11 = (f32[1,2048]{1,0:T(1,128)S(1)}, f32[1,2048]{1,0:T(1,128)S(1)}, u32[]{:S(2)}, u32[]{:S(2)}) collective-permute-start(f32[1,2048]{1,0:T(1,128)S(1)} %bank.9.total_ref), channel_id=1, source_target_pairs={{0,2},{1,3},{2,0},{3,1},{4,6},{5,7},{6,4},{7,5},{8,10},{9,11},{10,... | collective-permute-start | bytes 24584 | tf_op jit(solution)/shard_map/ppermute | solution.py:372
  38.0 1.3 %collective-permute-start.12 = (f32[1,2048]{1,0:T(1,128)S(1)}, f32[1,2048]{1,0:T(1,128)S(1)}, u32[]{:S(2)}, u32[]{:S(2)}) collective-permute-start(f32[1,2048]{1,0:T(1,128)S(1)} %bank.9.total_ref), channel_id=1, source_target_pairs={{0,3},{1,0},{2,1},{3,2},{4,7},{5,4},{6,5},{7,6},{8,11},{9,8},{10,9... | collective-permute-start | bytes 24584 | tf_op jit(solution)/shard_map/ppermute | solution.py:372
  39.4 0.7 %test.4 = (f32[128,2048]{1,0:T(8,128)S(1)}, f32[128,2048]{1,0:T(8,128)S(1)}) custom-call(bf16[128,768]{1,0:T(8,128)(2,1)S(1)} %collective-permute-done.13.refs_0_, bf16[768,2048]{1,0:T(8,128)(2,1)S(1)} %unit.1.refs_5_.refs_2_.refs_1_), custom_call_target="tpu_custom_call" | custom-call | flops 402653184 | bytes 5439488 | tf_op jit(solution)/shard_map/test/pallas_call | solution.py:149
  40.1 0.0 collective-permute-done.14.refs_0_
  40.1 0.7 %test.5 = (f32[128,2048]{1,0:T(8,128)S(1)}, f32[128,2048]{1,0:T(8,128)S(1)}) custom-call(bf16[128,768]{1,0:T(8,128)(2,1)S(1)} %collective-permute-done.14.refs_0_, bf16[768,2048]{1,0:T(8,128)(2,1)S(1)} %unit.1.refs_5_.refs_2_.refs_1_), custom_call_target="tpu_custom_call" | custom-call | flops 402653184 | bytes 5439488 | tf_op jit(solution)/shard_map/test/pallas_call | solution.py:149
  40.8 0.9 %collective-permute-done.12.refs_3_ = f32[1,2048]{1,0:T(1,128)S(1)} collective-permute-done((f32[1,2048]{1,0:T(1,128)S(1)}, f32[1,2048]{1,0:T(1,128)S(1)}, u32[]{:S(2)}, u32[]{:S(2)}) %collective-permute-start.12) | collective-permute-done | bytes 8224 | tf_op jit(solution)/shard_map/ppermute | solution.py:372
  41.7 0.4 rows.1
  42.1 0.1 collective-permute-start.15
  42.2 1.6 %collective-permute-start.16 = (f32[4,128]{1,0:T(4,128)S(1)}, f32[4,128]{1,0:T(4,128)S(1)}, u32[]{:S(2)}, u32[]{:S(2)}) collective-permute-start(f32[4,128]{1,0:T(4,128)S(1)} %get-tuple-element.36.refs_0_), channel_id=1, source_target_pairs={{0,8},{4,12},{8,0},{12,4},{1,9},{5,13},{9,1},{13,5},{2,10},{6,14},... | collective-permute-start | bytes 6152 | tf_op jit(solution)/shard_map/ppermute | solution.py:338
  43.7 0.3 collective-permute-start.17
  44.0 0.6 %logs.1 = (f32[1,2048]{1,0:T(1,128)S(1)}, f32[1,2048]{1,0:T(1,128)}) custom-call(f32[1,2048]{1,0:T(1,128)S(1)} %get-tuple-element.39.total_ref), custom_call_target="tpu_custom_call" | custom-call | flops 2048 | bytes 24576 | tf_op jit(solution)/shard_map/logs/pallas_call | solution.py:233
  44.6 1.2 %collective-permute-done.16.refs_2_ = f32[4,128]{1,0:T(4,128)S(1)} collective-permute-done((f32[4,128]{1,0:T(4,128)S(1)}, f32[4,128]{1,0:T(4,128)S(1)}, u32[]{:S(2)}, u32[]{:S(2)}) %collective-permute-start.16) | collective-permute-done | bytes 2080 | tf_op jit(solution)/shard_map/ppermute | solution.py:338
  45.8 0.9 %collective-permute-done.17.refs_3_ = f32[4,128]{1,0:T(4,128)S(1)} collective-permute-done((f32[4,128]{1,0:T(4,128)S(1)}, f32[4,128]{1,0:T(4,128)S(1)}, u32[]{:S(2)}, u32[]{:S(2)}) %collective-permute-start.17) | collective-permute-done | bytes 2080 | tf_op jit(solution)/shard_map/ppermute | solution.py:338
  46.8 2.3 %out.1 = f32[512,2048]{1,0:T(8,128)} custom-call(f32[4,128]{1,0:T(4,128)S(1)} %get-tuple-element.36.refs_0_, f32[4,128]{1,0:T(4,128)S(1)} %collective-permute-done.15.refs_1_, f32[4,128]{1,0:T(4,128)S(1)} %collective-permute-done.16.refs_2_, f32[4,128]{1,0:T(4,128)S(1)} %collective-permute-done.17.refs_3_, f32[256,2048]{1,0:T(8,128)S(1)} %get-tuple-element.26.refs_4_, ...), custom_call_target="tpu_custom_call" | custom-call | flops 3145728 | bytes 8388608 | tf_op jit(solution)/shard_map/out/pallas_call | solution.py:298
  (7 shorter events, 0.0 us)
Async XLA Ops:
  0.6 8.3 %collective-permute-start.2 = (bf16[512,768]{1,0:T(8,128)(2,1)}, bf16[512,768]{1,0:T(8,128)(2,1)S(1)}, u32[]{:S(2)}, u32[]{:S(2)}) collective-permute-start(bf16[512,768]{1,0:T(8,128)(2,1)} %bitcast.3), channel_id=1, source_target_pairs={{0,4},{4,0},{8,12},{12,8},{1,5},{5,1},{9,13},{13,9},{2,6},{6,2},{1... | collective-permute-start | bytes 2359304 | tf_op jit(solution)/shard_map/ppermute | solution.py:338
  1.2 11.6 %collective-permute-start.3 = (bf16[128,768]{1,0:T(8,128)(2,1)}, bf16[128,768]{1,0:T(8,128)(2,1)S(1)}, u32[]{:S(2)}, u32[]{:S(2)}) collective-permute-start(bf16[128,768]{1,0:T(8,128)(2,1)} %bitcast.6), channel_id=1, source_target_pairs={{0,4},{4,0},{8,12},{12,8},{1,5},{5,1},{9,13},{13,9},{2,6},{6,2},{1... | collective-permute-start | bytes 589832 | tf_op jit(solution)/shard_map/ppermute | solution.py:338
  1.3 1.1 %copy-start = (bf16[1,512,768]{2,1,0:T(8,128)(2,1)S(1)}, bf16[1,512,768]{2,1,0:T(8,128)(2,1)}, u32[]{:S(2)}) copy-start(bf16[1,512,768]{2,1,0:T(8,128)(2,1)} %param.4) | copy-start | bytes 2359300
  2.4 10.3 %collective-permute-start.5 = (bf16[176,768]{1,0:T(8,128)(2,1)S(1)}, bf16[176,768]{1,0:T(8,128)(2,1)S(1)}, u32[]{:S(2)}, u32[]{:S(2)}) collective-permute-start(bf16[176,768]{1,0:T(8,128)(2,1)S(1)} %cut.3.refs_0_), channel_id=1, source_target_pairs={{0,8},{4,12},{8,0},{12,4},{1,9},{5,13},{9,1},{13,5},{2,10},{6,14},... | collective-permute-start | bytes 811016 | tf_op jit(solution)/shard_map/ppermute | solution.py:338
  5.8 12.1 %collective-permute-start.1 = (bf16[176,768]{1,0:T(8,128)(2,1)S(1)}, bf16[176,768]{1,0:T(8,128)(2,1)S(1)}, u32[]{:S(2)}, u32[]{:S(2)}) collective-permute-start(bf16[176,768]{1,0:T(8,128)(2,1)S(1)} %get-tuple-element.23.refs_1_), channel_id=1, source_target_pairs={{0,8},{4,12},{8,0},{12,4},{1,9},{5,13},{9,1},{13,5},{2,10},{6,14},... | collective-permute-start | bytes 811016 | tf_op jit(solution)/shard_map/ppermute | solution.py:338
  8.9 3.8 %copy-start.1 = (bf16[1,128,768]{2,1,0:T(8,128)(2,1)S(1)}, bf16[1,128,768]{2,1,0:T(8,128)(2,1)}, u32[]{:S(2)}) copy-start(bf16[1,128,768]{2,1,0:T(8,128)(2,1)} %param.5) | copy-start | bytes 589828
  12.8 6.9 %collective-permute-start.6 = (bf16[176,768]{1,0:T(8,128)(2,1)S(1)}, bf16[176,768]{1,0:T(8,128)(2,1)S(1)}, u32[]{:S(2)}, u32[]{:S(2)}) collective-permute-start(bf16[176,768]{1,0:T(8,128)(2,1)S(1)} %collective-permute-done.5.refs_0_), channel_id=1, source_target_pairs={{0,4},{4,0},{8,12},{12,8},{1,5},{5,1},{9,13},{13,9},{2,6},{6,2},{1... | collective-permute-start | bytes 811016 | tf_op jit(solution)/shard_map/ppermute | solution.py:338
  18.0 3.2 %collective-permute-start.4 = (bf16[176,768]{1,0:T(8,128)(2,1)S(1)}, bf16[176,768]{1,0:T(8,128)(2,1)S(1)}, u32[]{:S(2)}, u32[]{:S(2)}) collective-permute-start(bf16[176,768]{1,0:T(8,128)(2,1)S(1)} %collective-permute-done.1.refs_0_), channel_id=1, source_target_pairs={{0,4},{4,0},{8,12},{12,8},{1,5},{5,1},{9,13},{13,9},{2,6},{6,2},{1... | collective-permute-start | bytes 811016 | tf_op jit(solution)/shard_map/ppermute | solution.py:338
  18.0 6.3 %collective-permute-start.8 = (bf16[96,768]{1,0:T(8,128)(2,1)S(1)}, bf16[96,768]{1,0:T(8,128)(2,1)S(1)}, u32[]{:S(2)}, u32[]{:S(2)}) collective-permute-start(bf16[96,768]{1,0:T(8,128)(2,1)S(1)} %get-tuple-element.24.refs_2_), channel_id=1, source_target_pairs={{0,8},{4,12},{8,0},{12,4},{1,9},{5,13},{9,1},{13,5},{2,10},{6,14},... | collective-permute-start | bytes 442376 | tf_op jit(solution)/shard_map/ppermute | solution.py:338
  24.2 5.7 %collective-permute-start.9 = (bf16[96,768]{1,0:T(8,128)(2,1)S(1)}, bf16[96,768]{1,0:T(8,128)(2,1)S(1)}, u32[]{:S(2)}, u32[]{:S(2)}) collective-permute-start(bf16[96,768]{1,0:T(8,128)(2,1)S(1)} %collective-permute-done.8.refs_0_), channel_id=1, source_target_pairs={{0,4},{4,0},{8,12},{12,8},{1,5},{5,1},{9,13},{13,9},{2,6},{6,2},{1... | collective-permute-start | bytes 442376 | tf_op jit(solution)/shard_map/ppermute | solution.py:338
  24.2 5.7 %collective-permute-start = (bf16[64,768]{1,0:T(8,128)(2,1)S(1)}, bf16[64,768]{1,0:T(8,128)(2,1)S(1)}, u32[]{:S(2)}, u32[]{:S(2)}) collective-permute-start(bf16[64,768]{1,0:T(8,128)(2,1)S(1)} %get-tuple-element.22.refs_3_), channel_id=1, source_target_pairs={{0,8},{4,12},{8,0},{12,4},{1,9},{5,13},{9,1},{13,5},{2,10},{6,14},... | collective-permute-start | bytes 294920 | tf_op jit(solution)/shard_map/ppermute | solution.py:338
  26.0 7.7 %collective-permute-start.13 = (bf16[128,768]{1,0:T(8,128)(2,1)S(1)}, bf16[128,768]{1,0:T(8,128)(2,1)S(1)}, u32[]{:S(2)}, u32[]{:S(2)}) collective-permute-start(bf16[128,768]{1,0:T(8,128)(2,1)S(1)} %bitcast.8), channel_id=1, source_target_pairs={{0,8},{4,12},{8,0},{12,4},{1,9},{5,13},{9,1},{13,5},{2,10},{6,14},... | collective-permute-start | bytes 589832 | tf_op jit(solution)/shard_map/ppermute | solution.py:338
  29.9 1.3 %collective-permute-start.7 = (bf16[64,768]{1,0:T(8,128)(2,1)S(1)}, bf16[64,768]{1,0:T(8,128)(2,1)S(1)}, u32[]{:S(2)}, u32[]{:S(2)}) collective-permute-start(bf16[64,768]{1,0:T(8,128)(2,1)S(1)} %collective-permute-done.refs_0_), channel_id=1, source_target_pairs={{0,4},{4,0},{8,12},{12,8},{1,5},{5,1},{9,13},{13,9},{2,6},{6,2},{1... | collective-permute-start | bytes 294920 | tf_op jit(solution)/shard_map/ppermute | solution.py:338
  33.6 6.4 %collective-permute-start.14 = (bf16[128,768]{1,0:T(8,128)(2,1)S(1)}, bf16[128,768]{1,0:T(8,128)(2,1)S(1)}, u32[]{:S(2)}, u32[]{:S(2)}) collective-permute-start(bf16[128,768]{1,0:T(8,128)(2,1)S(1)} %collective-permute-done.13.refs_0_), channel_id=1, source_target_pairs={{0,4},{4,0},{8,12},{12,8},{1,5},{5,1},{9,13},{13,9},{2,6},{6,2},{1... | collective-permute-start | bytes 589832 | tf_op jit(solution)/shard_map/ppermute | solution.py:338
  33.7 7.1 %collective-permute-start.10 = (f32[1,2048]{1,0:T(1,128)S(1)}, f32[1,2048]{1,0:T(1,128)S(1)}, u32[]{:S(2)}, u32[]{:S(2)}) collective-permute-start(f32[1,2048]{1,0:T(1,128)S(1)} %bank.9.total_ref), channel_id=1, source_target_pairs={{0,1},{1,2},{2,3},{3,0},{4,5},{5,6},{6,7},{7,4},{8,9},{9,10},{10,1... | collective-permute-start | bytes 24584 | tf_op jit(solution)/shard_map/ppermute | solution.py:372
  35.4 5.3 %collective-permute-start.11 = (f32[1,2048]{1,0:T(1,128)S(1)}, f32[1,2048]{1,0:T(1,128)S(1)}, u32[]{:S(2)}, u32[]{:S(2)}) collective-permute-start(f32[1,2048]{1,0:T(1,128)S(1)} %bank.9.total_ref), channel_id=1, source_target_pairs={{0,2},{1,3},{2,0},{3,1},{4,6},{5,7},{6,4},{7,5},{8,10},{9,11},{10,... | collective-permute-start | bytes 24584 | tf_op jit(solution)/shard_map/ppermute | solution.py:372
  38.0 3.7 %collective-permute-start.12 = (f32[1,2048]{1,0:T(1,128)S(1)}, f32[1,2048]{1,0:T(1,128)S(1)}, u32[]{:S(2)}, u32[]{:S(2)}) collective-permute-start(f32[1,2048]{1,0:T(1,128)S(1)} %bank.9.total_ref), channel_id=1, source_target_pairs={{0,3},{1,0},{2,1},{3,2},{4,7},{5,4},{6,5},{7,6},{8,11},{9,8},{10,9... | collective-permute-start | bytes 24584 | tf_op jit(solution)/shard_map/ppermute | solution.py:372
  42.1 2.5 %collective-permute-start.15 = (f32[4,128]{1,0:T(4,128)S(1)}, f32[4,128]{1,0:T(4,128)S(1)}, u32[]{:S(2)}, u32[]{:S(2)}) collective-permute-start(f32[4,128]{1,0:T(4,128)S(1)} %get-tuple-element.36.refs_0_), channel_id=1, source_target_pairs={{0,4},{4,0},{8,12},{12,8},{1,5},{5,1},{9,13},{13,9},{2,6},{6,2},{1... | collective-permute-start | bytes 6152 | tf_op jit(solution)/shard_map/ppermute | solution.py:338
  42.2 3.7 %collective-permute-start.16 = (f32[4,128]{1,0:T(4,128)S(1)}, f32[4,128]{1,0:T(4,128)S(1)}, u32[]{:S(2)}, u32[]{:S(2)}) collective-permute-start(f32[4,128]{1,0:T(4,128)S(1)} %get-tuple-element.36.refs_0_), channel_id=1, source_target_pairs={{0,8},{4,12},{8,0},{12,4},{1,9},{5,13},{9,1},{13,5},{2,10},{6,14},... | collective-permute-start | bytes 6152 | tf_op jit(solution)/shard_map/ppermute | solution.py:338
  43.7 3.0 %collective-permute-start.17 = (f32[4,128]{1,0:T(4,128)S(1)}, f32[4,128]{1,0:T(4,128)S(1)}, u32[]{:S(2)}, u32[]{:S(2)}) collective-permute-start(f32[4,128]{1,0:T(4,128)S(1)} %get-tuple-element.36.refs_0_), channel_id=1, source_target_pairs={{0,12},{4,8},{8,4},{12,0},{1,13},{5,9},{9,5},{13,1},{2,14},{6,10},... | collective-permute-start | bytes 6152 | tf_op jit(solution)/shard_map/ppermute | solution.py:338

commit v6 on v5

--- a/solution.py
+++ b/solution.py
@@ -222,37 +222,39 @@
     )(*totals, *powers)
 
 
-def log_kernel(total_ref, log_ref, again_ref):
-    value = jnp.log(total_ref[...])
-    log_ref[...] = value
-    again_ref[...] = value
-
-
-def log_call(total):
-    shape = jax.ShapeDtypeStruct(total.shape, jnp.float32)
+def log_kernel(total_ref, *refs):
+    scores, log_ref, outs = refs[: len(refs) // 2], refs[len(refs) // 2], refs[len(refs) // 2 + 1 :]
+    log_ref[...] = jnp.log(total_ref[...])
+    for score_ref, out_ref in zip(scores, outs):
+        height, columns = score_ref.shape
+        for first in range(0, height, 64):
+            for start in range(0, columns, LANES):
+                cut = slice(start, start + LANES)
+                rows = slice(first, min(first + 64, height))
+                out_ref[rows, cut] = score_ref[rows, cut] - log_ref[:, cut]
+
+
+def log_call(total, scores):
+    shapes = [jax.ShapeDtypeStruct(one.shape, jnp.float32) for one in (total, *scores)]
     return pl.pallas_call(
         log_kernel,
-        out_shape=(shape, shape),
-        in_specs=[VMEM],
-        out_specs=(VMEM, VMEM),
+        out_shape=shapes,
+        in_specs=[VMEM] * len(shapes),
+        out_specs=[VMEM] * len(shapes),
         compiler_params=params(16),
         name="logs",
         cost_estimate=pl.CostEstimate(
             flops=total.size, bytes_accessed=12 * total.size, transcendentals=total.size
         ),
-    )(total)
+    )(total, *scores)
 
 
 def out_kernel(origins, orders, pairs, core, height, *refs):
     count = len(origins)
-    parts, scores, (log_ref, out_ref, stage, sems) = (
-        refs[:count],
-        refs[count:-4],
-        refs[-4:],
-    )
+    parts, scores, (out_ref, stage, sems) = refs[:count], refs[count:-3], refs[-3:]
     width = parts[0].shape[1]
     line = height // width
-    step = math.gcd(width, 64)
+    step = math.gcd(width, 32)
     where = lax.axis_index("gal")
     pair_at, core_at = lax.div(where, core), lax.rem(where, core)
     rows_of = [(score, first) for score in scores for first in range(0, score.shape[0], height)]
@@ -271,9 +273,9 @@
             for piece in range(0, width, step):
                 at = len(copies) * step
                 begin = first + sub + piece
-                for start in range(0, log_ref.shape[1], LANES):
+                for start in range(0, stage.shape[1], LANES):
                     cut = slice(start, start + LANES)
-                    value = source[begin : begin + step, cut] - log_ref[:, cut]
+                    value = source[begin : begin + step, cut]
                     stage[at : at + step, cut] = value - wide[piece : piece + step, :]
                 target = pl.multiple_of(place + (sub + piece), step)
                 copies.append(
@@ -290,15 +292,15 @@
         copy.wait()
 
 
-def out_call(origins, orders, pairs, core, parts, scores, log_total):
-    columns = log_total.shape[1]
+def out_call(origins, orders, pairs, core, parts, scores):
+    columns = scores[0].shape[1]
     rows = sum(score.shape[0] for score in scores)
     height = rows // len(origins)
-    step = math.gcd(parts[0].shape[1], 64)
+    step = math.gcd(parts[0].shape[1], 32)
     return pl.pallas_call(
         functools.partial(out_kernel, origins, orders, pairs, core, height),
         out_shape=jax.ShapeDtypeStruct((rows, columns), jnp.float32),
-        in_specs=[VMEM] * (len(parts) + len(scores) + 1),
+        in_specs=[VMEM] * (len(parts) + len(scores)),
         out_specs=pl.BlockSpec(memory_space=pl.ANY),
         scratch_shapes=[
             pltpu.VMEM((rows, columns), jnp.float32),
@@ -309,7 +311,7 @@
         cost_estimate=pl.CostEstimate(
             flops=3 * rows * columns, bytes_accessed=8 * rows * columns, transcendentals=0
         ),
-    )(*parts, *scores, log_total)
+    )(*parts, *scores)
 
 
 def after(value, token):
@@ -319,7 +321,7 @@
 def chunk_sizes(rows):
     if rows % 128:
         return [rows]
-    first, second, last = rows * 11 // 32 // 16 * 16, rows * 11 // 32 // 16 * 16, rows // 8
+    first, second, last = rows * 10 // 32 // 16 * 16, rows * 11 // 32 // 16 * 16, rows // 8
     return [first, second, rows - first - second - last, last]
 
 
@@ -391,8 +393,8 @@
         orders.append(
             [origins.index(((p - pair) % pairs, f ^ flip)) for p, f in origins]
         )
-    log_total, normalizer = log_call(total)
-    logprob = out_call(origins, orders, pairs, core, parts, scores, log_total)
+    normalizer, *scores = log_call(total, scores)
+    logprob = out_call(origins, orders, pairs, core, parts, scores)
     return (logprob, normalizer.reshape(-1))
 
 

time: 49.3 us -> 49.6 us (level)
  transfers between devices with their start and end apart: 18 -> 18, of which waited for: 9 -> 8; matrix products, arithmetic and copies ran while one was open for 0% -> 0% of each run, Pallas kernels for 29% -> 30%
where the time goes in v6:
time: 49.6 us; the launch traced here: 49.4 us
  Pallas kernels  17.5 us (35%)
  starting transfers between devices  15.2 us (31%)
  waiting for transfers between devices  14.6 us (29%)
  local copies, waits for them, and re-layouts  1.14 us (2%)
  between operations  0.99 us (2%)
    ppermute x15, waiting for transfers between devices, shift(): return lax.ppermute(value, 'gal', moves)  13.6 us
    ppermute x15, starting transfers between devices, shift(): return lax.ppermute(value, 'gal', moves)  9.49 us
    pallas_call x5, Pallas kernels, bank_call(): pl.pallas_call(functools.partial(bank_kernel, len(blocks), tile), out_sha...  7.97 us
    ppermute x3, starting transfers between devices, per_device(): lax.ppermute(total, 'qb', [(i, (i + s) % groups) for i in range(groups)])  5.74 us
    pallas_call x1, Pallas kernels, unit_call(): pl.pallas_call(functools.partial(unit_kernel, step), out_shape=jax.ShapeD...  3.02 us
    pallas_call x3, Pallas kernels, test_call(): pl.pallas_call(functools.partial(test_kernel, len(blocks), tile), out_sha...  2.42 us
    pallas_call x1, Pallas kernels, out_call(): pl.pallas_call(functools.partial(out_kernel, origins, orders, pairs, core...  2.27 us
    unnamed x4, local copies, waits for them, and re-layouts  1.14 us
  transfers between devices with their start and end apart: 18, of which 8 were waited for; matrix products, arithmetic and copies ran while one was open for 0% of the time, Pallas kernels for 30%

profile of v6, /device:TPU:0, one launch (start us, length us, event | category | flops | bytes accessed | tf_op | source)
XLA Modules:
  0.0 49.4 jit_solution(9659705265233673420)
XLA Ops:
  0.6 0.6 %collective-permute-start.2 = (bf16[512,768]{1,0:T(8,128)(2,1)}, bf16[512,768]{1,0:T(8,128)(2,1)S(1)}, u32[]{:S(2)}, u32[]{:S(2)}) collective-permute-start(bf16[512,768]{1,0:T(8,128)(2,1)} %bitcast.3), channel_id=1, source_target_pairs={{0,4},{4,0},{8,12},{12,8},{1,5},{5,1},{9,13},{13,9},{2,6},{6,2},{1... | collective-permute-start | bytes 2359304 | tf_op jit(solution)/shard_map/ppermute | solution.py:340
  1.2 0.1 collective-permute-start.3
  1.3 1.1 %copy-done = bf16[1,512,768]{2,1,0:T(8,128)(2,1)S(1)} copy-done((bf16[1,512,768]{2,1,0:T(8,128)(2,1)S(1)}, bf16[1,512,768]{2,1,0:T(8,128)(2,1)}, u32[]{:S(2)}) %copy-start) | copy-done | bytes 786456
  2.4 0.3 cut.3.refs_0_
  2.7 3.0 %collective-permute-start.5 = (bf16[160,768]{1,0:T(8,128)(2,1)S(1)}, bf16[160,768]{1,0:T(8,128)(2,1)S(1)}, u32[]{:S(2)}, u32[]{:S(2)}) collective-permute-start(bf16[160,768]{1,0:T(8,128)(2,1)S(1)} %cut.3.refs_0_), channel_id=1, source_target_pairs={{0,8},{4,12},{8,0},{12,4},{1,9},{5,13},{9,1},{13,5},{2,10},{6,14},... | collective-permute-start | bytes 737288 | tf_op jit(solution)/shard_map/ppermute | solution.py:340
  5.7 0.4 cut.2
  6.1 0.1 collective-permute-start.1
  6.2 3.0 %unit.1.refs_5_.refs_2_.refs_1_ = bf16[768,2048]{1,0:T(8,128)(2,1)S(1)} custom-call(bf16[2048,768]{1,0:T(8,128)(2,1)} %values_ref.1), custom_call_target="tpu_custom_call" | custom-call | flops 6291456 | bytes 6291456 | tf_op jit(solution)/shard_map/unit/pallas_call | solution.py:81
  9.2 0.0 collective-permute-done.2.refs_4_
  9.2 0.0 copy-start.1
  9.2 3.6 %bank.5.refs_3_ = f32[1,2048]{1,0:T(1,128)S(1)} custom-call(bf16[160,768]{1,0:T(8,128)(2,1)S(1)} %cut.3.refs_0_, bf16[176,768]{1,0:T(8,128)(2,1)S(1)} %get-tuple-element.25.refs_1_, bf16[112,768]{1,0:T(8,128)(2,1)S(1)} %get-tuple-element.26.refs_2_, bf16[64,768]{1,0:T(8,128)(2,1)S(1)} %get-tuple-element.24.refs_3_, ...), custom_call_target="tpu_custom_call" | custom-call | flops 3221225472 | bytes 4718592 | tf_op jit(solution)/shard_map/bank/pallas_call | solution.py:119
  12.9 0.0 collective-permute-done.5.refs_0_
  12.9 0.1 collective-permute-start.6
  13.0 0.0 collective-permute-done.3.refs_1_
  13.0 1.1 %test.3 = (f32[256,2048]{1,0:T(8,128)S(1)}, f32[256,2048]{1,0:T(8,128)S(1)}) custom-call(bf16[128,768]{1,0:T(8,128)(2,1)S(1)} %bitcast.7, bf16[128,768]{1,0:T(8,128)(2,1)S(1)} %collective-permute-done.3.refs_1_, bf16[768,2048]{1,0:T(8,128)(2,1)S(1)} %unit.1.refs_5_.refs_2_.refs_1_), custom_call_target="tpu_custom_call" | custom-call | flops 805306368 | bytes 7733248 | tf_op jit(solution)/shard_map/test/pallas_call | solution.py:149
  14.1 3.6 %collective-permute-done.1.refs_0_ = bf16[176,768]{1,0:T(8,128)(2,1)S(1)} collective-permute-done((bf16[176,768]{1,0:T(8,128)(2,1)S(1)}, bf16[176,768]{1,0:T(8,128)(2,1)S(1)}, u32[]{:S(2)}, u32[]{:S(2)}) %collective-permute-start.1) | collective-permute-done | bytes 270368 | tf_op jit(solution)/shard_map/ppermute | solution.py:340
  17.7 0.0 collective-permute-start.4
  17.7 1.7 %collective-permute-start.8 = (bf16[112,768]{1,0:T(8,128)(2,1)S(1)}, bf16[112,768]{1,0:T(8,128)(2,1)S(1)}, u32[]{:S(2)}, u32[]{:S(2)}) collective-permute-start(bf16[112,768]{1,0:T(8,128)(2,1)S(1)} %get-tuple-element.26.refs_2_), channel_id=1, source_target_pairs={{0,8},{4,12},{8,0},{12,4},{1,9},{5,13},{9,1},{13,5},{2,10},{6,14},... | collective-permute-start | bytes 516104 | tf_op jit(solution)/shard_map/ppermute | solution.py:340
  19.4 1.3 %bank.6.refs_3_ = f32[1,2048]{1,0:T(1,128)S(1)} custom-call(bf16[160,768]{1,0:T(8,128)(2,1)S(1)} %collective-permute-done.5.refs_0_, bf16[160,768]{1,0:T(8,128)(2,1)S(1)} %collective-permute-done.6.refs_1_, bf16[768,2048]{1,0:T(8,128)(2,1)S(1)} %unit.1.refs_5_.refs_2_.refs_1_, f32[1,2048]{1,0:T(1,128)S(1)} %bank.5.refs_3_), custom_call_target="tpu_custom_call" | custom-call | flops 1006632960 | bytes 3637248 | tf_op jit(solution)/shard_map/bank/pallas_call | solution.py:119
  20.8 1.4 %bank.7.refs_3_ = f32[1,2048]{1,0:T(1,128)S(1)} custom-call(bf16[176,768]{1,0:T(8,128)(2,1)S(1)} %collective-permute-done.1.refs_0_, bf16[176,768]{1,0:T(8,128)(2,1)S(1)} %collective-permute-done.4.refs_1_, bf16[768,2048]{1,0:T(8,128)(2,1)S(1)} %unit.1.refs_5_.refs_2_.refs_1_, f32[1,2048]{1,0:T(1,128)S(1)} %bank.6.refs_3_), custom_call_target="tpu_custom_call" | custom-call | flops 1107296256 | bytes 3686400 | tf_op jit(solution)/shard_map/bank/pallas_call | solution.py:119
  22.2 2.3 %collective-permute-done.8.refs_0_ = bf16[112,768]{1,0:T(8,128)(2,1)S(1)} collective-permute-done((bf16[112,768]{1,0:T(8,128)(2,1)S(1)}, bf16[112,768]{1,0:T(8,128)(2,1)S(1)}, u32[]{:S(2)}, u32[]{:S(2)}) %collective-permute-start.8) | collective-permute-done | bytes 172064 | tf_op jit(solution)/shard_map/ppermute | solution.py:340
  24.5 0.0 collective-permute-start.9
  24.5 1.7 %collective-permute-start = (bf16[64,768]{1,0:T(8,128)(2,1)S(1)}, bf16[64,768]{1,0:T(8,128)(2,1)S(1)}, u32[]{:S(2)}, u32[]{:S(2)}) collective-permute-start(bf16[64,768]{1,0:T(8,128)(2,1)S(1)} %get-tuple-element.24.refs_3_), channel_id=1, source_target_pairs={{0,8},{4,12},{8,0},{12,4},{1,9},{5,13},{9,1},{13,5},{2,10},{6,14},... | collective-permute-start | bytes 294920 | tf_op jit(solution)/shard_map/ppermute | solution.py:340
  26.2 0.3 collective-permute-start.13
  26.5 3.6 %collective-permute-done.refs_0_ = bf16[64,768]{1,0:T(8,128)(2,1)S(1)} collective-permute-done((bf16[64,768]{1,0:T(8,128)(2,1)S(1)}, bf16[64,768]{1,0:T(8,128)(2,1)S(1)}, u32[]{:S(2)}, u32[]{:S(2)}) %collective-permute-start) | collective-permute-done | bytes 98336 | tf_op jit(solution)/shard_map/ppermute | solution.py:340
  30.2 0.0 collective-permute-start.7
  30.2 0.0 collective-permute-done.9.refs_1_
  30.2 1.0 %bank.8.refs_3_ = f32[1,2048]{1,0:T(1,128)S(1)} custom-call(bf16[112,768]{1,0:T(8,128)(2,1)S(1)} %collective-permute-done.8.refs_0_, bf16[112,768]{1,0:T(8,128)(2,1)S(1)} %collective-permute-done.9.refs_1_, bf16[768,2048]{1,0:T(8,128)(2,1)S(1)} %unit.1.refs_5_.refs_2_.refs_1_, f32[1,2048]{1,0:T(1,128)S(1)} %bank.7.refs_3_), custom_call_target="tpu_custom_call" | custom-call | flops 704643072 | bytes 3489792 | tf_op jit(solution)/shard_map/bank/pallas_call | solution.py:119
  31.2 0.3 collective-permute-done.7.refs_1_
  31.5 0.7 %bank.9.total_ref = f32[1,2048]{1,0:T(1,128)S(1)} custom-call(bf16[64,768]{1,0:T(8,128)(2,1)S(1)} %collective-permute-done.refs_0_, bf16[64,768]{1,0:T(8,128)(2,1)S(1)} %collective-permute-done.7.refs_1_, bf16[768,2048]{1,0:T(8,128)(2,1)S(1)} %unit.1.refs_5_.refs_2_.refs_1_, f32[1,2048]{1,0:T(1,128)S(1)} %bank.8.refs_3_), custom_call_target="tpu_custom_call" | custom-call | flops 402653184 | bytes 3342336 | tf_op jit(solution)/shard_map/bank/pallas_call | solution.py:119
  32.1 1.8 %collective-permute-done.13.refs_0_ = bf16[128,768]{1,0:T(8,128)(2,1)S(1)} collective-permute-done((bf16[128,768]{1,0:T(8,128)(2,1)S(1)}, bf16[128,768]{1,0:T(8,128)(2,1)S(1)}, u32[]{:S(2)}, u32[]{:S(2)}) %collective-permute-start.13) | collective-permute-done | bytes 196640 | tf_op jit(solution)/shard_map/ppermute | solution.py:340
  33.9 1.8 %collective-permute-start.10 = (f32[1,2048]{1,0:T(1,128)S(1)}, f32[1,2048]{1,0:T(1,128)S(1)}, u32[]{:S(2)}, u32[]{:S(2)}) collective-permute-start(f32[1,2048]{1,0:T(1,128)S(1)} %bank.9.total_ref), channel_id=1, source_target_pairs={{0,1},{1,2},{2,3},{3,0},{4,5},{5,6},{6,7},{7,4},{8,9},{9,10},{10,1... | collective-permute-start | bytes 24584 | tf_op jit(solution)/shard_map/ppermute | solution.py:374
  35.7 2.6 %collective-permute-start.11 = (f32[1,2048]{1,0:T(1,128)S(1)}, f32[1,2048]{1,0:T(1,128)S(1)}, u32[]{:S(2)}, u32[]{:S(2)}) collective-permute-start(f32[1,2048]{1,0:T(1,128)S(1)} %bank.9.total_ref), channel_id=1, source_target_pairs={{0,2},{1,3},{2,0},{3,1},{4,6},{5,7},{6,4},{7,5},{8,10},{9,11},{10,... | collective-permute-start | bytes 24584 | tf_op jit(solution)/shard_map/ppermute | solution.py:374
  38.3 1.3 %collective-permute-start.12 = (f32[1,2048]{1,0:T(1,128)S(1)}, f32[1,2048]{1,0:T(1,128)S(1)}, u32[]{:S(2)}, u32[]{:S(2)}) collective-permute-start(f32[1,2048]{1,0:T(1,128)S(1)} %bank.9.total_ref), channel_id=1, source_target_pairs={{0,3},{1,0},{2,1},{3,2},{4,7},{5,4},{6,5},{7,6},{8,11},{9,8},{10,9... | collective-permute-start | bytes 24584 | tf_op jit(solution)/shard_map/ppermute | solution.py:374
  39.6 0.7 %test.4 = (f32[128,2048]{1,0:T(8,128)S(1)}, f32[128,2048]{1,0:T(8,128)S(1)}) custom-call(bf16[128,768]{1,0:T(8,128)(2,1)S(1)} %collective-permute-done.13.refs_0_, bf16[768,2048]{1,0:T(8,128)(2,1)S(1)} %unit.1.refs_5_.refs_2_.refs_1_), custom_call_target="tpu_custom_call" | custom-call | flops 402653184 | bytes 5439488 | tf_op jit(solution)/shard_map/test/pallas_call | solution.py:149
  40.3 0.0 collective-permute-done.14.refs_0_
  40.3 0.7 %test.5 = (f32[128,2048]{1,0:T(8,128)S(1)}, f32[128,2048]{1,0:T(8,128)S(1)}) custom-call(bf16[128,768]{1,0:T(8,128)(2,1)S(1)} %collective-permute-done.14.refs_0_, bf16[768,2048]{1,0:T(8,128)(2,1)S(1)} %unit.1.refs_5_.refs_2_.refs_1_), custom_call_target="tpu_custom_call" | custom-call | flops 402653184 | bytes 5439488 | tf_op jit(solution)/shard_map/test/pallas_call | solution.py:149
  41.0 0.0 collective-permute-done.10.refs_1_
  41.0 0.9 %collective-permute-done.12.refs_3_ = f32[1,2048]{1,0:T(1,128)S(1)} collective-permute-done((f32[1,2048]{1,0:T(1,128)S(1)}, f32[1,2048]{1,0:T(1,128)S(1)}, u32[]{:S(2)}, u32[]{:S(2)}) %collective-permute-start.12) | collective-permute-done | bytes 8224 | tf_op jit(solution)/shard_map/ppermute | solution.py:374
  41.9 0.4 rows.1
  42.3 0.1 collective-permute-start.15
  42.4 1.6 %collective-permute-start.16 = (f32[4,128]{1,0:T(4,128)S(1)}, f32[4,128]{1,0:T(4,128)S(1)}, u32[]{:S(2)}, u32[]{:S(2)}) collective-permute-start(f32[4,128]{1,0:T(4,128)S(1)} %get-tuple-element.38.refs_0_), channel_id=1, source_target_pairs={{0,8},{4,12},{8,0},{12,4},{1,9},{5,13},{9,1},{13,5},{2,10},{6,14},... | collective-permute-start | bytes 6152 | tf_op jit(solution)/shard_map/ppermute | solution.py:340
  44.0 0.3 collective-permute-start.17
  44.3 0.7 %logs.1 = (f32[1,2048]{1,0:T(1,128)}, f32[256,2048]{1,0:T(8,128)S(1)}, f32[128,2048]{1,0:T(8,128)S(1)}, f32[128,2048]{1,0:T(8,128)S(1)}) custom-call(f32[1,2048]{1,0:T(1,128)S(1)} %get-tuple-element.39.total_ref, f32[256,2048]{1,0:T(8,128)S(1)} %get-tuple-element.28.refs_0_, f32[128,2048]{1,0:T(8,128)S(1)} %get-tuple-element.40.refs_1_, ...), custom_call_target="tpu_custom_call" | custom-call | flops 2048 | bytes 24576 | tf_op jit(solution)/shard_map/logs/pallas_call | solution.py:239
  45.0 0.0 collective-permute-done.15.refs_1_
  45.0 1.1 %collective-permute-done.16.refs_2_ = f32[4,128]{1,0:T(4,128)S(1)} collective-permute-done((f32[4,128]{1,0:T(4,128)S(1)}, f32[4,128]{1,0:T(4,128)S(1)}, u32[]{:S(2)}, u32[]{:S(2)}) %collective-permute-start.16) | collective-permute-done | bytes 2080 | tf_op jit(solution)/shard_map/ppermute | solution.py:340
  46.1 0.9 %collective-permute-done.17.refs_3_ = f32[4,128]{1,0:T(4,128)S(1)} collective-permute-done((f32[4,128]{1,0:T(4,128)S(1)}, f32[4,128]{1,0:T(4,128)S(1)}, u32[]{:S(2)}, u32[]{:S(2)}) %collective-permute-start.17) | collective-permute-done | bytes 2080 | tf_op jit(solution)/shard_map/ppermute | solution.py:340
  47.0 2.3 %out.1 = f32[512,2048]{1,0:T(8,128)} custom-call(f32[4,128]{1,0:T(4,128)S(1)} %get-tuple-element.38.refs_0_, f32[4,128]{1,0:T(4,128)S(1)} %collective-permute-done.15.refs_1_, f32[4,128]{1,0:T(4,128)S(1)} %collective-permute-done.16.refs_2_, f32[4,128]{1,0:T(4,128)S(1)} %collective-permute-done.17.refs_3_, f32[256,2048]{1,0:T(8,128)S(1)} %get-tuple-element.42.refs_4_, ...), custom_call_target="tpu_custom_call" | custom-call | flops 3145728 | bytes 8388608 | tf_op jit(solution)/shard_map/out/pallas_call | solution.py:300
  (7 shorter events, 0.0 us)
Async XLA Ops:
  0.6 8.6 %collective-permute-start.2 = (bf16[512,768]{1,0:T(8,128)(2,1)}, bf16[512,768]{1,0:T(8,128)(2,1)S(1)}, u32[]{:S(2)}, u32[]{:S(2)}) collective-permute-start(bf16[512,768]{1,0:T(8,128)(2,1)} %bitcast.3), channel_id=1, source_target_pairs={{0,4},{4,0},{8,12},{12,8},{1,5},{5,1},{9,13},{13,9},{2,6},{6,2},{1... | collective-permute-start | bytes 2359304 | tf_op jit(solution)/shard_map/ppermute | solution.py:340
  1.2 11.8 %collective-permute-start.3 = (bf16[128,768]{1,0:T(8,128)(2,1)}, bf16[128,768]{1,0:T(8,128)(2,1)S(1)}, u32[]{:S(2)}, u32[]{:S(2)}) collective-permute-start(bf16[128,768]{1,0:T(8,128)(2,1)} %bitcast.6), channel_id=1, source_target_pairs={{0,4},{4,0},{8,12},{12,8},{1,5},{5,1},{9,13},{13,9},{2,6},{6,2},{1... | collective-permute-start | bytes 589832 | tf_op jit(solution)/shard_map/ppermute | solution.py:340
  1.3 1.1 %copy-start = (bf16[1,512,768]{2,1,0:T(8,128)(2,1)S(1)}, bf16[1,512,768]{2,1,0:T(8,128)(2,1)}, u32[]{:S(2)}) copy-start(bf16[1,512,768]{2,1,0:T(8,128)(2,1)} %param.4) | copy-start | bytes 2359300
  2.7 10.2 %collective-permute-start.5 = (bf16[160,768]{1,0:T(8,128)(2,1)S(1)}, bf16[160,768]{1,0:T(8,128)(2,1)S(1)}, u32[]{:S(2)}, u32[]{:S(2)}) collective-permute-start(bf16[160,768]{1,0:T(8,128)(2,1)S(1)} %cut.3.refs_0_), channel_id=1, source_target_pairs={{0,8},{4,12},{8,0},{12,4},{1,9},{5,13},{9,1},{13,5},{2,10},{6,14},... | collective-permute-start | bytes 737288 | tf_op jit(solution)/shard_map/ppermute | solution.py:340
  6.1 11.6 %collective-permute-start.1 = (bf16[176,768]{1,0:T(8,128)(2,1)S(1)}, bf16[176,768]{1,0:T(8,128)(2,1)S(1)}, u32[]{:S(2)}, u32[]{:S(2)}) collective-permute-start(bf16[176,768]{1,0:T(8,128)(2,1)S(1)} %get-tuple-element.25.refs_1_), channel_id=1, source_target_pairs={{0,8},{4,12},{8,0},{12,4},{1,9},{5,13},{9,1},{13,5},{2,10},{6,14},... | collective-permute-start | bytes 811016 | tf_op jit(solution)/shard_map/ppermute | solution.py:340
  9.2 3.7 %copy-start.1 = (bf16[1,128,768]{2,1,0:T(8,128)(2,1)S(1)}, bf16[1,128,768]{2,1,0:T(8,128)(2,1)}, u32[]{:S(2)}) copy-start(bf16[1,128,768]{2,1,0:T(8,128)(2,1)} %param.5) | copy-start | bytes 589828
  12.9 6.6 %collective-permute-start.6 = (bf16[160,768]{1,0:T(8,128)(2,1)S(1)}, bf16[160,768]{1,0:T(8,128)(2,1)S(1)}, u32[]{:S(2)}, u32[]{:S(2)}) collective-permute-start(bf16[160,768]{1,0:T(8,128)(2,1)S(1)} %collective-permute-done.5.refs_0_), channel_id=1, source_target_pairs={{0,4},{4,0},{8,12},{12,8},{1,5},{5,1},{9,13},{13,9},{2,6},{6,2},{1... | collective-permute-start | bytes 737288 | tf_op jit(solution)/shard_map/ppermute | solution.py:340
  17.7 3.1 %collective-permute-start.4 = (bf16[176,768]{1,0:T(8,128)(2,1)S(1)}, bf16[176,768]{1,0:T(8,128)(2,1)S(1)}, u32[]{:S(2)}, u32[]{:S(2)}) collective-permute-start(bf16[176,768]{1,0:T(8,128)(2,1)S(1)} %collective-permute-done.1.refs_0_), channel_id=1, source_target_pairs={{0,4},{4,0},{8,12},{12,8},{1,5},{5,1},{9,13},{13,9},{2,6},{6,2},{1... | collective-permute-start | bytes 811016 | tf_op jit(solution)/shard_map/ppermute | solution.py:340
  17.7 6.8 %collective-permute-start.8 = (bf16[112,768]{1,0:T(8,128)(2,1)S(1)}, bf16[112,768]{1,0:T(8,128)(2,1)S(1)}, u32[]{:S(2)}, u32[]{:S(2)}) collective-permute-start(bf16[112,768]{1,0:T(8,128)(2,1)S(1)} %get-tuple-element.26.refs_2_), channel_id=1, source_target_pairs={{0,8},{4,12},{8,0},{12,4},{1,9},{5,13},{9,1},{13,5},{2,10},{6,14},... | collective-permute-start | bytes 516104 | tf_op jit(solution)/shard_map/ppermute | solution.py:340
  24.5 5.7 %collective-permute-start.9 = (bf16[112,768]{1,0:T(8,128)(2,1)S(1)}, bf16[112,768]{1,0:T(8,128)(2,1)S(1)}, u32[]{:S(2)}, u32[]{:S(2)}) collective-permute-start(bf16[112,768]{1,0:T(8,128)(2,1)S(1)} %collective-permute-done.8.refs_0_), channel_id=1, source_target_pairs={{0,4},{4,0},{8,12},{12,8},{1,5},{5,1},{9,13},{13,9},{2,6},{6,2},{1... | collective-permute-start | bytes 516104 | tf_op jit(solution)/shard_map/ppermute | solution.py:340
  24.5 5.7 %collective-permute-start = (bf16[64,768]{1,0:T(8,128)(2,1)S(1)}, bf16[64,768]{1,0:T(8,128)(2,1)S(1)}, u32[]{:S(2)}, u32[]{:S(2)}) collective-permute-start(bf16[64,768]{1,0:T(8,128)(2,1)S(1)} %get-tuple-element.24.refs_3_), channel_id=1, source_target_pairs={{0,8},{4,12},{8,0},{12,4},{1,9},{5,13},{9,1},{13,5},{2,10},{6,14},... | collective-permute-start | bytes 294920 | tf_op jit(solution)/shard_map/ppermute | solution.py:340
  26.2 7.7 %collective-permute-start.13 = (bf16[128,768]{1,0:T(8,128)(2,1)S(1)}, bf16[128,768]{1,0:T(8,128)(2,1)S(1)}, u32[]{:S(2)}, u32[]{:S(2)}) collective-permute-start(bf16[128,768]{1,0:T(8,128)(2,1)S(1)} %bitcast.8), channel_id=1, source_target_pairs={{0,8},{4,12},{8,0},{12,4},{1,9},{5,13},{9,1},{13,5},{2,10},{6,14},... | collective-permute-start | bytes 589832 | tf_op jit(solution)/shard_map/ppermute | solution.py:340
  30.2 1.3 %collective-permute-start.7 = (bf16[64,768]{1,0:T(8,128)(2,1)S(1)}, bf16[64,768]{1,0:T(8,128)(2,1)S(1)}, u32[]{:S(2)}, u32[]{:S(2)}) collective-permute-start(bf16[64,768]{1,0:T(8,128)(2,1)S(1)} %collective-permute-done.refs_0_), channel_id=1, source_target_pairs={{0,4},{4,0},{8,12},{12,8},{1,5},{5,1},{9,13},{13,9},{2,6},{6,2},{1... | collective-permute-start | bytes 294920 | tf_op jit(solution)/shard_map/ppermute | solution.py:340
  33.9 6.4 %collective-permute-start.14 = (bf16[128,768]{1,0:T(8,128)(2,1)S(1)}, bf16[128,768]{1,0:T(8,128)(2,1)S(1)}, u32[]{:S(2)}, u32[]{:S(2)}) collective-permute-start(bf16[128,768]{1,0:T(8,128)(2,1)S(1)} %collective-permute-done.13.refs_0_), channel_id=1, source_target_pairs={{0,4},{4,0},{8,12},{12,8},{1,5},{5,1},{9,13},{13,9},{2,6},{6,2},{1... | collective-permute-start | bytes 589832 | tf_op jit(solution)/shard_map/ppermute | solution.py:340
  33.9 7.1 %collective-permute-start.10 = (f32[1,2048]{1,0:T(1,128)S(1)}, f32[1,2048]{1,0:T(1,128)S(1)}, u32[]{:S(2)}, u32[]{:S(2)}) collective-permute-start(f32[1,2048]{1,0:T(1,128)S(1)} %bank.9.total_ref), channel_id=1, source_target_pairs={{0,1},{1,2},{2,3},{3,0},{4,5},{5,6},{6,7},{7,4},{8,9},{9,10},{10,1... | collective-permute-start | bytes 24584 | tf_op jit(solution)/shard_map/ppermute | solution.py:374
  35.7 5.3 %collective-permute-start.11 = (f32[1,2048]{1,0:T(1,128)S(1)}, f32[1,2048]{1,0:T(1,128)S(1)}, u32[]{:S(2)}, u32[]{:S(2)}) collective-permute-start(f32[1,2048]{1,0:T(1,128)S(1)} %bank.9.total_ref), channel_id=1, source_target_pairs={{0,2},{1,3},{2,0},{3,1},{4,6},{5,7},{6,4},{7,5},{8,10},{9,11},{10,... | collective-permute-start | bytes 24584 | tf_op jit(solution)/shard_map/ppermute | solution.py:374
  38.3 3.7 %collective-permute-start.12 = (f32[1,2048]{1,0:T(1,128)S(1)}, f32[1,2048]{1,0:T(1,128)S(1)}, u32[]{:S(2)}, u32[]{:S(2)}) collective-permute-start(f32[1,2048]{1,0:T(1,128)S(1)} %bank.9.total_ref), channel_id=1, source_target_pairs={{0,3},{1,0},{2,1},{3,2},{4,7},{5,4},{6,5},{7,6},{8,11},{9,8},{10,9... | collective-permute-start | bytes 24584 | tf_op jit(solution)/shard_map/ppermute | solution.py:374
  42.3 2.7 %collective-permute-start.15 = (f32[4,128]{1,0:T(4,128)S(1)}, f32[4,128]{1,0:T(4,128)S(1)}, u32[]{:S(2)}, u32[]{:S(2)}) collective-permute-start(f32[4,128]{1,0:T(4,128)S(1)} %get-tuple-element.38.refs_0_), channel_id=1, source_target_pairs={{0,4},{4,0},{8,12},{12,8},{1,5},{5,1},{9,13},{13,9},{2,6},{6,2},{1... | collective-permute-start | bytes 6152 | tf_op jit(solution)/shard_map/ppermute | solution.py:340
  42.4 3.7 %collective-permute-start.16 = (f32[4,128]{1,0:T(4,128)S(1)}, f32[4,128]{1,0:T(4,128)S(1)}, u32[]{:S(2)}, u32[]{:S(2)}) collective-permute-start(f32[4,128]{1,0:T(4,128)S(1)} %get-tuple-element.38.refs_0_), channel_id=1, source_target_pairs={{0,8},{4,12},{8,0},{12,4},{1,9},{5,13},{9,1},{13,5},{2,10},{6,14},... | collective-permute-start | bytes 6152 | tf_op jit(solution)/shard_map/ppermute | solution.py:340
  44.0 3.0 %collective-permute-start.17 = (f32[4,128]{1,0:T(4,128)S(1)}, f32[4,128]{1,0:T(4,128)S(1)}, u32[]{:S(2)}, u32[]{:S(2)}) collective-permute-start(f32[4,128]{1,0:T(4,128)S(1)} %get-tuple-element.38.refs_0_), channel_id=1, source_target_pairs={{0,12},{4,8},{8,4},{12,0},{1,13},{5,9},{9,5},{13,1},{2,14},{6,10},... | collective-permute-start | bytes 6152 | tf_op jit(solution)/shard_map/ppermute | solution.py:340
